TPU v7x, 32 devices: a whole 2x2x4 slice. The times are simulated.
32 devices in a mesh: head: 4 (over z), blk: 8 (over y, x, core).
Axes of the slice: x: 2, y: 2, z: 4, core: 2. Of those that a mesh axis runs over, the one named last changes fastest.
Arguments:
- tokens: bfloat16 [8192, 1024], P(('blk', 'head')), may hold values from -6 to 6
- cotangent: bfloat16 [8192, 1024], P(('blk', 'head')), may hold values from -6 to 6
- segment: int32 [8192], replicated, may hold values from 0 to 3, never falling along the last dimension, each value on 1 to 6144 neighbouring positions
- norm_gain: bfloat16 [1024], P(('head', 'blk')), may hold values from 0.5 to 1.5
- norm_shift: bfloat16 [1024], P(('head', 'blk')), may hold values from -1.5 to 1.5
- in_weight: bfloat16 [1024, 3072], P(('head', 'blk')), may hold values from -0.1875 to 0.1875
- query_bias: bfloat16 [1024], P(('head', 'blk')), may hold values from -2.5 to 2.5
- value_bias: bfloat16 [1024], P(('head', 'blk')), may hold values from -1.5 to 1.5
- out_weight: bfloat16 [1024, 1024], P(('head', 'blk')), may hold values from -3 to 3
- out_bias: bfloat16 [1024], P(('head', 'blk')), may hold values from -1.5 to 1.5
- post_gain: bfloat16 [1024], P(('head', 'blk')), may hold values from 0.5 to 1.5
- post_shift: bfloat16 [1024], P(('head', 'blk')), may hold values from -1.5 to 1.5
- up_weight: bfloat16 [1024, 4096], P(('head', 'blk')), may hold values from -0.1875 to 0.1875
- up_bias: bfloat16 [4096], P(('head', 'blk')), may hold values from -1.5 to 1.5
- down_weight: bfloat16 [4096, 1024], P(('head', 'blk')), may hold values from -0.09375 to 0.09375
- down_bias: bfloat16 [1024], P(('head', 'blk')), may hold values from -1.5 to 1.5
Outputs:
- output: bfloat16 [8192, 1024], P(('blk', 'head'))
- tokens_grad: bfloat16 [8192, 1024], P(('blk', 'head'))
- norm_gain_grad: float32 [1024], P(('head', 'blk'))
- norm_shift_grad: float32 [1024], P(('head', 'blk'))
- in_weight_grad: float32 [1024, 3072], P(('head', 'blk'))
- query_bias_grad: float32 [1024], P(('head', 'blk'))
- value_bias_grad: float32 [1024], P(('head', 'blk'))
- out_weight_grad: float32 [1024, 1024], P(('head', 'blk'))
- out_bias_grad: float32 [1024], P(('head', 'blk'))
- post_gain_grad: float32 [1024], P(('head', 'blk'))
- post_shift_grad: float32 [1024], P(('head', 'blk'))
- up_weight_grad: float32 [1024, 4096], P(('head', 'blk'))
- up_bias_grad: float32 [4096], P(('head', 'blk'))
- down_weight_grad: float32 [4096, 1024], P(('head', 'blk'))
- down_bias_grad: float32 [1024], P(('head', 'blk'))
Inputs may be any that keep to these rules, and one draw needn't show every extreme that they name: `segment`: document numbers never fall along the sequence; each document holds 1 to 6144 tokens and one holds exactly 6144.
All inputs are finite; a program needn't handle non-finite values.
Results may differ from a plain program's by a relative error of at most 0.019.
Values may be sent and summed in bfloat16 or wider, within the bound.
No kernel may reach another device: no remote copies, remote signals or barrier semaphores. Data moves between devices by JAX's collectives and lax.ppermute only.
A program may use at most 256 MiB of HBM per device.

v0:
```python
import jax
import jax.numpy as jnp
from jax import lax
from jax.sharding import PartitionSpec as P

HEADS = 16
HEAD_DIM = 64


EPS = 1e-05
NEGATIVE = -1e30
GELU_C = 0.7978845608028654


def norm_forward(rows, gain, shift):
    center = rows - jnp.mean(rows, axis=-1, keepdims=True)
    var = jnp.mean(center * center, axis=-1, keepdims=True)
    inverse = lax.rsqrt(var + EPS)
    unit = center * inverse
    return (unit * gain + shift, unit, inverse)


def norm_backward(grad, unit, inverse, gain):
    scaled = grad * gain
    inner = (
        scaled
        - jnp.mean(scaled, axis=-1, keepdims=True)
        - unit * jnp.mean(scaled * unit, axis=-1, keepdims=True)
    )
    return (inverse * inner, jnp.sum(grad * unit, axis=0), jnp.sum(grad, axis=0))


def gelu_parts(pre):
    cubic = pre * pre * pre
    tangent = jnp.tanh(GELU_C * (pre + 0.044715 * cubic))
    value = 0.5 * pre * (1.0 + tangent)
    slope = 0.5 * (1.0 + tangent) + 0.5 * pre * (1.0 - tangent * tangent) * GELU_C * (
        1.0 + 3.0 * 0.044715 * pre * pre
    )
    return (value, slope)


def on_device(
    tokens,
    cotangent,
    segment,
    norm_gain,
    norm_shift,
    in_weight,
    query_bias,
    value_bias,
    out_weight,
    out_bias,
    post_gain,
    post_shift,
    up_weight,
    up_bias,
    down_weight,
    down_bias,
):
    n_head = lax.axis_size("head")
    n_blk = lax.axis_size("blk")
    group = lax.axis_index("blk")
    tok_rows = tokens.shape[0]
    width = tokens.shape[1]
    block_rows = tok_rows * n_head
    head_group = HEADS // n_head
    group_width = head_group * HEAD_DIM
    scale = HEAD_DIM ** (-0.5)
    q_first = group * block_rows
    f32 = jnp.float32
    bf16 = jnp.bfloat16
    gain_a, shift_a, w_in, bias_q, bias_v, w_out, bias_out = (
        lax.all_gather(norm_gain, ("head", "blk"), axis=0, tiled=True),
        lax.all_gather(norm_shift, ("head", "blk"), axis=0, tiled=True),
        lax.all_gather(in_weight, ("head", "blk"), axis=0, tiled=True),
        lax.all_gather(query_bias, ("head", "blk"), axis=0, tiled=True),
        lax.all_gather(value_bias, ("head", "blk"), axis=0, tiled=True),
        lax.all_gather(out_weight, ("head", "blk"), axis=0, tiled=True),
        lax.all_gather(out_bias, ("head", "blk"), axis=0, tiled=True),
    )
    rows = tokens.astype(f32)
    normed, unit_in, inverse_in = norm_forward(rows, gain_a.astype(f32), shift_a.astype(f32))
    normed_low = normed.astype(bf16)
    bias_full = jnp.concatenate([bias_q, jnp.zeros((width,), bf16), bias_v]).astype(f32)
    projected = (jnp.dot(normed_low, w_in, preferred_element_type=f32) + bias_full).astype(bf16)
    grouped = lax.all_to_all(
        projected.reshape(tok_rows, 3, n_head, group_width),
        "head",
        split_axis=2,
        concat_axis=0,
        tiled=True,
    )
    grouped = grouped.reshape(block_rows, 3, head_group, HEAD_DIM)
    queries = grouped[:, 0]
    kv_local = grouped[:, 1:].reshape(block_rows, 2, group_width)
    seg_query = lax.dynamic_slice_in_dim(segment, q_first, block_rows)
    first_doc = seg_query[0]
    query_pos = q_first + lax.iota(jnp.int32, block_rows)

    def block_scores(keys, key_start):
        key_pos = key_start + lax.iota(jnp.int32, block_rows)
        seg_key = lax.dynamic_slice_in_dim(segment, key_start, block_rows)
        allowed = (key_pos[None, :] <= query_pos[:, None]) & (
            seg_key[None, :] == seg_query[:, None]
        )
        scores = jnp.einsum("qhd,khd->hqk", queries, keys, preferred_element_type=f32) * scale
        return (scores, allowed[None])

    def visible(key_start):
        last_doc = lax.dynamic_index_in_dim(segment, key_start + block_rows - 1, keepdims=False)
        return (key_start <= q_first + block_rows - 1) & (last_doc >= first_doc)

    def split_pair(block):
        pair = block.reshape(block_rows, 2, head_group, HEAD_DIM)
        return (pair[:, 0], pair[:, 1])

    start_state = (
        jnp.zeros((block_rows, head_group, HEAD_DIM), f32),
        jnp.full((head_group, block_rows), NEGATIVE, f32),
        jnp.zeros((head_group, block_rows), f32),
    )
    piece = lax.all_gather(kv_local, "blk", axis=0, tiled=True)
    count = piece.shape[0] // block_rows
    blocks = piece.reshape(count, block_rows, 2, group_width)

    def forward_advance(state, item):
        block, index = item
        key_start = index * block_rows

        def forward_update(inner):
            acc, run_max, run_sum = inner
            keys, values = split_pair(block)
            scores, allowed = block_scores(keys, key_start)
            new_max = jnp.maximum(run_max, jnp.max(jnp.where(allowed, scores, NEGATIVE), axis=2))
            weights = jnp.where(allowed, jnp.exp(scores - new_max[:, :, None]), 0.0)
            factor = jnp.exp(run_max - new_max)
            new_sum = run_sum * factor + jnp.sum(weights, axis=2)
            mixed = jnp.einsum(
                "hqk,khd->qhd", weights.astype(bf16), values, preferred_element_type=f32
            )
            return (acc * factor.T[:, :, None] + mixed, new_max, new_sum)

        return (lax.cond(visible(key_start), forward_update, lambda inner: inner, state), None)

    state, _ = lax.scan(forward_advance, start_state, (blocks, jnp.arange(count, dtype=jnp.int32)))
    acc, run_max, run_sum = state
    attended = acc / run_sum.T[:, :, None]
    log_total = run_max + jnp.log(run_sum)
    attended_low = attended.astype(bf16)
    back_rows = lax.all_to_all(
        attended_low.reshape(block_rows, 1, group_width),
        "head",
        split_axis=0,
        concat_axis=1,
        tiled=True,
    )
    back_rows = back_rows.reshape(tok_rows, width)
    branch = jnp.dot(back_rows, w_out, preferred_element_type=f32) + bias_out.astype(f32)
    middle = rows + branch
    gain_b, shift_b, w_up, bias_up, w_down, bias_down = (
        lax.all_gather(post_gain, ("head", "blk"), axis=0, tiled=True),
        lax.all_gather(post_shift, ("head", "blk"), axis=0, tiled=True),
        lax.all_gather(up_weight, ("head", "blk"), axis=0, tiled=True),
        lax.all_gather(up_bias, ("head", "blk"), axis=0, tiled=True),
        lax.all_gather(down_weight, ("head", "blk"), axis=0, tiled=True),
        lax.all_gather(down_bias, ("head", "blk"), axis=0, tiled=True),
    )
    hidden_in, unit_mid, inverse_mid = norm_forward(middle, gain_b.astype(f32), shift_b.astype(f32))
    hidden_low = hidden_in.astype(bf16)
    pre = jnp.dot(hidden_low, w_up, preferred_element_type=f32) + bias_up.astype(f32)
    act, slope = gelu_parts(pre)
    act_low = act.astype(bf16)
    result = middle + jnp.dot(act_low, w_down, preferred_element_type=f32) + bias_down.astype(f32)
    output = result.astype(bf16)
    grad_out = cotangent.astype(f32)
    down_bias_grad = jnp.sum(grad_out, axis=0)
    down_weight_grad = jnp.einsum("tf,td->fd", act_low, cotangent, preferred_element_type=f32)
    grad_act = jnp.einsum("td,fd->tf", cotangent, w_down, preferred_element_type=f32)
    grad_pre = (grad_act * slope).astype(bf16)
    up_bias_grad = jnp.sum(grad_pre.astype(f32), axis=0)
    up_weight_grad = jnp.einsum("td,tf->df", hidden_low, grad_pre, preferred_element_type=f32)
    grad_hidden = jnp.einsum("tf,df->td", grad_pre, w_up, preferred_element_type=f32)
    grad_mid_in, post_gain_grad, post_shift_grad = norm_backward(
        grad_hidden, unit_mid, inverse_mid, gain_b.astype(f32)
    )
    grad_middle = grad_out + grad_mid_in
    (
        post_gain_grad,
        post_shift_grad,
        up_weight_grad,
        up_bias_grad,
        down_weight_grad,
        down_bias_grad,
    ) = (
        lax.psum_scatter(post_gain_grad, ("head", "blk"), scatter_dimension=0, tiled=True),
        lax.psum_scatter(post_shift_grad, ("head", "blk"), scatter_dimension=0, tiled=True),
        lax.psum_scatter(up_weight_grad, ("head", "blk"), scatter_dimension=0, tiled=True),
        lax.psum_scatter(up_bias_grad, ("head", "blk"), scatter_dimension=0, tiled=True),
        lax.psum_scatter(down_weight_grad, ("head", "blk"), scatter_dimension=0, tiled=True),
        lax.psum_scatter(down_bias_grad, ("head", "blk"), scatter_dimension=0, tiled=True),
    )
    grad_branch = grad_middle.astype(bf16)
    out_bias_grad = jnp.sum(grad_branch.astype(f32), axis=0)
    out_weight_grad = jnp.einsum("td,te->de", back_rows, grad_branch, preferred_element_type=f32)
    grad_back = jnp.einsum("te,de->td", grad_branch, w_out, preferred_element_type=f32).astype(bf16)
    grad_heads = lax.all_to_all(
        grad_back.reshape(tok_rows, n_head, group_width),
        "head",
        split_axis=1,
        concat_axis=0,
        tiled=True,
    )
    grad_heads = grad_heads.reshape(block_rows, head_group, HEAD_DIM)
    delta = jnp.sum(grad_heads.astype(f32) * attended, axis=-1).T

    def block_backward(block, key_start):
        keys, values = split_pair(block)
        scores, allowed = block_scores(keys, key_start)
        probs = jnp.where(allowed, jnp.exp(scores - log_total[:, :, None]), 0.0)
        grad_probs = jnp.einsum("qhd,khd->hqk", grad_heads, values, preferred_element_type=f32)
        grad_scores = (probs * (grad_probs - delta[:, :, None])).astype(bf16)
        grad_values = jnp.einsum(
            "hqk,qhd->khd", probs.astype(bf16), grad_heads, preferred_element_type=f32
        )
        grad_keys = (
            jnp.einsum("hqk,qhd->khd", grad_scores, queries, preferred_element_type=f32) * scale
        )
        query_add = (
            jnp.einsum("hqk,khd->qhd", grad_scores, keys, preferred_element_type=f32) * scale
        )
        return (query_add, jnp.stack([grad_keys, grad_values], axis=1))

    back_state = (
        jnp.zeros((block_rows, head_group, HEAD_DIM), f32),
        jnp.zeros((block_rows * n_blk, 2, head_group, HEAD_DIM), f32),
    )
    piece = lax.all_gather(kv_local, "blk", axis=0, tiled=True)
    count = piece.shape[0] // block_rows
    blocks = piece.reshape(count, block_rows, 2, group_width)

    def backward_advance(state, item):
        block, index = item
        key_start = index * block_rows

        def backward_update(inner):
            grad_query, grad_pairs = inner
            query_add, pair_add = block_backward(block, key_start)
            current = lax.dynamic_slice_in_dim(grad_pairs, key_start, block_rows, 0)
            return (
                grad_query + query_add,
                lax.dynamic_update_slice_in_dim(grad_pairs, current + pair_add, key_start, 0),
            )

        return (lax.cond(visible(key_start), backward_update, lambda inner: inner, state), None)

    state, _ = lax.scan(backward_advance, back_state, (blocks, jnp.arange(count, dtype=jnp.int32)))
    grad_query, grad_pairs = state
    pair_sums = lax.psum_scatter(
        grad_pairs.reshape(block_rows * n_blk, 2, group_width).astype(jnp.bfloat16),
        "blk",
        scatter_dimension=0,
        tiled=True,
    ).astype(jnp.float32)
    grad_joint = jnp.concatenate(
        [grad_query.reshape(block_rows, 1, group_width).astype(bf16), pair_sums.astype(bf16)],
        axis=1,
    )
    grad_rows = lax.all_to_all(
        grad_joint.reshape(block_rows, 3, 1, group_width),
        "head",
        split_axis=0,
        concat_axis=2,
        tiled=True,
    )
    grad_proj = grad_rows.reshape(tok_rows, 3 * width)
    query_bias_grad = jnp.sum(grad_proj[:, :width].astype(f32), axis=0)
    value_bias_grad = jnp.sum(grad_proj[:, 2 * width :].astype(f32), axis=0)
    in_weight_grad = jnp.einsum("td,te->de", normed_low, grad_proj, preferred_element_type=f32)
    grad_normed = jnp.einsum("te,de->td", grad_proj, w_in, preferred_element_type=f32)
    grad_rows_in, norm_gain_grad, norm_shift_grad = norm_backward(
        grad_normed, unit_in, inverse_in, gain_a.astype(f32)
    )
    tokens_grad = (grad_middle + grad_rows_in).astype(bf16)
    (
        norm_gain_grad,
        norm_shift_grad,
        in_weight_grad,
        query_bias_grad,
        value_bias_grad,
        out_weight_grad,
        out_bias_grad,
    ) = (
        lax.psum_scatter(norm_gain_grad, ("head", "blk"), scatter_dimension=0, tiled=True),
        lax.psum_scatter(norm_shift_grad, ("head", "blk"), scatter_dimension=0, tiled=True),
        lax.psum_scatter(in_weight_grad, ("head", "blk"), scatter_dimension=0, tiled=True),
        lax.psum_scatter(query_bias_grad, ("head", "blk"), scatter_dimension=0, tiled=True),
        lax.psum_scatter(value_bias_grad, ("head", "blk"), scatter_dimension=0, tiled=True),
        lax.psum_scatter(out_weight_grad, ("head", "blk"), scatter_dimension=0, tiled=True),
        lax.psum_scatter(out_bias_grad, ("head", "blk"), scatter_dimension=0, tiled=True),
    )
    return (
        output,
        tokens_grad,
        norm_gain_grad,
        norm_shift_grad,
        in_weight_grad,
        query_bias_grad,
        value_bias_grad,
        out_weight_grad,
        out_bias_grad,
        post_gain_grad,
        post_shift_grad,
        up_weight_grad,
        up_bias_grad,
        down_weight_grad,
        down_bias_grad,
    )


def solution(mesh):
    placed = (
        P(("blk", "head"), None),
        P(("blk", "head"), None),
        P(),
        P(("head", "blk")),
        P(("head", "blk")),
        P(("head", "blk"), None),
        P(("head", "blk")),
        P(("head", "blk")),
        P(("head", "blk"), None),
        P(("head", "blk")),
        P(("head", "blk")),
        P(("head", "blk")),
        P(("head", "blk"), None),
        P(("head", "blk")),
        P(("head", "blk"), None),
        P(("head", "blk")),
    )
    return jax.shard_map(
        on_device,
        mesh=mesh,
        in_specs=placed,
        out_specs=(
            P(("blk", "head"), None),
            P(("blk", "head"), None),
            P(("head", "blk")),
            P(("head", "blk")),
            P(("head", "blk"), None),
            P(("head", "blk")),
            P(("head", "blk")),
            P(("head", "blk"), None),
            P(("head", "blk")),
            P(("head", "blk")),
            P(("head", "blk")),
            P(("head", "blk"), None),
            P(("head", "blk")),
            P(("head", "blk"), None),
            P(("head", "blk")),
        ),
        check_vma=False,
    )
```

profile of v0, /device:TPU:0, one launch (start us, length us, event | category | flops | bytes accessed | tf_op | source)
XLA Modules:
  0.0 1565.3 jit_solution(17215553345524749497)
XLA Ops:
  14.7 42.6 %all-reduce.18 = (bf16[1024]{0:T(1024)(128)(2,1)S(1)}, bf16[1024]{0:T(1024)(128)(2,1)S(1)}, bf16[1024]{0:T(1024)(128)(2,1)S(1)}, bf16[1024]{0:T(1024)(128)(2,1)S...) all-reduce(bf16[1024]{0:T(1024)(128)(2,1)S(1)} %dynamic-update-slic, ...), channel_id=1, replica_groups=mesh['head'=4,'blk'=8] {'head','blk'}, use_global_device_ids=true, to_apply=%add.3 | all-reduce | flops 8192 | bytes 32768
  60.0 23.3 %all-gather.7.cloned.1.call-done = bf16[1024,3072]{1,0:T(8,128)(2,1)} async-done(((bf16[32,3072]{1,0:T(8,128)(2,1)}), bf16[1024,3072]{1,0:T(8,128)(2,1)}) %all-gather.7.cloned.1.call-update) | async-done | bytes 6291472 | tf_op jit(solution)/shard_map/all_gather | solution.py:76
  83.2 6.0 fusion.44
  89.3 3.2 reshape.282
  92.8 40.3 %all_to_all.60 = bf16[256,3,4,256]{3,0,1,2:T(8,128)(2,1)S(1)} all-to-all(bf16[256,3,4,256]{3,0,1,2:T(8,128)(2,1)S(1)} %copy.93), channel_id=1, replica_groups=mesh['head'=4,'blk'=8] {'head'}, dimensions={2} | all-to-all | bytes 3145728 | tf_op jit(solution)/shard_map/all_to_all | solution.py:87
  135.3 2.8 reshape.283
  142.4 49.6 %all-gather.9.cloned.1.call-done = bf16[8192,2,256]{0,2,1:T(8,128)(2,1)} async-done(((bf16[1024,2,256]{0,2,1:T(8,128)(2,1)}), bf16[8192,2,256]{0,2,1:T(8,128)(2,1)}) %all-gather.9.cloned.1.call-update) | async-done | bytes 8388624 | tf_op jit(solution)/shard_map/all_gather | solution.py:123
  191.9 12.0 copy.95
  203.9 11.5 copy.96
  215.6 45.0 %while.38 = (s32[]{:T(128)}, f32[1024,4,64]{0,2,1:T(8,128)S(1)}, f32[4,1024]{1,0:T(4,128)S(1)}, f32[4,1024]{1,0:T(4,128)S(1)}, s32[8]{0:T(128)S(1)}, /*index=5*/...) while((s32[]{:T(128)}, f32[1024,4,64]{0,2,1:T(8,128)S(1)}, ...), condition=%wide.region_7.8_spmd.clone, body=%wide.region_2.7_spmd.clone.sunk | while | flops 1123563520 | bytes 60596688 | solution.py:146
  219.4 13.9 conditional.6
  222.7 3.0 fusion.4
  225.8 3.9 fusion.15
  229.7 3.7 fusion.7
  263.4 4.6 all-to-all-start.1
  268.1 106.1 %all-gather = bf16[32,1,128]{2,1,0:T(2,128)(2,1)S(1)} all-gather(bf16[1,1,128]{2,1,0:T(2,128)(2,1)S(1)} %bitcast.161), channel_id=1, replica_groups=mesh['head'=4,'blk'=8] {'head','blk'}, dimensions={0}, use_global_device_ids=true | all-gather | bytes 8448 | tf_op jit(solution)/shard_map/all_gather | solution.py:165
  379.3 2.6 fusion.71
  382.3 8.0 convolution_add_fusion
  390.3 29.5 %all-gather.15.cloned.1.call-done = bf16[4096,1024]{1,0:T(8,128)(2,1)} async-done(((bf16[128,1024]{1,0:T(8,128)(2,1)}), bf16[4096,1024]{1,0:T(8,128)(2,1)}) %all-gather.15.cloned.1.call-update) | async-done | bytes 8388624 | tf_op jit(solution)/shard_map/all_gather | solution.py:166
  419.8 11.8 convert_reduce_fusion
  431.7 3.2 multiply_reduce_fusion
  438.5 3.5 all-to-all-start.2
  442.1 15.1 all-to-all-done.2
  461.1 7.8 broadcast_in_dim.56
  468.9 81.4 %while.39 = (s32[]{:T(128)}, f32[1024,4,64]{0,2,1:T(8,128)}, f32[8192,2,4,64]{0,3,2,1:T(8,128)}, s32[8]{0:T(128)S(1)}, s32[]{:T(128)}, /*index=5*/s32[8192]{0:T(...) while((s32[]{:T(128)}, f32[1024,4,64]{0,2,1:T(8,128)}, ...), condition=%wide.region_16.17_spmd.clone, body=%wide.region_13.16_spmd.clone.sunk | while | flops 2731280384 | bytes 103375360 | solution.py:257
  472.9 50.1 %conditional.7 = ((f32[1024,4,64]{0,2,1:T(8,128)}, f32[8192,2,4,64]{0,3,2,1:T(8,128)})) conditional(s32[]{:T(128)} %convert_element_type.245, (f32[1024,4,64]{0,2,1:T(8,128)}, f32[8192,2,4,64]{0,3,2,1:T(8,128)}) %tuple.143, (s32[]{:T(128)}, s32[]{:T(128)}, s32[8192]{0:T(1024)}, s32[1024]{0:T(1024)S(1)}, bf16[8,1024,2,256]{1,3,2,0:T(8,128)(2,1)}, ...), branch_computations={%region_14.14_spmd, %region_15.15_spmd} | conditional | flops 2731280384 | bytes 103370856 | solution.py:255
  476.1 8.1 fusion.33
  484.2 10.3 fusion.27
  494.6 9.1 fusion.22
  503.7 3.9 fusion.31
  507.6 2.7 fusion.32
  512.6 10.4 dynamic_update_slice.3
  550.3 9.0 convert_element_type.157
  560.6 2.7 fusion.63
  564.6 313.6 %reduce-scatter.6.cloned.1.call-done = bf16[1024,2,256]{0,2,1:T(8,128)(2,1)} async-done(((bf16[8192,2,256]{0,2,1:T(8,128)(2,1)}), bf16[1024,2,256]{0,2,1:T(8,128)(2,1)}) %reduce-scatter.6.cloned.1.call-update) | async-done | bytes 1048592 | tf_op jit(solution)/shard_map/reduce_scatter | solution.py:259
  878.2 2.5 maximum_bitcast_fusion
  880.7 4.1 copy.102
  884.9 60.9 %all_to_all.61 = bf16[1024,3,1,256]{3,1,2,0:T(4,128)(2,1)S(1)} all-to-all(bf16[1024,3,1,256]{3,1,2,0:T(4,128)(2,1)} %copy.102), channel_id=1, replica_groups=mesh['head'=4,'blk'=8] {'head'}, dimensions={0} | all-to-all | bytes 3145728 | tf_op jit(solution)/shard_map/all_to_all | solution.py:269
  947.1 2.6 copy.104
  949.7 7.9 fusion.66
  958.7 10.8 fusion.70
  970.8 9.8 fusion.69
  981.3 8.4 fusion.46
  990.1 5.1 fusion.60
  995.2 38.9 %all-reduce.17 = (f32[1024]{0:T(1024)S(1)}, f32[1024]{0:T(1024)S(1)}, f32[1024]{0:T(1024)S(1)}, f32[1024]{0:T(1024)S(1)}, f32[1024]{0:T(1024)S(1)}, /*index=5*/f...) all-reduce(f32[1024]{0:T(1024)S(1)} %get-tuple-element.973, ...), channel_id=3, replica_groups=mesh['head'=4,'blk'=8] {'head','blk'}, use_global_device_ids=true, to_apply=%region_21.22.clone | all-reduce | flops 12288 | bytes 98304
  1040.5 145.6 %reduce-scatter.8.cloned.1.call-done = f32[32,3072]{1,0:T(8,128)} async-done(((f32[1024,3072]{1,0:T(8,128)}), f32[32,3072]{1,0:T(8,128)}) %reduce-scatter.8.cloned.1.call-update) | async-done | bytes 393232 | tf_op jit(solution)/shard_map/reduce_scatter | solution.py:296
  1186.1 184.7 %reduce-scatter.14.cloned.1.call-done = f32[128,1024]{1,0:T(8,128)} async-done(((f32[4096,1024]{1,0:T(8,128)}), f32[128,1024]{1,0:T(8,128)}) %reduce-scatter.14.cloned.1.call-update) | async-done | bytes 524304 | tf_op jit(solution)/shard_map/reduce_scatter | solution.py:200
  1370.8 187.2 %reduce-scatter.12.cloned.1.call-done = f32[32,4096]{1,0:T(8,128)} async-done(((f32[1024,4096]{1,0:T(8,128)}), f32[32,4096]{1,0:T(8,128)}) %reduce-scatter.12.cloned.1.call-update) | async-done | bytes 524304 | tf_op jit(solution)/shard_map/reduce_scatter | solution.py:198
  (247 shorter events, 85.5 us)
Async XLA Ops:
  7.2 76.1 %all-gather.7.cloned.1.call-start = ((), (), s32[]{:S(2)}) async-start(), calls=%async_computation.9 | async-start | bytes 6488064 | tf_op jit(solution)/shard_map/all_gather | solution.py:76
  7.9 184.0 %all-gather.9.cloned.1.call-start = ((), (), s32[]{:S(2)}) async-start(), calls=%async_computation.10 | async-start | bytes 9437184 | tf_op jit(solution)/shard_map/all_gather | solution.py:123
  57.2 32.0 %copy-start.17 = (f32[1024]{0:T(1024)}, f32[1024]{0:T(1024)S(1)}, u32[]{:S(2)}) copy-start(f32[1024]{0:T(1024)S(1)} %convert_element_type.136) | copy-start | bytes 12292
  57.2 32.0 %copy-start.19 = (f32[1024]{0:T(1024)}, f32[1024]{0:T(1024)S(1)}, u32[]{:S(2)}) copy-start(f32[1024]{0:T(1024)S(1)} %convert_element_type.137) | copy-start | bytes 12292
  58.5 30.8 %copy-start.23 = (f32[256]{0:T(256)}, f32[256]{0:T(256)S(1)}, u32[]{:S(2)}) copy-start(f32[256]{0:T(256)S(1)} %broadcast_multiply_fusion.5) | copy-start | bytes 3076
  60.0 29.3 %copy-start.27 = (f32[256]{0:T(256)}, f32[256]{0:T(256)S(1)}, u32[]{:S(2)}) copy-start(f32[256]{0:T(256)S(1)} %add_rsqrt_fusion.1) | copy-start | bytes 3076
  139.2 240.1 %all-gather.11.cloned.1.call-start = ((), (), s32[]{:S(2)}) async-start(), calls=%async_computation.11 | async-start | bytes 2162688 | tf_op jit(solution)/shard_map/all_gather | solution.py:79
  140.0 242.3 %all-gather.13.cloned.1.call-start = ((), (), s32[]{:S(2)}) async-start(), calls=%async_computation.12 | async-start | bytes 8650752 | tf_op jit(solution)/shard_map/all_gather | solution.py:164
  140.5 279.3 %all-gather.15.cloned.1.call-start = ((), (), s32[]{:S(2)}) async-start(), calls=%async_computation.13 | async-start | bytes 8650752 | tf_op jit(solution)/shard_map/all_gather | solution.py:166
  260.6 7.5 copy-start.35
  261.2 118.1 %copy-start.5 = (bf16[256,1024]{1,0:T(8,128)(2,1)S(1)}, bf16[256,1024]{1,0:T(8,128)(2,1)}, u32[]{:S(2)}) copy-start(bf16[256,1024]{1,0:T(8,128)(2,1)} %param.24) | copy-start | bytes 1572868
  263.4 110.8 %all-to-all-start.1 = ((bf16[4,2,32768]{2,1,0:T(2,128)(2,1)}), bf16[4,2,32768]{2,1,0:T(2,128)(2,1)}, u32[]{:S(2)}, u32[]{:S(2)}) async-start(bf16[4,2,32768]{2,1,0:T(2,128)(2,1)} %reshape.311), calls=%async_computation.1 | async-start | bytes 1048576 | tf_op jit(solution)/shard_map/all_to_all | solution.py:151
  268.1 166.8 %copy-start.13 = (f32[1024]{0:T(1024)}, f32[1024]{0:T(1024)S(1)}, u32[]{:S(2)}) copy-start(f32[1024]{0:T(1024)S(1)} %convert_element_type.143) | copy-start | bytes 12292
  268.1 114.2 %copy-start.15 = (f32[1024]{0:T(1024)}, f32[1024]{0:T(1024)S(1)}, u32[]{:S(2)}) copy-start(f32[1024]{0:T(1024)S(1)} %convert_element_type.144) | copy-start | bytes 12292
  381.9 52.9 %copy-start.1 = (f32[256,1024]{1,0:T(8,128)}, f32[256,1024]{1,0:T(8,128)S(1)}, u32[]{:S(2)}) copy-start(f32[256,1024]{1,0:T(8,128)S(1)} %get-tuple-element.1062) | copy-start | bytes 3145732
  382.0 52.9 %copy-start.21 = (f32[256]{0:T(256)}, f32[256]{0:T(256)S(1)}, u32[]{:S(2)}) copy-start(f32[256]{0:T(256)S(1)} %broadcast_multiply_fusion.4) | copy-start | bytes 3076
  382.2 52.7 %copy-start.25 = (f32[256]{0:T(256)}, f32[256]{0:T(256)S(1)}, u32[]{:S(2)}) copy-start(f32[256]{0:T(256)S(1)} %add_rsqrt_fusion) | copy-start | bytes 3076
  382.3 37.5 %copy-start.10 = (bf16[256,1024]{1,0:T(8,128)(2,1)S(1)}, bf16[256,1024]{1,0:T(8,128)(2,1)}, u32[]{:S(2)}) copy-start(bf16[256,1024]{1,0:T(8,128)(2,1)} %param.25) | copy-start | bytes 1572868
  419.8 11.8 copy-start.36
  431.7 3.2 copy-start.12
  431.7 5.3 copy-start.8
  436.0 1.0 copy-start.3
  438.5 18.6 %all-to-all-start.2 = ((bf16[256,4,256]{2,0,1:T(8,128)(2,1)}), bf16[256,4,256]{2,0,1:T(8,128)(2,1)S(1)}, u32[]{:S(2)}, u32[]{:S(2)}) async-start(bf16[256,4,256]{2,0,1:T(8,128)(2,1)} %bitcast.128), calls=%async_computation.2 | async-start | bytes 1048576 | tf_op jit(solution)/shard_map/all_to_all | solution.py:207
  442.0 436.2 %reduce-scatter.6.cloned.1.call-start = ((), (), s32[]{:S(2)}) async-start(), calls=%async_computation.14 | async-start | bytes 9437184 | tf_op jit(solution)/shard_map/reduce_scatter | solution.py:259
  507.6 2.7 copy-start
  559.2 1.2 copy-start.4
  559.2 1.4 copy-start.9
  559.3 481.2 %reduce-scatter.10.cloned.1.call-start = ((), (), s32[]{:S(2)}) async-start(), calls=%async_computation.16 | async-start | bytes 4325376 | tf_op jit(solution)/shard_map/reduce_scatter | solution.py:299
  563.3 622.8 %reduce-scatter.8.cloned.1.call-start = ((), (), s32[]{:S(2)}) async-start(), calls=%async_computation.15 | async-start | bytes 12976128 | tf_op jit(solution)/shard_map/reduce_scatter | solution.py:296
  945.7 4.0 copy-start.6
  945.7 4.0 copy-start.18
  945.7 4.0 copy-start.20
  945.7 4.0 copy-start.24
  945.7 4.0 copy-start.28
  957.7 1.0 copy-start.11
  957.7 413.1 %reduce-scatter.14.cloned.1.call-start = ((), (), s32[]{:S(2)}) async-start(), calls=%async_computation.18 | async-start | bytes 17301504 | tf_op jit(solution)/shard_map/reduce_scatter | solution.py:200
  969.5 1.2 copy-start.2
  969.5 1.2 copy-start.14
  969.5 1.2 copy-start.16
  969.5 1.2 copy-start.22
  969.5 1.2 copy-start.26
  969.6 588.5 %reduce-scatter.12.cloned.1.call-start = ((), (), s32[]{:S(2)}) async-start(), calls=%async_computation.17 | async-start | bytes 17301504 | tf_op jit(solution)/shard_map/reduce_scatter | solution.py:198
  981.3 8.4 copy-start.7
  990.0 5.1 copy-start.29
  990.0 5.1 copy-start.30
  990.0 5.1 copy-start.31
  990.0 5.1 copy-start.32
  990.0 5.1 copy-start.33
  (1 other events, 0.7 us)
Sparse Core Ops, SparseCore 0:
  10.9 72.3 all-gather.6
  139.4 52.5 all-gather.8
  194.8 56.4 all-gather.10
  254.0 82.2 all-gather.12
  339.1 80.6 all-gather.14
  559.4 318.7 reduce-scatter.5
  881.2 145.4 reduce-scatter.9
  1034.3 151.7 reduce-scatter.7
  1189.0 181.8 reduce-scatter.13
  1373.5 184.4 reduce-scatter.11
where the time goes:
time: 1580 us; the launch traced here: 1570 us
  waiting for transfers between devices  951 us (60%)
  blocking collectives  289 us (18%)
  local copies, waits for them, and re-layouts  122 us (8%)
  matrix products  118 us (7%)
  loops' own time  32.7 us (2%)
  other arithmetic  29.2 us (2%)
    reduce_scatter x1, waiting for transfers between devices, on_device(): lax.psum_scatter(grad_pairs.reshape(block_rows * n_blk, 2, group_width).a...  314 us
    reduce_scatter x1, waiting for transfers between devices, on_device(): lax.psum_scatter(up_weight_grad, ('head', 'blk'), scatter_dimension=0, ti...  187 us
    reduce_scatter x1, waiting for transfers between devices, on_device(): lax.psum_scatter(down_weight_grad, ('head', 'blk'), scatter_dimension=0,...  185 us
    reduce_scatter x1, waiting for transfers between devices, on_device(): lax.psum_scatter(in_weight_grad, ('head', 'blk'), scatter_dimension=0, ti...  146 us
    all_gather x1, blocking collectives, on_device(): lax.all_gather(up_bias, ('head', 'blk'), axis=0, tiled=True)  106 us
    unnamed x2, blocking collectives  81.4 us
    all_to_all x1, blocking collectives, on_device(): lax.all_to_all(grad_joint.reshape(block_rows, 3, 1, group_width), 'head',...  60.9 us
    all_gather x1, waiting for transfers between devices, on_device(): piece = lax.all_gather(kv_local, 'blk', axis=0, tiled=True)  49.6 us
  transfers between devices with their start and end apart: 12, of which 8 were waited for; matrix products, arithmetic and copies ran while one was open for 9% of the time, Pallas kernels for 0%

commit v1 on v0

v1 whole, which is shorter than its diff:
```python
import functools

import jax
import jax.numpy as jnp
from jax import lax
from jax.experimental import pallas as pl
from jax.experimental.pallas import tpu as pltpu
from jax.sharding import Mesh
from jax.sharding import PartitionSpec as P

HEADS = 16
HEAD_DIM = 64
DOCS = 4
BLOCK_Q = 512
BLOCK_K = 512
VMEM_BYTES = 56 * 1024 * 1024

EPS = 1e-05
NEGATIVE = -1e30
GELU_C = 0.7978845608028654
SCALE = HEAD_DIM ** (-0.5)
ALL = ("head", "u", "v", "rest")
f32 = jnp.float32
bf16 = jnp.bfloat16


def norm_forward(rows, gain, shift):
    center = rows - jnp.mean(rows, axis=-1, keepdims=True)
    var = jnp.mean(center * center, axis=-1, keepdims=True)
    inverse = lax.rsqrt(var + EPS)
    unit = center * inverse
    return (unit * gain + shift, unit, inverse)


def norm_inner(grad, unit, inverse, gain):
    scaled = grad * gain
    inner = (
        scaled
        - jnp.mean(scaled, axis=-1, keepdims=True)
        - unit * jnp.mean(scaled * unit, axis=-1, keepdims=True)
    )
    return inverse * inner


def gelu_parts(pre):
    cubic = pre * pre * pre
    tangent = jnp.tanh(GELU_C * (pre + 0.044715 * cubic))
    value = 0.5 * pre * (1.0 + tangent)
    slope = 0.5 * (1.0 + tangent) + 0.5 * pre * (1.0 - tangent * tangent) * GELU_C * (
        1.0 + 3.0 * 0.044715 * pre * pre
    )
    return (value, slope)


def shifted(x, axis, k):
    n = lax.axis_size(axis)
    return lax.ppermute(x, axis, [(i, (i + k) % n) for i in range(n)])


def put(buffer, x, index):
    return lax.dynamic_update_index_in_dim(buffer, x, index, 0)


def gather_axis(x, axis):
    n = lax.axis_size(axis)
    if n == 1:
        return x[None]
    me = lax.axis_index(axis)
    out = put(jnp.zeros((n,) + x.shape, x.dtype), x, me)
    for k in range(1, n):
        out = put(out, shifted(x, axis, k), (me - k) % n)
    return out


def gather_line(x, axis):
    n = lax.axis_size(axis)
    if n != 4:
        return gather_axis(x, axis)
    me = lax.axis_index(axis)
    up = [(i, i + 1) for i in range(n - 1)]
    down = [(i + 1, i) for i in range(n - 1)]
    left, right = [x], [x]
    for _ in range(n - 1):
        left.append(lax.ppermute(left[-1], axis, up))
        right.append(lax.ppermute(right[-1], axis, down))
    low = me < 2
    first = jnp.where(low, right[1], left[1])
    second = jnp.where(low, right[2], left[2])
    inner = jnp.where(me == 1, left[1], right[1])
    third = jnp.where(me == 0, right[3], jnp.where(me == 3, left[3], inner))
    out = put(jnp.zeros((n,) + x.shape, x.dtype), x, me)
    out = put(out, first, jnp.where(low, me + 1, me - 1))
    out = put(out, second, jnp.where(low, me + 2, me - 2))
    return put(out, third, jnp.where(me == 0, 3, jnp.where(me == 3, 0, jnp.where(me == 1, 0, 3))))


def reduce_axis(x, axis):
    n = lax.axis_size(axis)
    if n == 1:
        return x[0].astype(f32)
    me = lax.axis_index(axis)
    total = lax.dynamic_index_in_dim(x, me, 0, keepdims=False).astype(f32)
    for k in range(1, n):
        piece = lax.dynamic_index_in_dim(x, (me + k) % n, 0, keepdims=False)
        total = total + shifted(piece, axis, k).astype(f32)
    return total


def exchange_axis(x, axis):
    n = lax.axis_size(axis)
    if n == 1:
        return x
    me = lax.axis_index(axis)
    mine = lax.dynamic_index_in_dim(x, me, 0, keepdims=False)
    out = put(jnp.zeros_like(x), mine, me)
    for k in range(1, n):
        piece = lax.dynamic_index_in_dim(x, (me + k) % n, 0, keepdims=False)
        out = put(out, shifted(piece, axis, k), (me - k) % n)
    return out


def allowed_keys(kb, starts, pos):
    t = kb * BLOCK_K + lax.broadcasted_iota(jnp.int32, (BLOCK_K, BLOCK_Q), 0)
    return (t >= starts) & (t <= pos)


def lay_rows(kv_ref, rows_ref):
    def lay(i, _):
        rows_ref[pl.ds(pl.multiple_of(i * BLOCK_K, BLOCK_K), BLOCK_K), :] = kv_ref[i].T
        return 0

    lax.fori_loop(0, kv_ref.shape[0], lay, 0)


def forward_kernel(lo_ref, mid_ref, q0_ref, q_ref, kv_ref, start_ref, o_ref, wide_ref, lse_ref, rows_ref):
    step = pl.program_id(0)

    @pl.when(step == 0)
    def _():
        lay_rows(kv_ref, rows_ref)

    first = q0_ref[step]
    q = q_ref[0] * jnp.asarray(SCALE, bf16)
    q_pad = jnp.concatenate([q, jnp.zeros_like(q)], axis=0)
    starts = start_ref[0]
    pos = first + lax.broadcasted_iota(jnp.int32, (1, BLOCK_Q), 1)

    def body(masked, kb, carry):
        top, total, acc = carry
        rows = rows_ref[pl.ds(pl.multiple_of(kb * BLOCK_K, BLOCK_K), BLOCK_K), :]
        s = jnp.dot(rows, q_pad, preferred_element_type=f32)
        if masked:
            s = jnp.where(allowed_keys(kb, starts, pos), s, NEGATIVE)
        new_top = jnp.maximum(top, jnp.max(s, axis=0, keepdims=True))
        p = jnp.exp(s - new_top)
        factor = jnp.exp(top - new_top)
        values = kv_ref[kb, HEAD_DIM:, :]
        acc = acc * factor + jnp.dot(values, p.astype(bf16), preferred_element_type=f32)
        return (new_top, total * factor + jnp.sum(p, axis=0, keepdims=True), acc)

    diagonal = first // BLOCK_K
    mid = jnp.minimum(mid_ref[step], diagonal)
    carry = (
        jnp.full((1, BLOCK_Q), NEGATIVE, f32),
        jnp.zeros((1, BLOCK_Q), f32),
        jnp.zeros((HEAD_DIM, BLOCK_Q), f32),
    )
    carry = lax.fori_loop(lo_ref[step], mid, functools.partial(body, True), carry)
    carry = lax.fori_loop(mid, diagonal, functools.partial(body, False), carry)
    last = (first + BLOCK_Q + BLOCK_K - 1) // BLOCK_K
    top, total, acc = lax.fori_loop(diagonal, last, functools.partial(body, True), carry)
    out = acc / total
    wide_ref[0] = out
    lse_ref[0] = top + jnp.log(total)
    low = out.astype(bf16)
    piece = o_ref.shape[3]
    for i in range(o_ref.shape[0]):
        o_ref[i, 0] = low[:, i * piece : (i + 1) * piece]


def backward_kernel(
    n_steps, lo_ref, mid_ref, q0_ref, q_ref, kv_ref, start_ref, do_ref, wide_ref, lse_ref, dq_ref, dkv_ref, rows_ref, acc_ref
):
    step = pl.program_id(0)

    @pl.when(step == 0)
    def _():
        lay_rows(kv_ref, rows_ref)
        acc_ref[...] = jnp.zeros_like(acc_ref)

    @pl.when(step < n_steps)
    def _():
        first = q0_ref[step]
        q = q_ref[0] * jnp.asarray(SCALE, bf16)
        do = jnp.concatenate([do_ref[i, 0] for i in range(do_ref.shape[0])], axis=1)
        zero = jnp.zeros_like(q)
        q_pad = jnp.concatenate([q, zero], axis=0)
        do_pad = jnp.concatenate([zero, do], axis=0)
        q_rows = q_pad.T
        do_rows = do_pad.T
        starts = start_ref[0]
        lse = lse_ref[0]
        delta = jnp.sum(do.astype(f32) * wide_ref[0], axis=0, keepdims=True)
        pos = first + lax.broadcasted_iota(jnp.int32, (1, BLOCK_Q), 1)

        def body(masked, kb, dq):
            at = pl.ds(pl.multiple_of(kb * BLOCK_K, BLOCK_K), BLOCK_K)
            rows = rows_ref[at, :]
            s = jnp.dot(rows, q_pad, preferred_element_type=f32)
            p = jnp.exp(s - lse)
            if masked:
                p = jnp.where(allowed_keys(kb, starts, pos), p, 0.0)
            dp = jnp.dot(rows, do_pad, preferred_element_type=f32)
            ds = (p * (dp - delta)).astype(bf16)
            acc_ref[at, :] += jnp.dot(p.astype(bf16), do_rows, preferred_element_type=f32) + jnp.dot(
                ds, q_rows, preferred_element_type=f32
            )
            return dq + jnp.dot(kv_ref[kb, :HEAD_DIM, :], ds, preferred_element_type=f32)

        diagonal = first // BLOCK_K
        mid = jnp.minimum(mid_ref[step], diagonal)
        dq = jnp.zeros((HEAD_DIM, BLOCK_Q), f32)
        dq = lax.fori_loop(lo_ref[step], mid, functools.partial(body, True), dq)
        dq = lax.fori_loop(mid, diagonal, functools.partial(body, False), dq)
        last = (first + BLOCK_Q + BLOCK_K - 1) // BLOCK_K
        dq = lax.fori_loop(diagonal, last, functools.partial(body, True), dq)
        dq_ref[0] = (dq * SCALE).astype(bf16)

    @pl.when(step >= n_steps)
    def _():
        kb = jnp.maximum(step - n_steps, 0)
        at = pl.ds(pl.multiple_of(kb * BLOCK_K, BLOCK_K), BLOCK_K)
        dkv_ref[0] = acc_ref[at, :].astype(bf16).T


def attention_specs(block_rows, tok_rows, keys):
    subs = block_rows // BLOCK_Q
    pieces = BLOCK_Q // tok_rows
    n_kb = keys // BLOCK_K

    def wrap(index):
        return lambda i, *_: index(i)

    q_spec = lambda cap: pl.BlockSpec((1, HEAD_DIM, BLOCK_Q), wrap(lambda i: (cap(i) // subs, 0, cap(i) % subs)))
    row_spec = lambda cap: pl.BlockSpec((1, 1, BLOCK_Q), wrap(lambda i: (cap(i) // subs, 0, cap(i) % subs)))
    piece_spec = lambda cap: pl.BlockSpec(
        (pieces, 1, HEAD_DIM, tok_rows), wrap(lambda i: (cap(i) % subs, cap(i) // subs, 0, 0))
    )
    kv_spec = pl.BlockSpec(
        (n_kb, 2 * HEAD_DIM, BLOCK_K), wrap(lambda i: (0, 0, 0)), pipeline_mode=pl.Buffered(1)
    )
    return q_spec, row_spec, piece_spec, kv_spec


def attention_forward(bounds, qkv, kv, starts, n_head, tok_rows):
    hb, _, block_rows = qkv.shape
    keys = kv.shape[0] * BLOCK_K
    n_steps = hb * block_rows // BLOCK_Q
    q_spec, row_spec, piece_spec, kv_spec = attention_specs(block_rows, tok_rows, keys)
    same = lambda i: i
    return pl.pallas_call(
        forward_kernel,
        grid_spec=pltpu.PrefetchScalarGridSpec(
            num_scalar_prefetch=3,
            grid=(n_steps,),
            in_specs=[q_spec(same), kv_spec, row_spec(same)],
            out_specs=[piece_spec(same), q_spec(same), row_spec(same)],
            scratch_shapes=[pltpu.VMEM((keys, 2 * HEAD_DIM), bf16)],
        ),
        out_shape=[
            jax.ShapeDtypeStruct((n_head, hb, HEAD_DIM, tok_rows), bf16),
            jax.ShapeDtypeStruct((hb, HEAD_DIM, block_rows), f32),
            jax.ShapeDtypeStruct((hb, 1, block_rows), f32),
        ],
        compiler_params=pltpu.CompilerParams(vmem_limit_bytes=VMEM_BYTES),
        name="attention_forward",
    )(*bounds, qkv, kv, starts)


def attention_backward(bounds, qkv, kv, starts, do, wide, lse):
    hb, _, block_rows = qkv.shape
    n_kb = kv.shape[0]
    keys = n_kb * BLOCK_K
    n_steps = hb * block_rows // BLOCK_Q
    q_spec, row_spec, piece_spec, kv_spec = attention_specs(block_rows, do.shape[3], keys)
    cap = lambda i: jnp.minimum(i, n_steps - 1)
    return pl.pallas_call(
        functools.partial(backward_kernel, n_steps),
        grid_spec=pltpu.PrefetchScalarGridSpec(
            num_scalar_prefetch=3,
            grid=(n_steps + n_kb,),
            in_specs=[q_spec(cap), kv_spec, row_spec(cap), piece_spec(cap), q_spec(cap), row_spec(cap)],
            out_specs=[
                q_spec(cap),
                pl.BlockSpec((1, 2 * HEAD_DIM, BLOCK_K), lambda i, *_: (jnp.maximum(i - n_steps, 0), 0, 0)),
            ],
            scratch_shapes=[pltpu.VMEM((keys, 2 * HEAD_DIM), bf16), pltpu.VMEM((keys, 2 * HEAD_DIM), f32)],
        ),
        out_shape=[
            jax.ShapeDtypeStruct((hb, HEAD_DIM, block_rows), bf16),
            jax.ShapeDtypeStruct((n_kb, 2 * HEAD_DIM, BLOCK_K), bf16),
        ],
        compiler_params=pltpu.CompilerParams(vmem_limit_bytes=VMEM_BYTES),
        name="attention_backward",
    )(*bounds, qkv, kv, starts, do, wide, lse)


def on_device(
    tokens,
    cotangent,
    segment,
    norm_gain,
    norm_shift,
    in_weight,
    query_bias,
    value_bias,
    out_weight,
    out_bias,
    post_gain,
    post_shift,
    up_weight,
    up_bias,
    down_weight,
    down_bias,
):
    n_head, n_u, n_v, n_rest = (lax.axis_size(a) for a in ALL)
    hb = n_u * n_v
    n_blk = hb * n_rest
    n_all = n_head * n_blk
    me_head, me_u, me_v, me_rest = (lax.axis_index(a) for a in ALL)
    me_blk = (me_u * n_v + me_v) * n_rest + me_rest
    tok_rows, width = tokens.shape
    block_rows = tok_rows * n_head
    length = segment.shape[0]
    w_rows = in_weight.shape[0]
    group = 3 * hb * HEAD_DIM

    w_up = lax.all_gather(up_weight, ALL, axis=0, tiled=True)
    w_down = lax.all_gather(down_weight, ALL, axis=0, tiled=True)
    w_out = lax.all_gather(out_weight, ALL, axis=0, tiled=True)

    parts = [norm_gain, norm_shift, query_bias, value_bias, out_bias, post_gain, post_shift, down_bias, up_bias]
    packed = jnp.concatenate(parts).reshape(1, -1)
    for axis in ("rest", "v", "u", "head"):
        packed = gather_axis(packed, axis)
    packed = packed.reshape(n_all, -1)
    vectors, at = [], 0
    for part in parts:
        size = part.shape[0]
        vectors.append(packed[:, at : at + size].reshape(-1).astype(f32))
        at += size
    gain_a, shift_a, bias_q, bias_v, bias_out, gain_b, shift_b, bias_down, bias_up = vectors

    cols = in_weight.reshape(w_rows, 3, n_head, hb, HEAD_DIM).transpose(2, 0, 3, 1, 4).reshape(n_head, w_rows, group)
    w_in = exchange_axis(cols, "head")
    for axis in ("v", "u", "rest"):
        w_in = gather_axis(w_in, axis)
    w_in = w_in.transpose(3, 1, 2, 0, 4, 5).reshape(width, group)

    rows_all = gather_line(tokens, "head").reshape(block_rows, width).astype(f32)
    normed, unit_all, inverse_all = norm_forward(rows_all, gain_a, shift_a)
    normed_low = normed.astype(bf16)
    group_bias = jnp.stack([bias_q, jnp.zeros_like(bias_q), bias_v]).reshape(3, n_head, hb, HEAD_DIM)
    group_bias = lax.dynamic_index_in_dim(group_bias, me_head, 1, keepdims=False).transpose(1, 0, 2).reshape(group, 1)
    projected = lax.dot_general(w_in, normed_low, (((0,), (1,)), ((), ())), preferred_element_type=f32)
    projected = (projected + group_bias).astype(bf16)
    qkv = lax.all_to_all(
        projected.reshape(hb, 3 * HEAD_DIM, block_rows), ("u", "v"), split_axis=0, concat_axis=0, tiled=True
    )
    subs_k = block_rows // BLOCK_K
    kv = gather_axis(qkv[:, HEAD_DIM:], "rest")
    kv = kv.reshape(n_rest, hb, 2 * HEAD_DIM, subs_k, BLOCK_K).transpose(1, 0, 3, 2, 4)
    kv = kv.reshape(n_blk * subs_k, 2 * HEAD_DIM, BLOCK_K)

    doc_start = jnp.zeros_like(segment)
    for doc in range(1, DOCS):
        first = jnp.sum((segment < doc).astype(jnp.int32))
        doc_start = jnp.where(segment == doc, first, doc_start)
    starts = lax.dynamic_index_in_dim(doc_start.reshape(hb, n_rest, block_rows), me_rest, 1, keepdims=False)
    starts_q = starts.reshape(-1, BLOCK_Q)
    lo = starts_q[:, 0] // BLOCK_K
    mid = (starts_q[:, -1] + BLOCK_K - 1) // BLOCK_K
    q_first = (jnp.arange(hb, dtype=jnp.int32)[:, None] * n_rest + me_rest) * block_rows
    q_first = (q_first + jnp.arange(block_rows // BLOCK_Q, dtype=jnp.int32)[None] * BLOCK_Q).reshape(-1)
    bounds = (lo, mid, q_first)
    starts = starts.reshape(hb, 1, block_rows)

    attended, wide, lse = attention_forward(bounds, qkv, kv, starts, n_head, tok_rows)
    back = lax.all_to_all(
        attended.reshape(HEADS, HEAD_DIM, tok_rows), ("head", "u", "v"), split_axis=0, concat_axis=0, tiled=True
    ).reshape(width, tok_rows)

    rows = tokens.astype(f32)
    branch = lax.dot_general(back, w_out, (((0,), (0,)), ((), ())), preferred_element_type=f32) + bias_out
    middle = rows + branch
    hidden_in, unit_mid, inverse_mid = norm_forward(middle, gain_b, shift_b)
    hidden_low = hidden_in.astype(bf16)
    pre = jnp.dot(hidden_low, w_up, preferred_element_type=f32) + bias_up
    act, slope = gelu_parts(pre)
    act_low = act.astype(bf16)
    result = middle + jnp.dot(act_low, w_down, preferred_element_type=f32) + bias_down
    output = result.astype(bf16)
    grad_out = cotangent.astype(f32)
    grad_act = jnp.einsum("td,fd->tf", cotangent, w_down, preferred_element_type=f32)
    grad_pre = (grad_act * slope).astype(bf16)
    grad_hidden = jnp.einsum("tf,df->td", grad_pre, w_up, preferred_element_type=f32)
    grad_middle = grad_out + norm_inner(grad_hidden, unit_mid, inverse_mid, gain_b)
    grad_branch = grad_middle.astype(bf16)
    grad_back = lax.dot_general(w_out, grad_branch, (((1,), (1,)), ((), ())), preferred_element_type=f32).astype(bf16)
    grad_heads = lax.all_to_all(
        grad_back.reshape(HEADS, HEAD_DIM, tok_rows), ("head", "u", "v"), split_axis=0, concat_axis=0, tiled=True
    ).reshape(n_head, hb, HEAD_DIM, tok_rows)

    down_grad = jnp.einsum("tf,td->fd", act_low, cotangent, preferred_element_type=f32).astype(bf16)
    up_grad = jnp.einsum("td,tf->df", hidden_low, grad_pre, preferred_element_type=f32).astype(bf16)
    out_grad = jnp.einsum("dt,te->de", back, grad_branch, preferred_element_type=f32).astype(bf16)
    down_weight_grad = lax.psum_scatter(down_grad, ALL, scatter_dimension=0, tiled=True).astype(f32)
    up_weight_grad = lax.psum_scatter(up_grad, ALL, scatter_dimension=0, tiled=True).astype(f32)
    out_weight_grad = lax.psum_scatter(out_grad, ALL, scatter_dimension=0, tiled=True).astype(f32)
    sums = [
        jnp.sum(grad_branch.astype(f32), axis=0),
        jnp.sum(grad_hidden * unit_mid, axis=0),
        jnp.sum(grad_hidden, axis=0),
        jnp.sum(grad_out, axis=0),
        jnp.sum(grad_pre.astype(f32), axis=0),
    ]
    small = jnp.concatenate([s.reshape(n_all, -1) for s in sums], axis=1)
    small = small.reshape(n_head, n_u, n_v, n_rest, 1, -1)
    small = reduce_axis(small, "head")
    for axis in ("u", "v", "rest"):
        small = reduce_axis(small, axis)
    small = small.reshape(-1)
    size = width // n_all
    out_bias_grad, post_gain_grad, post_shift_grad, down_bias_grad = (
        small[i * size : (i + 1) * size] for i in range(4)
    )
    up_bias_grad = small[4 * size :]

    dq, dkv = attention_backward(bounds, qkv, kv, starts, grad_heads, wide, lse)
    dkv = dkv.reshape(hb, n_rest, subs_k, 2 * HEAD_DIM, BLOCK_K).transpose(1, 0, 3, 2, 4)
    dkv = reduce_axis(dkv.reshape(n_rest, hb, 2 * HEAD_DIM, block_rows), "rest").astype(bf16)
    grad_proj = lax.all_to_all(
        jnp.concatenate([dq, dkv], axis=1), ("u", "v"), split_axis=0, concat_axis=0, tiled=True
    ).reshape(group, block_rows)

    grad_normed = lax.dot_general(grad_proj, w_in, (((0,), (1,)), ((), ())), preferred_element_type=f32)
    grad_tokens = reduce_axis(grad_normed.astype(bf16).reshape(n_head, tok_rows, width), "head")
    unit_in = lax.dynamic_index_in_dim(unit_all.reshape(n_head, tok_rows, width), me_head, 0, keepdims=False)
    inverse_in = lax.dynamic_index_in_dim(inverse_all.reshape(n_head, tok_rows, 1), me_head, 0, keepdims=False)
    tokens_grad = (grad_middle + norm_inner(grad_tokens, unit_in, inverse_in, gain_a)).astype(bf16)

    in_grad = lax.dot_general(normed_low, grad_proj, (((0,), (1,)), ((), ())), preferred_element_type=f32)
    gain_grad = jnp.sum(grad_normed * unit_all, axis=0).reshape(n_head, n_blk, w_rows)
    shift_grad = jnp.sum(grad_normed, axis=0).reshape(n_head, n_blk, w_rows)
    col_sum = jnp.sum(grad_proj.astype(f32), axis=1).reshape(hb, 3, HEAD_DIM)
    mine = (jnp.arange(n_head) == me_head)[:, None, None]
    query_sum = jnp.where(mine, col_sum[:, 0].reshape(1, n_blk, w_rows), 0.0)
    value_sum = jnp.where(mine, col_sum[:, 2].reshape(1, n_blk, w_rows), 0.0)
    extra = jnp.stack([gain_grad, shift_grad, query_sum, value_sum], axis=-1)
    extra = jnp.pad(extra, ((0, 0), (0, 0), (0, 0), (0, 124)))
    joined = jnp.concatenate([in_grad.reshape(n_head, n_blk, w_rows, group), extra], axis=-1).astype(bf16)
    joined = joined.transpose(1, 0, 2, 3).reshape(hb, n_rest, n_head, w_rows, group + 128).transpose(1, 0, 2, 3, 4)
    joined = reduce_axis(joined, "rest").astype(bf16).reshape(n_u, n_v, n_head, w_rows, group + 128)
    joined = reduce_axis(joined, "u").astype(bf16)
    joined = reduce_axis(joined, "v").astype(bf16)
    joined = exchange_axis(joined, "head").astype(f32)
    in_weight_grad = joined[:, :, :group].reshape(n_head, w_rows, hb, 3, HEAD_DIM).transpose(1, 3, 0, 2, 4)
    in_weight_grad = in_weight_grad.reshape(w_rows, 3 * width)
    extra = jnp.sum(joined[:, :, group : group + 4], axis=0)
    return (
        output,
        tokens_grad,
        extra[:, 0],
        extra[:, 1],
        in_weight_grad,
        extra[:, 2],
        extra[:, 3],
        out_weight_grad,
        out_bias_grad,
        post_gain_grad,
        post_shift_grad,
        up_weight_grad,
        up_bias_grad,
        down_weight_grad,
        down_bias_grad,
    )


def solution(mesh):
    n_head, n_blk = mesh.shape["head"], mesh.shape["blk"]
    hb = HEADS // n_head
    n_u = 2 if hb % 2 == 0 else 1
    fine = Mesh(mesh.devices.reshape(n_head, n_u, hb // n_u, n_blk // hb), ALL)
    tok = P(("u", "v", "rest", "head"), None)
    vec = P(ALL)
    mat = P(ALL, None)
    return jax.shard_map(
        on_device,
        mesh=fine,
        in_specs=(tok, tok, P(), vec, vec, mat, vec, vec, mat, vec, vec, vec, mat, vec, mat, vec),
        out_specs=(tok, tok, vec, vec, mat, vec, vec, mat, vec, vec, vec, mat, vec, mat, vec),
        check_vma=False,
    )
```

time: 1580 us -> 723 us (0.46)
  waiting for transfers between devices: 951 us -> 364 us
  blocking collectives: 289 us -> 0 us
  Pallas kernels: 0 us -> 94.6 us
  starting transfers between devices: 8.97 us -> 101 us
  local copies, waits for them, and re-layouts: 122 us -> 56.6 us
  matrix products: 118 us -> 62.4 us
  loops' own time: 32.7 us -> 0 us
    reduce_scatter x5 -> x3, waiting for transfers between devices: 831 us -> 177 us  [the longest x1 147 us: on_device(): lax.psum_scatter(down_grad, ALL, scatter_dimension=0, tiled=True)]
    ppermute x0 -> x35, waiting for transfers between devices: none -> 127 us  [the longest x29 110 us: shifted(): return lax.ppermute(x, axis, [(i, (i + k) % n) for i in range(n)])]
    all_gather x1 -> x0, blocking collectives: 106 us -> none  [on_device(): lax.all_gather(up_bias, ('head', 'blk'), axis=0, tiled=True)]
    all_to_all x2 -> x0, blocking collectives: 101 us -> none  [the longest x1 60.9 us: on_device(): lax.all_to_all(grad_joint.reshape(block_rows, 3, 1, group_width), 'head',...]
    all_gather x5 -> x3, waiting for transfers between devices: 102 us -> 1.95 us  [the longest x1 1.93 us: on_device(): w_down = lax.all_gather(down_weight, ALL, axis=0, tiled=True)]
    pallas_call x0 -> x2, Pallas kernels: none -> 94.6 us  [the longest x1 54.1 us: attention_backward(): pl.pallas_call(functools.partial(backward_kernel, n_steps), grid_spec=plt...]
    unnamed x2 -> x0, blocking collectives: 81.4 us -> none
    ppermute x0 -> x35, starting transfers between devices: none -> 58.1 us  [the longest x29 39 us: shifted(): return lax.ppermute(x, axis, [(i, (i + k) % n) for i in range(n)])]
  transfers between devices with their start and end apart: 12 -> 45, of which waited for: 8 -> 24; matrix products, arithmetic and copies ran while one was open for 9% -> 17% of each run, Pallas kernels for 0% -> 13%
where the time goes in v1:
time: 723 us; the launch traced here: 717 us
  waiting for transfers between devices  364 us (50%)
  starting transfers between devices  101 us (14%)
  Pallas kernels  94.6 us (13%)
  matrix products  62.4 us (9%)
  local copies, waits for them, and re-layouts  56.6 us (8%)
  other arithmetic  23.6 us (3%)
  between operations  15.2 us (2%)
    reduce_scatter x1, waiting for transfers between devices, on_device(): lax.psum_scatter(down_grad, ALL, scatter_dimension=0, tiled=True)  147 us
    ppermute x29, waiting for transfers between devices, shifted(): return lax.ppermute(x, axis, [(i, (i + k) % n) for i in range(n)])  110 us
    pallas_call x1, Pallas kernels, attention_backward(): pl.pallas_call(functools.partial(backward_kernel, n_steps), grid_spec=plt...  54.1 us
    pallas_call x1, Pallas kernels, attention_forward(): pl.pallas_call(forward_kernel, grid_spec=pltpu.PrefetchScalarGridSpec(num...  40.5 us
    ppermute x29, starting transfers between devices, shifted(): return lax.ppermute(x, axis, [(i, (i + k) % n) for i in range(n)])  39 us
    reduce_scatter x1, waiting for transfers between devices, on_device(): lax.psum_scatter(up_grad, ALL, scatter_dimension=0, tiled=True).astype(f32)  30.2 us
    all_to_all x1, waiting for transfers between devices, on_device(): lax.all_to_all(projected.reshape(hb, 3 * HEAD_DIM, block_rows), ('u', 'v'...  22.9 us
    all_to_all x1, waiting for transfers between devices, on_device(): lax.all_to_all(attended.reshape(HEADS, HEAD_DIM, tok_rows), ('head', 'u',...  18.8 us
  transfers between devices with their start and end apart: 45, of which 24 were waited for; matrix products, arithmetic and copies ran while one was open for 17% of the time, Pallas kernels for 13%

profile of v1, /device:TPU:0, one launch (start us, length us, event | category | flops | bytes accessed | tf_op | source)
XLA Modules:
  0.0 716.7 jit_solution(12434829956525295556)
XLA Ops:
  10.7 6.4 collective-permute-start.7
  17.1 6.1 concatenate.25
  38.0 3.3 collective-permute-done.15
  41.4 4.4 collective-permute-done.16
  47.0 2.5 collective-permute-done.17
  49.5 3.0 collective-permute-start.2
  56.1 7.6 %collective-permute-done.3 = bf16[4,32,768]{2,1,0:T(8,128)(2,1)S(1)} collective-permute-done((bf16[4,32,768]{2,1,0:T(8,128)(2,1)S(1)}, bf16[4,32,768]{2,1,0:T(8,128)(2,1)S(1)}, u32[]{:S(2)}, u32[]{:S(2)}) %collective-permute-start.3) | collective-permute-done | bytes 196640 | tf_op jit(solution)/shard_map/ppermute | solution.py:57
  66.8 4.6 collective-permute-start.9
  73.3 3.3 collective-permute-done.8
  78.4 4.3 collective-permute-start.11
  83.0 9.4 %collective-permute-done.10 = bf16[256,1024]{1,0:T(8,128)(2,1)S(1)} collective-permute-done((bf16[256,1024]{1,0:T(8,128)(2,1)S(1)}, bf16[256,1024]{1,0:T(8,128)(2,1)S(1)}, u32[]{:S(2)}, u32[]{:S(2)}) %collective-permute-start.10) | collective-permute-done | bytes 524320 | tf_op jit(solution)/shard_map/ppermute | solution.py:85
  92.5 3.8 collective-permute-done.11
  97.7 2.8 subtract_multiply_fusion
  100.5 3.1 add_convert_fusion.2
  103.6 15.0 %all-to-all-start = ((bf16[4,192,1024]{2,1,0:T(8,128)(2,1)}), bf16[4,192,1024]{2,1,0:T(8,128)(2,1)}, u32[]{:S(2)}, u32[]{:S(2)}) async-start(bf16[4,192,1024]{2,1,0:T(8,128)(2,1)} %bitcast.266), calls=%async_computation | async-start | bytes 3145728 | tf_op jit(solution)/shard_map/all_to_all | solution.py:367
  119.3 22.9 %all-to-all-done.q_ref = bf16[4,192,1024]{2,1,0:T(8,128)(2,1)} async-done(((bf16[4,192,1024]{2,1,0:T(8,128)(2,1)}), bf16[4,192,1024]{2,1,0:T(8,128)(2,1)}, u32[]{:S(2)}, u32[]{:S(2)}) %all-to-all-start) | async-done | bytes 1572896 | tf_op jit(solution)/shard_map/all_to_all | solution.py:367
  156.7 4.1 copy.139
  160.9 40.5 %attention_forward.1 = (bf16[4,4,64,256]{3,2,1,0:T(8,128)(2,1)}, f32[4,64,1024]{2,1,0:T(8,128)}, f32[4,1,1024]{2,1,0:T(1,128)}) custom-call(s32[8]{0:T(128)} %get-tuple-element.95.lo_ref, s32[8]{0:T(128)} %get-tuple-element.94.mid_ref, s32[8]{0:T(128)} %add.426.q0_ref, bf16[4,192,1024]{2,1,0:T(8,128)(2,1)} %all-to-all-done.q_ref, ...), custom_call_target="tpu_custom_call" | custom-call | tf_op jit(solution)/shard_map/attention_forward/pallas_call | solution.py:261
  201.4 15.1 %all-to-all-start.1 = ((bf16[16,64,256]{2,1,0:T(8,128)(2,1)}), bf16[16,64,256]{2,1,0:T(8,128)(2,1)S(1)}, u32[]{:S(2)}, u32[]{:S(2)}) async-start(bf16[16,64,256]{2,1,0:T(8,128)(2,1)} %bitcast.269), calls=%async_computation.1 | async-start | bytes 1048576 | tf_op jit(solution)/shard_map/all_to_all | solution.py:389
  216.7 18.8 %all-to-all-done.1 = bf16[16,64,256]{2,1,0:T(8,128)(2,1)S(1)} async-done(((bf16[16,64,256]{2,1,0:T(8,128)(2,1)}), bf16[16,64,256]{2,1,0:T(8,128)(2,1)S(1)}, u32[]{:S(2)}, u32[]{:S(2)}) %all-to-all-start.1) | async-done | bytes 524320 | tf_op jit(solution)/shard_map/all_to_all | solution.py:389
  236.4 2.7 fusion.60
  239.3 7.8 %convolution_add_fusion = f32[256,4096]{1,0:T(8,128)} fusion(bf16[1024,4096]{1,0:T(8,128)(2,1)} %all-gather.6.cloned.1.call-done, f32[4096]{0:T(1024)S(1)} %fusion.39, f32[256,1024]{1,0:T(8,128)S(1)} %get-tuple-element.89, f32[1024]{0:T(1024)S(1)} %reshape.411, f32[1024]{0:T(1024)S(1)} %reshape.410, f32[256]{0:T(256)S(1)} %add_rsqrt_fusion.1, ...), kind=kOutput, calls=%fused_computation.5 | convolution fusion | flops 2149842944 | bytes 13658112 | tf_op jit(solution)/shard_map/dot_general | solution.py:398
  249.1 7.8 %convert_reduce_fusion = (f32[4096]{0:T(1024)S(1)}, bf16[256,4096]{1,0:T(8,128)(2,1)S(1)}) fusion(f32[256,4096]{1,0:T(8,128)} %convolution_add_fusion, bf16[256,1024]{1,0:T(8,128)(2,1)} %param.17, bf16[4096,1024]{1,0:T(8,128)(2,1)} %all-gather.8.cloned.1.call-done), kind=kOutput, calls=%fused_computation.16 | convolution fusion | flops 2169499648 | bytes 15220736 | tf_op jit(solution)/shard_map/td,fd->tf/dot_general | solution.py:404
  257.0 2.7 multiply_reduce_fusion.2
  263.4 7.3 %convolution_convert_fusion.1 = bf16[1024,4096]{1,0:T(8,128)(2,1)} fusion(bf16[256,4096]{1,0:T(8,128)(2,1)} %copy-done.6, f32[256,1024]{1,0:T(8,128)S(1)} %get-tuple-element.89, f32[1024]{0:T(1024)S(1)} %reshape.411, f32[1024]{0:T(1024)S(1)} %reshape.410, f32[256]{0:T(256)S(1)} %add_rsqrt_fusion.1, f32[256]{0:T(256)S(1)} %broadcast_multiply_fusion.5), kind=kOutput, calls=%fused_computation.1 | convolution fusion | flops 2152988672 | bytes 11544576 | tf_op jit(solution)/shard_map/td,tf->df/dot_general | solution.py:415
  271.2 8.6 %convolution_convert_fusion = bf16[4096,1024]{1,0:T(8,128)(2,1)} fusion(bf16[256,1024]{1,0:T(8,128)(2,1)} %param.17, f32[256,4096]{1,0:T(8,128)} %convolution_add_fusion), kind=kOutput, calls=%fused_computation | convolution fusion | flops 2161115136 | bytes 13107200 | tf_op jit(solution)/shard_map/tf,td->fd/dot_general | solution.py:414
  279.8 3.5 fusion.14
  285.3 7.4 %all-to-all-start.2 = ((bf16[16,64,256]{2,1,0:T(8,128)(2,1)}), bf16[16,64,256]{2,1,0:T(8,128)(2,1)}, u32[]{:S(2)}, u32[]{:S(2)}) async-start(bf16[16,64,256]{2,1,0:T(8,128)(2,1)} %bitcast.264), calls=%async_computation.2 | async-start | bytes 1048576 | tf_op jit(solution)/shard_map/all_to_all | solution.py:410
  292.7 13.8 %all-to-all-done.2 = bf16[16,64,256]{2,1,0:T(8,128)(2,1)} async-done(((bf16[16,64,256]{2,1,0:T(8,128)(2,1)}), bf16[16,64,256]{2,1,0:T(8,128)(2,1)}, u32[]{:S(2)}, u32[]{:S(2)}) %all-to-all-start.2) | async-done | bytes 524320 | tf_op jit(solution)/shard_map/all_to_all | solution.py:410
  306.5 54.1 %attention_backward.1 = (bf16[4,64,1024]{2,1,0:T(8,128)(2,1)}, bf16[16,128,512]{2,1,0:T(8,128)(2,1)}) custom-call(s32[8]{0:T(128)} %get-tuple-element.95.lo_ref, s32[8]{0:T(128)} %get-tuple-element.94.mid_ref, s32[8]{0:T(128)} %add.426.q0_ref, bf16[4,192,1024]{2,1,0:T(8,128)(2,1)} %all-to-all-done.q_ref, bf16[16,128,512]{2,1,0:T(8,128)(2,1)} %bitcast.248, ...), custom_call_target="tpu_custom_call" | custom-call | tf_op jit(solution)/shard_map/attention_backward/pallas_call | solution.py:287
  360.6 4.1 copy.141
  377.0 3.9 copy.143
  380.9 4.5 all-to-all-start.3
  387.6 18.6 %collective-permute-done.32 = f32[2,2,1,256]{3,2,1,0:T(1,128)S(1)} collective-permute-done((f32[2,2,1,256]{3,2,1,0:T(1,128)S(1)}, f32[2,2,1,256]{3,2,1,0:T(1,128)S(1)}, u32[]{:S(2)}, u32[]{:S(2)}) %collective-permute-start.32) | collective-permute-done | bytes 4128 | tf_op jit(solution)/shard_map/ppermute | solution.py:57
  406.8 3.0 collective-permute-done.33
  411.8 6.6 multiply_reduce_fusion
  420.1 2.9 copy.144
  424.4 3.3 convolution_convert_fusion.3
  429.9 7.0 fusion.13
  437.6 2.6 collective-permute-start.22
  443.1 13.9 %collective-permute-done.22 = bf16[256,1024]{1,0:T(8,128)(2,1)S(1)} collective-permute-done((bf16[256,1024]{1,0:T(8,128)(2,1)S(1)}, bf16[256,1024]{1,0:T(8,128)(2,1)S(1)}, u32[]{:S(2)}, u32[]{:S(2)}) %collective-permute-start.22) | collective-permute-done | bytes 524320 | tf_op jit(solution)/shard_map/ppermute | solution.py:57
  456.9 38.4 %collective-permute-done.21 = bf16[256,1024]{1,0:T(8,128)(2,1)S(1)} collective-permute-done((bf16[256,1024]{1,0:T(8,128)(2,1)S(1)}, bf16[256,1024]{1,0:T(8,128)(2,1)S(1)}, u32[]{:S(2)}, u32[]{:S(2)}) %collective-permute-start.21) | collective-permute-done | bytes 524320 | tf_op jit(solution)/shard_map/ppermute | solution.py:57
  496.1 11.7 %collective-permute-done.25 = bf16[4,32,896]{2,1,0:T(8,128)(2,1)S(1)} collective-permute-done((bf16[4,32,896]{2,1,0:T(8,128)(2,1)S(1)}, bf16[4,32,896]{2,1,0:T(8,128)(2,1)S(1)}, u32[]{:S(2)}, u32[]{:S(2)}) %collective-permute-start.25) | collective-permute-done | bytes 229408 | tf_op jit(solution)/shard_map/ppermute | solution.py:57
  508.0 6.9 collective-permute-start.26
  517.5 3.7 collective-permute-start.27
  521.2 2.9 collective-permute-start.28
  529.0 30.2 %reduce-scatter.6.cloned.1.call-done = bf16[32,4096]{1,0:T(8,128)(2,1)} async-done(((bf16[1024,4096]{1,0:T(8,128)(2,1)}), bf16[32,4096]{1,0:T(8,128)(2,1)}) %reduce-scatter.6.cloned.1.call-update) | async-done | bytes 262160 | tf_op jit(solution)/shard_map/reduce_scatter | solution.py:418
  561.0 146.9 %reduce-scatter.8.cloned.1.call-done = bf16[128,1024]{1,0:T(8,128)(2,1)} async-done(((bf16[4096,1024]{1,0:T(8,128)(2,1)}), bf16[128,1024]{1,0:T(8,128)(2,1)}) %reduce-scatter.8.cloned.1.call-update) | async-done | bytes 262160 | tf_op jit(solution)/shard_map/reduce_scatter | solution.py:417
  (237 shorter events, 93.6 us)
Async XLA Ops:
  7.2 21.2 %copy-start.8 = (bf16[256,1024]{1,0:T(8,128)(2,1)S(1)}, bf16[256,1024]{1,0:T(8,128)(2,1)}, u32[]{:S(2)}) copy-start(bf16[256,1024]{1,0:T(8,128)(2,1)} %param.16) | copy-start | bytes 1572868
  7.2 209.5 %all-gather.4.cloned.1.call-start = ((), (), s32[]{:S(2)}) async-start(), calls=%async_computation.7 | async-start | bytes 2162688 | tf_op jit(solution)/shard_map/all_gather | solution.py:340
  7.9 231.4 %all-gather.6.cloned.1.call-start = ((), (), s32[]{:S(2)}) async-start(), calls=%async_computation.8 | async-start | bytes 8650752 | tf_op jit(solution)/shard_map/all_gather | solution.py:338
  8.7 240.4 %all-gather.8.cloned.1.call-start = ((), (), s32[]{:S(2)}) async-start(), calls=%async_computation.9 | async-start | bytes 8650752 | tf_op jit(solution)/shard_map/all_gather | solution.py:339
  9.4 56.1 %collective-permute-start.6 = (bf16[256,1024]{1,0:T(8,128)(2,1)}, bf16[256,1024]{1,0:T(8,128)(2,1)S(1)}, u32[]{:S(2)}, u32[]{:S(2)}) collective-permute-start(bf16[256,1024]{1,0:T(8,128)(2,1)} %param.16), channel_id=1, source_target_pairs={{8,0},{16,8},{24,16},{9,1},{17,9},{25,17},{10,2},{18,10},{26,18},{... | collective-permute-start | bytes 1572872 | tf_op jit(solution)/shard_map/ppermute | solution.py:85
  10.7 56.1 %collective-permute-start.7 = (bf16[256,1024]{1,0:T(8,128)(2,1)}, bf16[256,1024]{1,0:T(8,128)(2,1)}, u32[]{:S(2)}, u32[]{:S(2)}) collective-permute-start(bf16[256,1024]{1,0:T(8,128)(2,1)} %param.16), channel_id=1, source_target_pairs={{0,8},{8,16},{16,24},{1,9},{9,17},{17,25},{2,10},{10,18},{18,26},{... | collective-permute-start | bytes 1572872 | tf_op jit(solution)/shard_map/ppermute | solution.py:84
  23.2 5.4 collective-permute-start.12
  25.8 27.1 %collective-permute-start = (bf16[32,768]{1,0:T(8,128)(2,1)}, bf16[32,768]{1,0:T(8,128)(2,1)}, u32[]{:S(2)}, u32[]{:S(2)}) collective-permute-start(bf16[32,768]{1,0:T(8,128)(2,1)} %get-tuple-element.65), channel_id=1, source_target_pairs={{0,8},{8,16},{16,24},{24,0},{1,9},{9,17},{17,25},{25,1},{2,10},{10... | collective-permute-start | bytes 147464 | tf_op jit(solution)/shard_map/ppermute | solution.py:57
  27.0 26.7 %collective-permute-start.1 = (bf16[32,768]{1,0:T(8,128)(2,1)S(1)}, bf16[32,768]{1,0:T(8,128)(2,1)}, u32[]{:S(2)}, u32[]{:S(2)}) collective-permute-start(bf16[32,768]{1,0:T(8,128)(2,1)S(1)} %get-tuple-element.64), channel_id=1, source_target_pairs={{0,16},{8,24},{16,0},{24,8},{1,17},{9,25},{17,1},{25,9},{2,18},{10... | collective-permute-start | bytes 147464 | tf_op jit(solution)/shard_map/ppermute | solution.py:57
  28.6 3.6 collective-permute-start.13
  32.3 3.6 collective-permute-start.14
  35.9 5.4 collective-permute-start.15
  41.3 4.5 collective-permute-start.16
  45.8 3.6 collective-permute-start.17
  49.5 5.1 collective-permute-start.2
  54.5 9.2 %collective-permute-start.3 = (bf16[4,32,768]{2,1,0:T(8,128)(2,1)S(1)}, bf16[4,32,768]{2,1,0:T(8,128)(2,1)S(1)}, u32[]{:S(2)}, u32[]{:S(2)}) collective-permute-start(bf16[4,32,768]{2,1,0:T(8,128)(2,1)S(1)} %bitcast_dynamic-update-slice_fusion.13), channel_id=1, source_target_pairs={{0,2},{2,0},{1,3},{3,1},{4,6},{6,4},{5,7},{7,5},{8,10},{10,8},{9,1... | collective-permute-start | bytes 589832 | tf_op jit(solution)/shard_map/ppermute | solution.py:57
  63.7 7.9 %collective-permute-start.4 = (bf16[2,4,32,768]{3,2,0,1:T(8,128)(2,1)S(1)}, bf16[2,4,32,768]{3,2,0,1:T(8,128)(2,1)}, u32[]{:S(2)}, u32[]{:S(2)}) collective-permute-start(bf16[2,4,32,768]{3,2,0,1:T(8,128)(2,1)S(1)} %bitcast_dynamic-update-slice_fusion.9), channel_id=1, source_target_pairs={{0,4},{4,0},{1,5},{5,1},{2,6},{6,2},{3,7},{7,3},{8,12},{12,8},{9,1... | collective-permute-start | bytes 1179656 | tf_op jit(solution)/shard_map/ppermute | solution.py:57
  65.5 11.1 %collective-permute-start.8 = (bf16[256,1024]{1,0:T(8,128)(2,1)S(1)}, bf16[256,1024]{1,0:T(8,128)(2,1)S(1)}, u32[]{:S(2)}, u32[]{:S(2)}) collective-permute-start(bf16[256,1024]{1,0:T(8,128)(2,1)S(1)} %collective-permute-done.6), channel_id=1, source_target_pairs={{8,0},{16,8},{24,16},{9,1},{17,9},{25,17},{10,2},{18,10},{26,18},{... | collective-permute-start | bytes 1572872 | tf_op jit(solution)/shard_map/ppermute | solution.py:85
  66.8 11.6 %collective-permute-start.9 = (bf16[256,1024]{1,0:T(8,128)(2,1)}, bf16[256,1024]{1,0:T(8,128)(2,1)S(1)}, u32[]{:S(2)}, u32[]{:S(2)}) collective-permute-start(bf16[256,1024]{1,0:T(8,128)(2,1)} %collective-permute-done.7), channel_id=1, source_target_pairs={{0,8},{8,16},{16,24},{1,9},{9,17},{17,25},{2,10},{10,18},{18,26},{... | collective-permute-start | bytes 1572872 | tf_op jit(solution)/shard_map/ppermute | solution.py:84
  72.7 10.2 %collective-permute-start.5 = (bf16[2,2,4,32,768]{4,3,1,0,2:T(8,128)(2,1)S(1)}, bf16[2,2,4,32,768]{4,3,1,0,2:T(8,128)(2,1)S(1)}, u32[]{:S(2)}, u32[]{:S(2)}) collective-permute-start(bf16[2,2,4,32,768]{4,3,1,0,2:T(8,128)(2,1)S(1)} %bitcast_dynamic-update-slice_fusion.7), channel_id=1, source_target_pairs={{0,1},{1,0},{2,3},{3,2},{4,5},{5,4},{6,7},{7,6},{8,9},{9,8},{10,11... | collective-permute-start | bytes 2359304 | tf_op jit(solution)/shard_map/ppermute | solution.py:57
  76.6 15.9 %collective-permute-start.10 = (bf16[256,1024]{1,0:T(8,128)(2,1)S(1)}, bf16[256,1024]{1,0:T(8,128)(2,1)S(1)}, u32[]{:S(2)}, u32[]{:S(2)}) collective-permute-start(bf16[256,1024]{1,0:T(8,128)(2,1)S(1)} %collective-permute-done.8), channel_id=1, source_target_pairs={{8,0},{16,8},{24,16},{9,1},{17,9},{25,17},{10,2},{18,10},{26,18},{... | collective-permute-start | bytes 1572872 | tf_op jit(solution)/shard_map/ppermute | solution.py:85
  78.4 17.9 %collective-permute-start.11 = (bf16[256,1024]{1,0:T(8,128)(2,1)S(1)}, bf16[256,1024]{1,0:T(8,128)(2,1)S(1)}, u32[]{:S(2)}, u32[]{:S(2)}) collective-permute-start(bf16[256,1024]{1,0:T(8,128)(2,1)S(1)} %collective-permute-done.9), channel_id=1, source_target_pairs={{0,8},{8,16},{16,24},{1,9},{9,17},{17,25},{2,10},{10,18},{18,26},{... | collective-permute-start | bytes 1572872 | tf_op jit(solution)/shard_map/ppermute | solution.py:84
  103.6 38.6 %all-to-all-start = ((bf16[4,192,1024]{2,1,0:T(8,128)(2,1)}), bf16[4,192,1024]{2,1,0:T(8,128)(2,1)}, u32[]{:S(2)}, u32[]{:S(2)}) async-start(bf16[4,192,1024]{2,1,0:T(8,128)(2,1)} %bitcast.266), calls=%async_computation | async-start | bytes 3145728 | tf_op jit(solution)/shard_map/all_to_all | solution.py:367
  144.7 9.3 %collective-permute-start.18 = (bf16[4,128,1024]{2,1,0:T(8,128)(2,1)}, bf16[4,128,1024]{2,1,0:T(8,128)(2,1)}, u32[]{:S(2)}, u32[]{:S(2)}) collective-permute-start(bf16[4,128,1024]{2,1,0:T(8,128)(2,1)} %get-tuple-element.56), channel_id=1, source_target_pairs={{0,1},{1,0},{2,3},{3,2},{4,5},{5,4},{6,7},{7,6},{8,9},{9,8},{10,11... | collective-permute-start | bytes 3145736 | tf_op jit(solution)/shard_map/ppermute | solution.py:57
  201.4 34.2 %all-to-all-start.1 = ((bf16[16,64,256]{2,1,0:T(8,128)(2,1)}), bf16[16,64,256]{2,1,0:T(8,128)(2,1)S(1)}, u32[]{:S(2)}, u32[]{:S(2)}) async-start(bf16[16,64,256]{2,1,0:T(8,128)(2,1)} %bitcast.269), calls=%async_computation.1 | async-start | bytes 1048576 | tf_op jit(solution)/shard_map/all_to_all | solution.py:389
  216.5 299.5 %reduce-scatter.4.cloned.1.call-start = ((), (), s32[]{:S(2)}) async-start(), calls=%async_computation.10 | async-start | bytes 2162688 | tf_op jit(solution)/shard_map/reduce_scatter | solution.py:419
  263.3 295.9 %reduce-scatter.6.cloned.1.call-start = ((), (), s32[]{:S(2)}) async-start(), calls=%async_computation.11 | async-start | bytes 8650752 | tf_op jit(solution)/shard_map/reduce_scatter | solution.py:418
  270.7 437.2 %reduce-scatter.8.cloned.1.call-start = ((), (), s32[]{:S(2)}) async-start(), calls=%async_computation.12 | async-start | bytes 8650752 | tf_op jit(solution)/shard_map/reduce_scatter | solution.py:417
  285.3 21.2 %all-to-all-start.2 = ((bf16[16,64,256]{2,1,0:T(8,128)(2,1)}), bf16[16,64,256]{2,1,0:T(8,128)(2,1)}, u32[]{:S(2)}, u32[]{:S(2)}) async-start(bf16[16,64,256]{2,1,0:T(8,128)(2,1)} %bitcast.264), calls=%async_computation.2 | async-start | bytes 1048576 | tf_op jit(solution)/shard_map/all_to_all | solution.py:410
  367.1 5.8 collective-permute-start.19
  367.7 17.7 %collective-permute-start.31 = (f32[2,2,2,1,256]{4,3,2,1,0:T(1,128)S(1)}, f32[2,2,2,1,256]{4,3,2,1,0:T(1,128)S(1)}, u32[]{:S(2)}, u32[]{:S(2)}) collective-permute-start(f32[2,2,2,1,256]{4,3,2,1,0:T(1,128)S(1)} %get-tuple-element.68), channel_id=1, source_target_pairs={{0,24},{8,0},{16,8},{24,16},{1,25},{9,1},{17,9},{25,17},{2,26},{10... | collective-permute-start | bytes 24584 | tf_op jit(solution)/shard_map/ppermute | solution.py:57
  369.8 15.7 %collective-permute-start.30 = (f32[2,2,2,1,256]{4,3,2,1,0:T(1,128)S(1)}, f32[2,2,2,1,256]{4,3,2,1,0:T(1,128)S(1)}, u32[]{:S(2)}, u32[]{:S(2)}) collective-permute-start(f32[2,2,2,1,256]{4,3,2,1,0:T(1,128)S(1)} %get-tuple-element.69), channel_id=1, source_target_pairs={{0,16},{8,24},{16,0},{24,8},{1,17},{9,25},{17,1},{25,9},{2,18},{10... | collective-permute-start | bytes 24584 | tf_op jit(solution)/shard_map/ppermute | solution.py:57
  370.5 14.9 %collective-permute-start.29 = (f32[2,2,2,1,256]{4,3,2,1,0:T(1,128)S(1)}, f32[2,2,2,1,256]{4,3,2,1,0:T(1,128)S(1)}, u32[]{:S(2)}, u32[]{:S(2)}) collective-permute-start(f32[2,2,2,1,256]{4,3,2,1,0:T(1,128)S(1)} %get-tuple-element.67), channel_id=1, source_target_pairs={{0,8},{8,16},{16,24},{24,0},{1,9},{9,17},{17,25},{25,1},{2,10},{10... | collective-permute-start | bytes 24584 | tf_op jit(solution)/shard_map/ppermute | solution.py:57
  380.9 29.0 %all-to-all-start.3 = ((bf16[4,192,1024]{2,1,0:T(8,128)(2,1)}), bf16[4,192,1024]{2,1,0:T(8,128)(2,1)}, u32[]{:S(2)}, u32[]{:S(2)}) async-start(bf16[4,192,1024]{2,1,0:T(8,128)(2,1)} %copy.143), calls=%async_computation.3 | async-start | bytes 3145728 | tf_op jit(solution)/shard_map/all_to_all | solution.py:442
  385.5 20.7 %collective-permute-start.32 = (f32[2,2,1,256]{3,2,1,0:T(1,128)S(1)}, f32[2,2,1,256]{3,2,1,0:T(1,128)S(1)}, u32[]{:S(2)}, u32[]{:S(2)}) collective-permute-start(f32[2,2,1,256]{3,2,1,0:T(1,128)S(1)} %fusion.44), channel_id=1, source_target_pairs={{0,4},{4,0},{1,5},{5,1},{2,6},{6,2},{3,7},{7,3},{8,12},{12,8},{9,1... | collective-permute-start | bytes 12296 | tf_op jit(solution)/shard_map/ppermute | solution.py:57
  406.2 3.7 collective-permute-start.33
  409.9 27.0 %collective-permute-start.34 = (f32[1,256]{1,0:T(1,128)S(1)}, f32[1,256]{1,0:T(1,128)S(1)}, u32[]{:S(2)}, u32[]{:S(2)}) collective-permute-start(f32[1,256]{1,0:T(1,128)S(1)} %fusion.51), channel_id=1, source_target_pairs={{0,1},{1,0},{2,3},{3,2},{4,5},{5,4},{6,7},{7,6},{8,9},{9,8},{10,11... | collective-permute-start | bytes 3080 | tf_op jit(solution)/shard_map/ppermute | solution.py:57
  428.0 12.9 %collective-permute-start.23 = (bf16[4,4,32,896]{3,2,0,1:T(8,128)(2,1)S(1)}, bf16[4,4,32,896]{3,2,0,1:T(8,128)(2,1)S(1)}, u32[]{:S(2)}, u32[]{:S(2)}) collective-permute-start(bf16[4,4,32,896]{3,2,0,1:T(8,128)(2,1)S(1)} %dynamic-slice_bitcast_fusion.1), channel_id=1, source_target_pairs={{0,1},{1,0},{2,3},{3,2},{4,5},{5,4},{6,7},{7,6},{8,9},{9,8},{10,11... | collective-permute-start | bytes 2752520 | tf_op jit(solution)/shard_map/ppermute | solution.py:57
  437.5 57.9 %copy-start.2 = (f32[4,256,1024]{2,1,0:T(8,128)S(1)}, f32[4,256,1024]{2,1,0:T(8,128)}, u32[]{:S(2)}) copy-start(f32[4,256,1024]{2,1,0:T(8,128)} %get-tuple-element.51) | copy-start | bytes 12582916
  437.6 19.3 %collective-permute-start.22 = (bf16[256,1024]{1,0:T(8,128)(2,1)S(1)}, bf16[256,1024]{1,0:T(8,128)(2,1)S(1)}, u32[]{:S(2)}, u32[]{:S(2)}) collective-permute-start(bf16[256,1024]{1,0:T(8,128)(2,1)S(1)} %get-tuple-element.54), channel_id=1, source_target_pairs={{0,24},{8,0},{16,8},{24,16},{1,25},{9,1},{17,9},{25,17},{2,26},{10... | collective-permute-start | bytes 1572872 | tf_op jit(solution)/shard_map/ppermute | solution.py:57
  440.2 55.2 %collective-permute-start.21 = (bf16[256,1024]{1,0:T(8,128)(2,1)S(1)}, bf16[256,1024]{1,0:T(8,128)(2,1)S(1)}, u32[]{:S(2)}, u32[]{:S(2)}) collective-permute-start(bf16[256,1024]{1,0:T(8,128)(2,1)S(1)} %get-tuple-element.55), channel_id=1, source_target_pairs={{0,16},{8,24},{16,0},{24,8},{1,17},{9,25},{17,1},{25,9},{2,18},{10... | collective-permute-start | bytes 1572872 | tf_op jit(solution)/shard_map/ppermute | solution.py:57
  440.6 54.8 %collective-permute-start.20 = (bf16[256,1024]{1,0:T(8,128)(2,1)S(1)}, bf16[256,1024]{1,0:T(8,128)(2,1)S(1)}, u32[]{:S(2)}, u32[]{:S(2)}) collective-permute-start(bf16[256,1024]{1,0:T(8,128)(2,1)S(1)} %get-tuple-element.53), channel_id=1, source_target_pairs={{0,8},{8,16},{16,24},{24,0},{1,9},{9,17},{17,25},{25,1},{2,10},{10... | collective-permute-start | bytes 1572872 | tf_op jit(solution)/shard_map/ppermute | solution.py:57
  441.3 54.5 %collective-permute-start.24 = (bf16[2,4,32,896]{3,2,1,0:T(8,128)(2,1)S(1)}, bf16[2,4,32,896]{3,2,1,0:T(8,128)(2,1)S(1)}, u32[]{:S(2)}, u32[]{:S(2)}) collective-permute-start(bf16[2,4,32,896]{3,2,1,0:T(8,128)(2,1)S(1)} %dynamic-slice_bitcast_fusion.5), channel_id=1, source_target_pairs={{0,4},{4,0},{1,5},{5,1},{2,6},{6,2},{3,7},{7,3},{8,12},{12,8},{9,1... | collective-permute-start | bytes 1376264 | tf_op jit(solution)/shard_map/ppermute | solution.py:57
  495.4 19.5 %copy-start.1 = (f32[256,1024]{1,0:T(8,128)S(1)}, f32[256,1024]{1,0:T(8,128)}, u32[]{:S(2)}) copy-start(f32[256,1024]{1,0:T(8,128)} %copy-done) | copy-start | bytes 3145732
  496.0 11.8 %collective-permute-start.25 = (bf16[4,32,896]{2,1,0:T(8,128)(2,1)S(1)}, bf16[4,32,896]{2,1,0:T(8,128)(2,1)S(1)}, u32[]{:S(2)}, u32[]{:S(2)}) collective-permute-start(bf16[4,32,896]{2,1,0:T(8,128)(2,1)S(1)} %dynamic-slice_bitcast_fusion.6), channel_id=1, source_target_pairs={{0,2},{2,0},{1,3},{3,1},{4,6},{6,4},{5,7},{7,5},{8,10},{10,8},{9,1... | collective-permute-start | bytes 688136 | tf_op jit(solution)/shard_map/ppermute | solution.py:57
  508.0 16.1 %collective-permute-start.26 = (bf16[32,896]{1,0:T(8,128)(2,1)S(1)}, bf16[32,896]{1,0:T(8,128)(2,1)S(1)}, u32[]{:S(2)}, u32[]{:S(2)}) collective-permute-start(bf16[32,896]{1,0:T(8,128)(2,1)S(1)} %get-tuple-element.61), channel_id=1, source_target_pairs={{0,8},{8,16},{16,24},{24,0},{1,9},{9,17},{17,25},{25,1},{2,10},{10... | collective-permute-start | bytes 172040 | tf_op jit(solution)/shard_map/ppermute | solution.py:57
  517.5 7.0 collective-permute-start.27
  521.2 4.8 collective-permute-start.28
  (11 other events, 65.9 us)
Sparse Core Ops, SparseCore 0:
  10.9 61.8 all-gather.3
  75.6 85.9 all-gather.5
  164.5 84.5 all-gather.7
  263.5 139.6 reduce-scatter.3
  405.4 153.7 reduce-scatter.5
  561.5 146.3 reduce-scatter.7

commit v2 on v1

--- a/solution.py
+++ b/solution.py
@@ -72,17 +72,23 @@
     return out
 
 
-def gather_line(x, axis):
+def gather_line(x, axis, beside):
     n = lax.axis_size(axis)
     if n != 4:
+        for make in beside:
+            if make is not None:
+                make()
         return gather_axis(x, axis)
     me = lax.axis_index(axis)
     up = [(i, i + 1) for i in range(n - 1)]
     down = [(i + 1, i) for i in range(n - 1)]
     left, right = [x], [x]
-    for _ in range(n - 1):
+    for i in range(n - 1):
         left.append(lax.ppermute(left[-1], axis, up))
         right.append(lax.ppermute(right[-1], axis, down))
+        if beside[i] is not None:
+            made = beside[i]()
+            left[-1], right[-1], _ = lax.optimization_barrier((left[-1], right[-1], made))
     low = me < 2
     first = jnp.where(low, right[1], left[1])
     second = jnp.where(low, right[2], left[2])
@@ -335,29 +341,56 @@
     w_rows = in_weight.shape[0]
     group = 3 * hb * HEAD_DIM
 
-    w_up = lax.all_gather(up_weight, ALL, axis=0, tiled=True)
-    w_down = lax.all_gather(down_weight, ALL, axis=0, tiled=True)
-    w_out = lax.all_gather(out_weight, ALL, axis=0, tiled=True)
+    chips = n_head * hb
+    f_rows = down_weight.shape[0] // 2
+
+    up_cols = up_weight.reshape(w_rows, chips, n_rest, 2, f_rows).transpose(2, 0, 3, 1, 4)
+    up_cols = exchange_axis(up_cols.reshape(n_rest, w_rows, 2 * chips * f_rows), "rest").reshape(n_rest * w_rows, -1)
+    out_rows = gather_axis(out_weight, "rest").reshape(n_rest * w_rows, width)
+    down_rows = down_weight.reshape(2, f_rows, width)
+    f_half = chips * f_rows
+    if f_rows == n_rest * w_rows:
+        joint = jnp.concatenate([up_cols, down_rows[0], down_rows[1], out_rows], axis=1)
+        joint = lax.all_gather(joint, ("head", "u", "v"), axis=0, tiled=True)
+        w_up = joint[:, : 2 * f_half]
+        w_down = joint[:, 2 * f_half : 2 * f_half + width], joint[:, 2 * f_half + width : 2 * f_half + 2 * width]
+        w_out = joint[:, 2 * f_half + 2 * width :]
+    else:
+        w_up, w_down_a, w_down_b, w_out = (
+            lax.all_gather(w, ("head", "u", "v"), axis=0, tiled=True)
+            for w in (up_cols, down_rows[0], down_rows[1], out_rows)
+        )
+        w_down = w_down_a, w_down_b
 
     parts = [norm_gain, norm_shift, query_bias, value_bias, out_bias, post_gain, post_shift, down_bias, up_bias]
-    packed = jnp.concatenate(parts).reshape(1, -1)
-    for axis in ("rest", "v", "u", "head"):
-        packed = gather_axis(packed, axis)
-    packed = packed.reshape(n_all, -1)
+    packed = [jnp.concatenate(parts).reshape(1, -1)]
+
+    cols = in_weight.reshape(w_rows, 3, n_head, hb, HEAD_DIM).transpose(2, 0, 3, 1, 4).reshape(n_head, w_rows, group)
+    w_in = [cols]
+
+    def chain_one():
+        for axis in ("rest", "v"):
+            packed[0] = gather_axis(packed[0], axis)
+        w_in[0] = exchange_axis(w_in[0], "head")
+        return (packed[0], w_in[0])
+
+    def chain_two():
+        for axis in ("u", "head"):
+            packed[0] = gather_axis(packed[0], axis)
+        w_in[0] = gather_axis(w_in[0], "v")
+        return (packed[0], w_in[0])
+
+    rows_all = gather_line(tokens, "head", [chain_one, chain_two, None]).reshape(block_rows, width).astype(f32)
+    packed = packed[0].reshape(n_all, -1)
     vectors, at = [], 0
     for part in parts:
         size = part.shape[0]
         vectors.append(packed[:, at : at + size].reshape(-1).astype(f32))
         at += size
     gain_a, shift_a, bias_q, bias_v, bias_out, gain_b, shift_b, bias_down, bias_up = vectors
-
-    cols = in_weight.reshape(w_rows, 3, n_head, hb, HEAD_DIM).transpose(2, 0, 3, 1, 4).reshape(n_head, w_rows, group)
-    w_in = exchange_axis(cols, "head")
-    for axis in ("v", "u", "rest"):
-        w_in = gather_axis(w_in, axis)
+    w_in = gather_axis(gather_axis(w_in[0], "u"), "rest")
     w_in = w_in.transpose(3, 1, 2, 0, 4, 5).reshape(width, group)
 
-    rows_all = gather_line(tokens, "head").reshape(block_rows, width).astype(f32)
     normed, unit_all, inverse_all = norm_forward(rows_all, gain_a, shift_a)
     normed_low = normed.astype(bf16)
     group_bias = jnp.stack([bias_q, jnp.zeros_like(bias_q), bias_v]).reshape(3, n_head, hb, HEAD_DIM)
@@ -395,15 +428,25 @@
     middle = rows + branch
     hidden_in, unit_mid, inverse_mid = norm_forward(middle, gain_b, shift_b)
     hidden_low = hidden_in.astype(bf16)
-    pre = jnp.dot(hidden_low, w_up, preferred_element_type=f32) + bias_up
+    hidden_all = gather_axis(hidden_low, "rest").reshape(n_rest * tok_rows, width)
+    cot_all = gather_axis(cotangent, "rest").reshape(n_rest * tok_rows, width)
+    bias_units = lax.dynamic_index_in_dim(bias_up.reshape(chips, n_rest, 2, f_rows), me_rest, 1, keepdims=False)
+    bias_units = bias_units.transpose(1, 0, 2).reshape(-1)
+    pre = jnp.dot(hidden_all, w_up, preferred_element_type=f32) + bias_units
     act, slope = gelu_parts(pre)
     act_low = act.astype(bf16)
-    result = middle + jnp.dot(act_low, w_down, preferred_element_type=f32) + bias_down
-    output = result.astype(bf16)
+    acts = act_low[:, :f_half], act_low[:, f_half:]
+    down = jnp.dot(acts[0], w_down[0], preferred_element_type=f32)
+    down = down + jnp.dot(acts[1], w_down[1], preferred_element_type=f32)
+    down = reduce_axis(down.reshape(n_rest, tok_rows, width), "rest")
+    output = (middle + down + bias_down).astype(bf16)
     grad_out = cotangent.astype(f32)
-    grad_act = jnp.einsum("td,fd->tf", cotangent, w_down, preferred_element_type=f32)
+    grad_act = jnp.concatenate(
+        [jnp.einsum("td,fd->tf", cot_all, w, preferred_element_type=f32) for w in w_down], axis=1
+    )
     grad_pre = (grad_act * slope).astype(bf16)
     grad_hidden = jnp.einsum("tf,df->td", grad_pre, w_up, preferred_element_type=f32)
+    grad_hidden = reduce_axis(grad_hidden.reshape(n_rest, tok_rows, width), "rest")
     grad_middle = grad_out + norm_inner(grad_hidden, unit_mid, inverse_mid, gain_b)
     grad_branch = grad_middle.astype(bf16)
     grad_back = lax.dot_general(w_out, grad_branch, (((1,), (1,)), ((), ())), preferred_element_type=f32).astype(bf16)
@@ -411,30 +454,28 @@
         grad_back.reshape(HEADS, HEAD_DIM, tok_rows), ("head", "u", "v"), split_axis=0, concat_axis=0, tiled=True
     ).reshape(n_head, hb, HEAD_DIM, tok_rows)
 
-    down_grad = jnp.einsum("tf,td->fd", act_low, cotangent, preferred_element_type=f32).astype(bf16)
-    up_grad = jnp.einsum("td,tf->df", hidden_low, grad_pre, preferred_element_type=f32).astype(bf16)
+    down_grads = [jnp.einsum("tf,td->fd", a, cot_all, preferred_element_type=f32).astype(bf16) for a in acts]
+    up_grad = jnp.einsum("td,tf->df", hidden_all, grad_pre, preferred_element_type=f32).astype(bf16)
     out_grad = jnp.einsum("dt,te->de", back, grad_branch, preferred_element_type=f32).astype(bf16)
-    down_weight_grad = lax.psum_scatter(down_grad, ALL, scatter_dimension=0, tiled=True).astype(f32)
-    up_weight_grad = lax.psum_scatter(up_grad, ALL, scatter_dimension=0, tiled=True).astype(f32)
-    out_weight_grad = lax.psum_scatter(out_grad, ALL, scatter_dimension=0, tiled=True).astype(f32)
+    out_grad = out_grad.reshape(chips, n_rest, w_rows, width).transpose(1, 0, 2, 3)
+    out_grad = reduce_axis(out_grad, "rest").astype(bf16)
+    plane = lambda x: x.reshape(n_head, n_u, n_v, -1, x.shape[-1])
+    by_u = [plane(up_grad).transpose(1, 2, 0, 3, 4)]
+    by_v = [plane(x).transpose(2, 1, 0, 3, 4) for x in (*down_grads, out_grad)]
     sums = [
         jnp.sum(grad_branch.astype(f32), axis=0),
         jnp.sum(grad_hidden * unit_mid, axis=0),
         jnp.sum(grad_hidden, axis=0),
         jnp.sum(grad_out, axis=0),
-        jnp.sum(grad_pre.astype(f32), axis=0),
     ]
-    small = jnp.concatenate([s.reshape(n_all, -1) for s in sums], axis=1)
-    small = small.reshape(n_head, n_u, n_v, n_rest, 1, -1)
-    small = reduce_axis(small, "head")
-    for axis in ("u", "v", "rest"):
-        small = reduce_axis(small, axis)
-    small = small.reshape(-1)
-    size = width // n_all
-    out_bias_grad, post_gain_grad, post_shift_grad, down_bias_grad = (
-        small[i * size : (i + 1) * size] for i in range(4)
-    )
-    up_bias_grad = small[4 * size :]
+    small = jnp.stack([s.reshape(chips, n_rest, -1) for s in sums], axis=2).reshape(chips, n_rest, -1)
+    small = reduce_axis(small.transpose(1, 0, 2), "rest")
+    unit_sum = jnp.sum(grad_pre.astype(f32), axis=0).reshape(2, chips, f_rows).transpose(1, 0, 2).reshape(chips, -1)
+    small = jnp.concatenate([small, unit_sum], axis=1).reshape(n_head, n_u, n_v, -1)
+
+    grad_heads, by_u, by_v, small = lax.optimization_barrier((grad_heads, by_u, by_v, small))
+    by_u = [reduce_axis(x, "u").astype(bf16) for x in by_u]
+    by_v = [reduce_axis(x, "v").astype(bf16) for x in by_v]
 
     dq, dkv = attention_backward(bounds, qkv, kv, starts, grad_heads, wide, lse)
     dkv = dkv.reshape(hb, n_rest, subs_k, 2 * HEAD_DIM, BLOCK_K).transpose(1, 0, 3, 2, 4)
@@ -443,8 +484,26 @@
         jnp.concatenate([dq, dkv], axis=1), ("u", "v"), split_axis=0, concat_axis=0, tiled=True
     ).reshape(group, block_rows)
 
+    grad_proj, by_u, by_v, small = lax.optimization_barrier((grad_proj, by_u, by_v, small))
+    by_u = [reduce_axis(x, "v").astype(bf16) for x in by_u]
+    by_v = [reduce_axis(x, "u").astype(bf16) for x in by_v]
+    small = reduce_axis(reduce_axis(small, "head"), "u")
+    small = reduce_axis(small, "v")
+
     grad_normed = lax.dot_general(grad_proj, w_in, (((0,), (1,)), ((), ())), preferred_element_type=f32)
     grad_tokens = reduce_axis(grad_normed.astype(bf16).reshape(n_head, tok_rows, width), "head")
+    grad_tokens, by_u, by_v = lax.optimization_barrier((grad_tokens, by_u, by_v))
+    up_weight_grad = reduce_axis(by_u[0], "head").astype(bf16).reshape(n_rest, w_rows, -1)
+    up_weight_grad = exchange_axis(up_weight_grad, "rest").astype(f32)
+    up_weight_grad = up_weight_grad.reshape(n_rest, w_rows, 2, chips, f_rows).transpose(1, 3, 0, 2, 4)
+    up_weight_grad = up_weight_grad.reshape(w_rows, -1)
+    down_a, down_b, out_weight_grad = (reduce_axis(x, "head") for x in by_v)
+    down_weight_grad = jnp.concatenate([down_a, down_b], axis=0)
+    size = width // n_all
+    out_bias_grad, post_gain_grad, post_shift_grad, down_bias_grad = (
+        small[i * size : (i + 1) * size] for i in range(4)
+    )
+    up_bias_grad = small[4 * size :]
     unit_in = lax.dynamic_index_in_dim(unit_all.reshape(n_head, tok_rows, width), me_head, 0, keepdims=False)
     inverse_in = lax.dynamic_index_in_dim(inverse_all.reshape(n_head, tok_rows, 1), me_head, 0, keepdims=False)
     tokens_grad = (grad_middle + norm_inner(grad_tokens, unit_in, inverse_in, gain_a)).astype(bf16)

time: 723 us -> 606 us (0.84)
  waiting for transfers between devices: 364 us -> 219 us
  other arithmetic: 23.6 us -> 44.2 us
  local copies, waits for them, and re-layouts: 56.6 us -> 77 us
  matrix products: 62.4 us -> 46.3 us
  Pallas kernels: 94.6 us -> 85.1 us
  starting transfers between devices: 101 us -> 109 us
    reduce_scatter x3 -> x0, waiting for transfers between devices: 177 us -> none  [the longest x1 147 us: on_device(): lax.psum_scatter(down_grad, ALL, scatter_dimension=0, tiled=True)]
    ppermute x29 -> x57, starting transfers between devices: 39 us -> 71.2 us  [shifted(): return lax.ppermute(x, axis, [(i, (i + k) % n) for i in range(n)])]
    ppermute x29 -> x57, waiting for transfers between devices: 110 us -> 141 us  [shifted(): return lax.ppermute(x, axis, [(i, (i + k) % n) for i in range(n)])]
    ppermute x3, waiting for transfers between devices: 12.8 us -> 33 us  [gather_line(): right.append(lax.ppermute(right[-1], axis, down))]
    squeeze x9 -> x23, local copies, waits for them, and re-layouts: 2.66 us -> 16.2 us  [reduce_axis(): piece = lax.dynamic_index_in_dim(x, (me + k) % n, 0, keepdims=False)]
    dot_general x5 -> x8, matrix products: 38.5 us -> 26 us  [the longest x2 6.86 us: on_device(): jnp.einsum('tf,td->fd', a, cot_all, preferred_element_type=f32).astype(bf16)]
    convert_element_type x3 -> x10, other arithmetic: 5.07 us -> 16.7 us  [the longest x3 7.97 us: on_device(): by_v = [reduce_axis(x, 'v').astype(bf16) for x in by_v]]
    all_to_all x1, waiting for transfers between devices: 18.8 us -> 8.4 us  [on_device(): lax.all_to_all(attended.reshape(HEADS, HEAD_DIM, tok_rows), ('head', 'u',...]
  transfers between devices with their start and end apart: 45 -> 68, of which waited for: 24 -> 28; matrix products, arithmetic and copies ran while one was open for 17% -> 22% of each run, Pallas kernels for 13% -> 6%
where the time goes in v2:
time: 606 us; the launch traced here: 597 us
  waiting for transfers between devices  219 us (36%)
  starting transfers between devices  109 us (18%)
  Pallas kernels  85.1 us (14%)
  local copies, waits for them, and re-layouts  77 us (13%)
  matrix products  46.3 us (8%)
  other arithmetic  44.2 us (7%)
  between operations  16 us (3%)
    ppermute x57, waiting for transfers between devices, shifted(): return lax.ppermute(x, axis, [(i, (i + k) % n) for i in range(n)])  141 us
    ppermute x57, starting transfers between devices, shifted(): return lax.ppermute(x, axis, [(i, (i + k) % n) for i in range(n)])  71.2 us
    pallas_call x1, Pallas kernels, attention_backward(): pl.pallas_call(functools.partial(backward_kernel, n_steps), grid_spec=plt...  48.6 us
    pallas_call x1, Pallas kernels, attention_forward(): pl.pallas_call(forward_kernel, grid_spec=pltpu.PrefetchScalarGridSpec(num...  36.5 us
    ppermute x3, waiting for transfers between devices, gather_line(): right.append(lax.ppermute(right[-1], axis, down))  33 us
    squeeze x23, local copies, waits for them, and re-layouts, reduce_axis(): piece = lax.dynamic_index_in_dim(x, (me + k) % n, 0, keepdims=False)  16.2 us
    ppermute x3, waiting for transfers between devices, gather_line(): left.append(lax.ppermute(left[-1], axis, up))  14.4 us
    all_to_all x1, waiting for transfers between devices, on_device(): lax.all_to_all(projected.reshape(hb, 3 * HEAD_DIM, block_rows), ('u', 'v'...  12.5 us
  transfers between devices with their start and end apart: 68, of which 28 were waited for; matrix products, arithmetic and copies ran while one was open for 22% of the time, Pallas kernels for 6%

profile of v2, /device:TPU:0, one launch (start us, length us, event | category | flops | bytes accessed | tf_op | source)
XLA Modules:
  0.0 597.0 jit_solution(7848303810723934211)
XLA Ops:
  12.4 4.7 collective-permute-start.6
  20.9 2.6 collective-permute-start
  23.5 3.3 collective-permute-start.1
  35.2 11.1 %collective-permute-done.13 = bf16[2,2,2,1,384]{4,2,1,3,0:T(2,128)(2,1)S(1)} collective-permute-done((bf16[2,2,2,1,384]{4,2,1,3,0:T(2,128)(2,1)S(1)}, bf16[2,2,2,1,384]{4,2,1,3,0:T(2,128)(2,1)S(1)}, u32[]{:S(2)}, u32[]{:S(2)}) %collective-permute-start.13) | collective-permute-done | bytes 6176 | tf_op jit(solution)/shard_map/ppermute | solution.py:57
  46.2 2.7 collective-permute-start.14
  51.5 3.6 collective-permute-done.15
  63.9 7.7 %collective-permute-done.3 = bf16[4,32,768]{2,1,0:T(8,128)(2,1)S(1)} collective-permute-done((bf16[4,32,768]{2,1,0:T(8,128)(2,1)}, bf16[4,32,768]{2,1,0:T(8,128)(2,1)S(1)}, u32[]{:S(2)}, u32[]{:S(2)}) %collective-permute-start.3) | collective-permute-done | bytes 196640 | tf_op jit(solution)/shard_map/ppermute | solution.py:57
  74.7 2.9 collective-permute-start.10
  82.1 14.4 %collective-permute-done.10 = bf16[256,1024]{1,0:T(8,128)(2,1)S(1)} collective-permute-done((bf16[256,1024]{1,0:T(8,128)(2,1)S(1)}, bf16[256,1024]{1,0:T(8,128)(2,1)S(1)}, u32[]{:S(2)}, u32[]{:S(2)}) %collective-permute-start.10) | collective-permute-done | bytes 524320 | tf_op jit(solution)/shard_map/ppermute | solution.py:87
  96.5 6.5 %collective-permute-done.11 = bf16[256,1024]{1,0:T(8,128)(2,1)S(1)} collective-permute-done((bf16[256,1024]{1,0:T(8,128)(2,1)}, bf16[256,1024]{1,0:T(8,128)(2,1)S(1)}, u32[]{:S(2)}, u32[]{:S(2)}) %collective-permute-start.11) | collective-permute-done | bytes 524320 | tf_op jit(solution)/shard_map/ppermute | solution.py:88
  104.3 4.6 collective-permute-start.17
  109.2 26.5 %collective-permute-done.16 = bf16[256,1024]{1,0:T(8,128)(2,1)S(1)} collective-permute-done((bf16[256,1024]{1,0:T(8,128)(2,1)S(1)}, bf16[256,1024]{1,0:T(8,128)(2,1)S(1)}, u32[]{:S(2)}, u32[]{:S(2)}) %collective-permute-start.16) | collective-permute-done | bytes 524320 | tf_op jit(solution)/shard_map/ppermute | solution.py:88
  138.2 2.9 subtract_multiply_fusion
  141.1 3.0 add_convert_fusion.2
  144.2 4.7 all-to-all-start
  149.6 12.5 %all-to-all-done.q_ref = bf16[4,192,1024]{2,1,0:T(8,128)(2,1)} async-done(((bf16[4,192,1024]{2,1,0:T(8,128)(2,1)}), bf16[4,192,1024]{2,1,0:T(8,128)(2,1)}, u32[]{:S(2)}, u32[]{:S(2)}) %all-to-all-start) | async-done | bytes 1572896 | tf_op jit(solution)/shard_map/all_to_all | solution.py:400
  175.3 4.1 copy.185
  179.4 36.5 %attention_forward.1 = (bf16[4,4,64,256]{3,2,1,0:T(8,128)(2,1)}, f32[4,64,1024]{2,1,0:T(8,128)}, f32[4,1,1024]{2,1,0:T(1,128)}) custom-call(s32[8]{0:T(128)} %get-tuple-element.160.lo_ref, s32[8]{0:T(128)} %get-tuple-element.159.mid_ref, s32[8]{0:T(128)} %add.618.q0_ref, bf16[4,192,1024]{2,1,0:T(8,128)(2,1)} %all-to-all-done.q_ref, ...), custom_call_target="tpu_custom_call" | custom-call | tf_op jit(solution)/shard_map/attention_forward/pallas_call | solution.py:267
  215.9 7.2 %all-to-all-start.1 = ((bf16[16,64,256]{2,1,0:T(8,128)(2,1)}), bf16[16,64,256]{2,1,0:T(8,128)(2,1)S(1)}, u32[]{:S(2)}, u32[]{:S(2)}) async-start(bf16[16,64,256]{2,1,0:T(8,128)(2,1)} %bitcast.413), calls=%async_computation.1 | async-start | bytes 1048576 | tf_op jit(solution)/shard_map/all_to_all | solution.py:422
  230.3 8.4 %all-to-all-done.1 = bf16[16,64,256]{2,1,0:T(8,128)(2,1)S(1)} async-done(((bf16[16,64,256]{2,1,0:T(8,128)(2,1)}), bf16[16,64,256]{2,1,0:T(8,128)(2,1)S(1)}, u32[]{:S(2)}, u32[]{:S(2)}) %all-to-all-start.1) | async-done | bytes 524320 | tf_op jit(solution)/shard_map/all_to_all | solution.py:422
  242.1 3.3 fusion.20
  249.3 6.4 %convert_reduce_fusion = (f32[2048]{0:T(1024)S(1)}, bf16[512,2048]{1,0:T(8,128)(2,1)S(1)}, bf16[512,2048]{1,0:T(8,128)(2,1)S(1)}) fusion(f32[2048]{0:T(1024)S(1)} %add.662, f32[512,1024]{1,0:T(8,128)S(1)} %fusion.20, f32[512,1024]{1,0:T(8,128)S(1)} %fusion.24, bf16[512,1024]{1,0:T(8,128)(2,1)S(1)} %bitcast.410, bf16[1024,5120]{1,0:T(8,128)(2,1)S(1)} %copy-done.28), kind=kOutput, calls=%fused_computation.17 | convolution fusion | flops 2173696000 | bytes 13647872 | tf_op jit(solution)/shard_map/dot_general | solution.py:435
  261.4 4.4 convolution_convert_fusion
  265.8 3.9 convolution_convert_fusion.3
  275.8 5.5 all-to-all-start.2
  282.0 2.9 convolution_convert_fusion.2
  288.3 3.0 fusion.19
  291.3 5.5 all-to-all-done.2
  296.8 48.6 %attention_backward.1 = (bf16[4,64,1024]{2,1,0:T(8,128)(2,1)}, bf16[16,128,512]{2,1,0:T(8,128)(2,1)}) custom-call(s32[8]{0:T(128)} %get-tuple-element.160.lo_ref, s32[8]{0:T(128)} %get-tuple-element.159.mid_ref, s32[8]{0:T(128)} %add.618.q0_ref, bf16[4,192,1024]{2,1,0:T(8,128)(2,1)} %all-to-all-done.q_ref, bf16[16,128,512]{2,1,0:T(8,128)(2,1)} %bitcast.370, ...), custom_call_target="tpu_custom_call" | custom-call | tf_op jit(solution)/shard_map/attention_backward/pallas_call | solution.py:293
  345.4 4.2 copy.193
  351.9 3.1 dynamic-slice_bitcast_fusion
  370.0 3.9 copy.195
  373.9 4.6 all-to-all-start.3
  378.5 40.4 %collective-permute-done.31 = bf16[2,4,32,1024]{3,2,0,1:T(8,128)(2,1)} collective-permute-done((bf16[2,4,32,1024]{3,2,0,1:T(8,128)(2,1)}, bf16[2,4,32,1024]{3,2,0,1:T(8,128)(2,1)}, u32[]{:S(2)}, u32[]{:S(2)}) %collective-permute-start.31) | collective-permute-done | bytes 524320 | tf_op jit(solution)/shard_map/ppermute | solution.py:57
  421.1 3.1 fusion.17
  426.8 3.7 fusion.9
  430.6 4.3 all-to-all-done.3
  436.5 6.1 %multiply_reduce_fusion = (bf16[1024]{0:T(1024)(128)(2,1)S(1)}, bf16[1024]{0:T(1024)(128)(2,1)S(1)}, bf16[1024,1024]{1,0:T(8,128)(2,1)S(1)}, bf16[1024,1024]{1,0:T(8,128)(2,1)}) fusion(bf16[4,256,1024]{2,1,0:T(8,128)(2,1)S(1)} %bitcast_dynamic-update-slice_fusion.6, f32[1024]{0:T(1024)S(1)} %bitcast.421, f32[1024]{0:T(1024)S(1)} %bitcast.422, ...), kind=kOutput, calls=%fused_computation.15 | convolution fusion | flops 1621096448 | bytes 9457664 | tf_op jit(solution)/shard_map/dot_general | solution.py:493
  452.0 3.9 copy.196
  456.0 3.9 convolution_convert_fusion.4
  469.7 11.6 %collective-permute-done.51 = f32[2,256]{1,0:T(2,128)S(1)} collective-permute-done((f32[2,256]{1,0:T(2,128)S(1)}, f32[2,256]{1,0:T(2,128)S(1)}, u32[]{:S(2)}, u32[]{:S(2)}) %collective-permute-start.51) | collective-permute-done | bytes 2080 | tf_op jit(solution)/shard_map/ppermute | solution.py:57
  492.7 25.3 %collective-permute-done.33 = bf16[256,1024]{1,0:T(8,128)(2,1)S(1)} collective-permute-done((bf16[256,1024]{1,0:T(8,128)(2,1)S(1)}, bf16[256,1024]{1,0:T(8,128)(2,1)S(1)}, u32[]{:S(2)}, u32[]{:S(2)}) %collective-permute-start.33) | collective-permute-done | bytes 524320 | tf_op jit(solution)/shard_map/ppermute | solution.py:57
  531.5 9.0 %collective-permute-start.60 = (bf16[64,1024]{1,0:T(8,128)(2,1)S(1)}, bf16[64,1024]{1,0:T(8,128)(2,1)S(1)}, u32[]{:S(2)}, u32[]{:S(2)}) collective-permute-start(bf16[64,1024]{1,0:T(8,128)(2,1)S(1)} %get-tuple-element.112), channel_id=1, source_target_pairs={{0,8},{8,16},{16,24},{24,0},{1,9},{9,17},{17,25},{25,1},{2,10},{10... | collective-permute-start | bytes 393224 | tf_op jit(solution)/shard_map/ppermute | solution.py:57
  542.6 5.6 collective-permute-done.61
  548.1 4.8 collective-permute-start.57
  555.1 9.7 %collective-permute-done.58 = bf16[64,1024]{1,0:T(8,128)(2,1)S(1)} collective-permute-done((bf16[64,1024]{1,0:T(8,128)(2,1)S(1)}, bf16[64,1024]{1,0:T(8,128)(2,1)S(1)}, u32[]{:S(2)}, u32[]{:S(2)}) %collective-permute-start.58) | collective-permute-done | bytes 131104 | tf_op jit(solution)/shard_map/ppermute | solution.py:57
  567.3 8.6 %collective-permute-done.54 = bf16[64,2048]{1,0:T(8,128)(2,1)S(1)} collective-permute-done((bf16[64,2048]{1,0:T(8,128)(2,1)S(1)}, bf16[64,2048]{1,0:T(8,128)(2,1)S(1)}, u32[]{:S(2)}, u32[]{:S(2)}) %collective-permute-start.54) | collective-permute-done | bytes 262176 | tf_op jit(solution)/shard_map/ppermute | solution.py:57
  583.4 3.3 collective-permute-done.43
  (415 shorter events, 168.4 us)
Async XLA Ops:
  7.2 231.6 %all-gather.2.cloned.1.call-start = ((), (), s32[]{:S(2)}) async-start(), calls=%async_computation.4 | async-start | bytes 11141120 | tf_op jit(solution)/shard_map/all_gather | solution.py:354
  12.4 62.3 %collective-permute-start.6 = (bf16[256,1024]{1,0:T(8,128)(2,1)S(1)}, bf16[256,1024]{1,0:T(8,128)(2,1)S(1)}, u32[]{:S(2)}, u32[]{:S(2)}) collective-permute-start(bf16[256,1024]{1,0:T(8,128)(2,1)S(1)} %copy-done.15), channel_id=1, source_target_pairs={{0,8},{8,16},{16,24},{1,9},{9,17},{17,25},{2,10},{10,18},{18,26},{... | collective-permute-start | bytes 1572872 | tf_op jit(solution)/shard_map/ppermute | solution.py:87
  17.0 57.7 %collective-permute-start.7 = (bf16[256,1024]{1,0:T(8,128)(2,1)S(1)}, bf16[256,1024]{1,0:T(8,128)(2,1)}, u32[]{:S(2)}, u32[]{:S(2)}) collective-permute-start(bf16[256,1024]{1,0:T(8,128)(2,1)S(1)} %copy-done.15), channel_id=1, source_target_pairs={{8,0},{16,8},{24,16},{9,1},{17,9},{25,17},{10,2},{18,10},{26,18},{... | collective-permute-start | bytes 1572872 | tf_op jit(solution)/shard_map/ppermute | solution.py:88
  18.5 9.3 %collective-permute-start.8 = (bf16[1,384]{1,0:T(2,128)(2,1)S(1)}, bf16[1,384]{1,0:T(2,128)(2,1)S(1)}, u32[]{:S(2)}, u32[]{:S(2)}) collective-permute-start(bf16[1,384]{1,0:T(2,128)(2,1)S(1)} %reshape.463), channel_id=1, source_target_pairs={{0,1},{1,0},{2,3},{3,2},{4,5},{5,4},{6,7},{7,6},{8,9},{9,8},{10,11... | collective-permute-start | bytes 2312 | tf_op jit(solution)/shard_map/ppermute | solution.py:57
  20.9 37.7 %collective-permute-start = (bf16[32,768]{1,0:T(8,128)(2,1)S(1)}, bf16[32,768]{1,0:T(8,128)(2,1)S(1)}, u32[]{:S(2)}, u32[]{:S(2)}) collective-permute-start(bf16[32,768]{1,0:T(8,128)(2,1)S(1)} %get-tuple-element.131), channel_id=1, source_target_pairs={{0,8},{8,16},{16,24},{24,0},{1,9},{9,17},{17,25},{25,1},{2,10},{10... | collective-permute-start | bytes 147464 | tf_op jit(solution)/shard_map/ppermute | solution.py:57
  23.5 35.6 %collective-permute-start.1 = (bf16[32,768]{1,0:T(8,128)(2,1)S(1)}, bf16[32,768]{1,0:T(8,128)(2,1)S(1)}, u32[]{:S(2)}, u32[]{:S(2)}) collective-permute-start(bf16[32,768]{1,0:T(8,128)(2,1)S(1)} %get-tuple-element.130), channel_id=1, source_target_pairs={{0,16},{8,24},{16,0},{24,8},{1,17},{9,25},{17,1},{25,9},{2,18},{10... | collective-permute-start | bytes 147464 | tf_op jit(solution)/shard_map/ppermute | solution.py:57
  35.1 11.1 %collective-permute-start.13 = (bf16[2,2,2,1,384]{4,2,1,3,0:T(2,128)(2,1)S(1)}, bf16[2,2,2,1,384]{4,2,1,3,0:T(2,128)(2,1)S(1)}, u32[]{:S(2)}, u32[]{:S(2)}) collective-permute-start(bf16[2,2,2,1,384]{4,2,1,3,0:T(2,128)(2,1)S(1)} %constant_dynamic-update-slice_fusion.6), channel_id=1, source_target_pairs={{0,8},{8,16},{16,24},{24,0},{1,9},{9,17},{17,25},{25,1},{2,10},{10... | collective-permute-start | bytes 18440 | tf_op jit(solution)/shard_map/ppermute | solution.py:57
  61.3 10.2 %collective-permute-start.3 = (bf16[4,32,768]{2,1,0:T(8,128)(2,1)}, bf16[4,32,768]{2,1,0:T(8,128)(2,1)S(1)}, u32[]{:S(2)}, u32[]{:S(2)}) collective-permute-start(bf16[4,32,768]{2,1,0:T(8,128)(2,1)} %bitcast_dynamic-update-slice_fusion.21), channel_id=1, source_target_pairs={{0,2},{2,0},{1,3},{3,1},{4,6},{6,4},{5,7},{7,5},{8,10},{10,8},{9,1... | collective-permute-start | bytes 589832 | tf_op jit(solution)/shard_map/ppermute | solution.py:57
  71.5 7.9 %collective-permute-start.4 = (bf16[2,4,32,768]{3,2,0,1:T(8,128)(2,1)S(1)}, bf16[2,4,32,768]{3,2,0,1:T(8,128)(2,1)}, u32[]{:S(2)}, u32[]{:S(2)}) collective-permute-start(bf16[2,4,32,768]{3,2,0,1:T(8,128)(2,1)S(1)} %bitcast_dynamic-update-slice_fusion.13), channel_id=1, source_target_pairs={{0,4},{4,0},{1,5},{5,1},{2,6},{6,2},{3,7},{7,3},{8,12},{12,8},{9,1... | collective-permute-start | bytes 1179656 | tf_op jit(solution)/shard_map/ppermute | solution.py:57
  74.7 21.8 %collective-permute-start.10 = (bf16[256,1024]{1,0:T(8,128)(2,1)S(1)}, bf16[256,1024]{1,0:T(8,128)(2,1)S(1)}, u32[]{:S(2)}, u32[]{:S(2)}) collective-permute-start(bf16[256,1024]{1,0:T(8,128)(2,1)S(1)} %collective-permute-done.6), channel_id=1, source_target_pairs={{0,8},{8,16},{16,24},{1,9},{9,17},{17,25},{2,10},{10,18},{18,26},{... | collective-permute-start | bytes 1572872 | tf_op jit(solution)/shard_map/ppermute | solution.py:87
  77.6 25.4 %collective-permute-start.11 = (bf16[256,1024]{1,0:T(8,128)(2,1)}, bf16[256,1024]{1,0:T(8,128)(2,1)S(1)}, u32[]{:S(2)}, u32[]{:S(2)}) collective-permute-start(bf16[256,1024]{1,0:T(8,128)(2,1)} %collective-permute-done.7), channel_id=1, source_target_pairs={{8,0},{16,8},{24,16},{9,1},{17,9},{25,17},{10,2},{18,10},{26,18},{... | collective-permute-start | bytes 1572872 | tf_op jit(solution)/shard_map/ppermute | solution.py:88
  80.5 28.6 %collective-permute-start.5 = (bf16[2,2,4,32,768]{4,3,1,0,2:T(8,128)(2,1)S(1)}, bf16[2,2,4,32,768]{4,3,1,0,2:T(8,128)(2,1)S(1)}, u32[]{:S(2)}, u32[]{:S(2)}) collective-permute-start(bf16[2,2,4,32,768]{4,3,1,0,2:T(8,128)(2,1)S(1)} %bitcast_dynamic-update-slice_fusion.11), channel_id=1, source_target_pairs={{0,1},{1,0},{2,3},{3,2},{4,5},{5,4},{6,7},{7,6},{8,9},{9,8},{10,11... | collective-permute-start | bytes 2359304 | tf_op jit(solution)/shard_map/ppermute | solution.py:57
  103.1 32.7 %collective-permute-start.16 = (bf16[256,1024]{1,0:T(8,128)(2,1)S(1)}, bf16[256,1024]{1,0:T(8,128)(2,1)S(1)}, u32[]{:S(2)}, u32[]{:S(2)}) collective-permute-start(bf16[256,1024]{1,0:T(8,128)(2,1)S(1)} %collective-permute-done.11), channel_id=1, source_target_pairs={{8,0},{16,8},{24,16},{9,1},{17,9},{25,17},{10,2},{18,10},{26,18},{... | collective-permute-start | bytes 1572872 | tf_op jit(solution)/shard_map/ppermute | solution.py:88
  104.3 31.4 %collective-permute-start.17 = (bf16[256,1024]{1,0:T(8,128)(2,1)S(1)}, bf16[256,1024]{1,0:T(8,128)(2,1)S(1)}, u32[]{:S(2)}, u32[]{:S(2)}) collective-permute-start(bf16[256,1024]{1,0:T(8,128)(2,1)S(1)} %collective-permute-done.10), channel_id=1, source_target_pairs={{0,8},{8,16},{16,24},{1,9},{9,17},{17,25},{2,10},{10,18},{18,26},{... | collective-permute-start | bytes 1572872 | tf_op jit(solution)/shard_map/ppermute | solution.py:87
  144.2 17.9 %all-to-all-start = ((bf16[4,192,1024]{2,1,0:T(8,128)(2,1)}), bf16[4,192,1024]{2,1,0:T(8,128)(2,1)}, u32[]{:S(2)}, u32[]{:S(2)}) async-start(bf16[4,192,1024]{2,1,0:T(8,128)(2,1)} %bitcast.405), calls=%async_computation | async-start | bytes 3145728 | tf_op jit(solution)/shard_map/all_to_all | solution.py:400
  164.5 8.0 %collective-permute-start.18 = (bf16[4,128,1024]{2,1,0:T(8,128)(2,1)}, bf16[4,128,1024]{2,1,0:T(8,128)(2,1)}, u32[]{:S(2)}, u32[]{:S(2)}) collective-permute-start(bf16[4,128,1024]{2,1,0:T(8,128)(2,1)} %get-tuple-element.103), channel_id=1, source_target_pairs={{0,1},{1,0},{2,3},{3,2},{4,5},{5,4},{6,7},{7,6},{8,9},{9,8},{10,11... | collective-permute-start | bytes 3145736 | tf_op jit(solution)/shard_map/ppermute | solution.py:57
  215.9 22.8 %all-to-all-start.1 = ((bf16[16,64,256]{2,1,0:T(8,128)(2,1)}), bf16[16,64,256]{2,1,0:T(8,128)(2,1)S(1)}, u32[]{:S(2)}, u32[]{:S(2)}) async-start(bf16[16,64,256]{2,1,0:T(8,128)(2,1)} %bitcast.413), calls=%async_computation.1 | async-start | bytes 1048576 | tf_op jit(solution)/shard_map/all_to_all | solution.py:422
  258.1 11.6 %collective-permute-start.24 = (f32[256,1024]{1,0:T(8,128)S(1)}, f32[256,1024]{1,0:T(8,128)S(1)}, u32[]{:S(2)}, u32[]{:S(2)}) collective-permute-start(f32[256,1024]{1,0:T(8,128)S(1)} %dynamic-slice_bitcast_fusion.6), channel_id=1, source_target_pairs={{0,1},{1,0},{2,3},{3,2},{4,5},{5,4},{6,7},{7,6},{8,9},{9,8},{10,11... | collective-permute-start | bytes 3145736 | tf_op jit(solution)/shard_map/ppermute | solution.py:57
  260.9 9.5 %collective-permute-start.22 = (f32[256,1024]{1,0:T(8,128)S(1)}, f32[256,1024]{1,0:T(8,128)S(1)}, u32[]{:S(2)}, u32[]{:S(2)}) collective-permute-start(f32[256,1024]{1,0:T(8,128)S(1)} %dynamic-slice_bitcast_fusion.7), channel_id=1, source_target_pairs={{0,1},{1,0},{2,3},{3,2},{4,5},{5,4},{6,7},{7,6},{8,9},{9,8},{10,11... | collective-permute-start | bytes 3145736 | tf_op jit(solution)/shard_map/ppermute | solution.py:57
  274.2 14.1 %collective-permute-start.25 = (bf16[16,32,1024]{2,1,0:T(8,128)(2,1)}, bf16[16,32,1024]{2,1,0:T(8,128)(2,1)}, u32[]{:S(2)}, u32[]{:S(2)}) collective-permute-start(bf16[16,32,1024]{2,1,0:T(8,128)(2,1)} %dynamic-slice_bitcast_fusion.5), channel_id=1, source_target_pairs={{0,1},{1,0},{2,3},{3,2},{4,5},{5,4},{6,7},{7,6},{8,9},{9,8},{10,11... | collective-permute-start | bytes 3145736 | tf_op jit(solution)/shard_map/ppermute | solution.py:57
  275.8 21.0 %all-to-all-start.2 = ((bf16[16,64,256]{2,1,0:T(8,128)(2,1)}), bf16[16,64,256]{2,1,0:T(8,128)(2,1)}, u32[]{:S(2)}, u32[]{:S(2)}) async-start(bf16[16,64,256]{2,1,0:T(8,128)(2,1)} %bitcast.414), calls=%async_computation.2 | async-start | bytes 1048576 | tf_op jit(solution)/shard_map/all_to_all | solution.py:453
  351.8 14.0 %collective-permute-start.27 = (bf16[4,128,1024]{1,2,0:T(8,128)(2,1)}, bf16[4,128,1024]{1,2,0:T(8,128)(2,1)}, u32[]{:S(2)}, u32[]{:S(2)}) collective-permute-start(bf16[4,128,1024]{1,2,0:T(8,128)(2,1)} %dynamic-slice_bitcast_fusion.4), channel_id=1, source_target_pairs={{0,1},{1,0},{2,3},{3,2},{4,5},{5,4},{6,7},{7,6},{8,9},{9,8},{10,11... | collective-permute-start | bytes 3145736 | tf_op jit(solution)/shard_map/ppermute | solution.py:57
  355.0 71.8 %collective-permute-start.28 = (bf16[2,4,64,2048]{3,2,0,1:T(8,128)(2,1)}, bf16[2,4,64,2048]{3,2,0,1:T(8,128)(2,1)}, u32[]{:S(2)}, u32[]{:S(2)}) collective-permute-start(bf16[2,4,64,2048]{3,2,0,1:T(8,128)(2,1)} %dynamic-slice_bitcast_fusion), channel_id=1, source_target_pairs={{0,4},{4,0},{1,5},{5,1},{2,6},{6,2},{3,7},{7,3},{8,12},{12,8},{9,1... | collective-permute-start | bytes 6291464 | tf_op jit(solution)/shard_map/ppermute | solution.py:57
  358.8 62.2 %collective-permute-start.29 = (bf16[2,4,64,1024]{3,2,1,0:T(8,128)(2,1)}, bf16[2,4,64,1024]{3,2,1,0:T(8,128)(2,1)}, u32[]{:S(2)}, u32[]{:S(2)}) collective-permute-start(bf16[2,4,64,1024]{3,2,1,0:T(8,128)(2,1)} %dynamic-slice_bitcast_fusion.3), channel_id=1, source_target_pairs={{0,2},{2,0},{1,3},{3,1},{4,6},{6,4},{5,7},{7,5},{8,10},{10,8},{9,1... | collective-permute-start | bytes 3145736 | tf_op jit(solution)/shard_map/ppermute | solution.py:57
  360.5 63.7 %collective-permute-start.30 = (bf16[2,4,64,1024]{3,2,1,0:T(8,128)(2,1)}, bf16[2,4,64,1024]{3,2,1,0:T(8,128)(2,1)}, u32[]{:S(2)}, u32[]{:S(2)}) collective-permute-start(bf16[2,4,64,1024]{3,2,1,0:T(8,128)(2,1)} %dynamic-slice_bitcast_fusion.2), channel_id=1, source_target_pairs={{0,2},{2,0},{1,3},{3,1},{4,6},{6,4},{5,7},{7,5},{8,10},{10,8},{9,1... | collective-permute-start | bytes 3145736 | tf_op jit(solution)/shard_map/ppermute | solution.py:57
  362.8 56.0 %collective-permute-start.31 = (bf16[2,4,32,1024]{3,2,0,1:T(8,128)(2,1)}, bf16[2,4,32,1024]{3,2,0,1:T(8,128)(2,1)}, u32[]{:S(2)}, u32[]{:S(2)}) collective-permute-start(bf16[2,4,32,1024]{3,2,0,1:T(8,128)(2,1)} %dynamic-slice_bitcast_fusion.14), channel_id=1, source_target_pairs={{0,2},{2,0},{1,3},{3,1},{4,6},{6,4},{5,7},{7,5},{8,10},{10,8},{9,1... | collective-permute-start | bytes 1572872 | tf_op jit(solution)/shard_map/ppermute | solution.py:57
  373.9 60.9 %all-to-all-start.3 = ((bf16[4,192,1024]{2,1,0:T(8,128)(2,1)}), bf16[4,192,1024]{2,1,0:T(8,128)(2,1)}, u32[]{:S(2)}, u32[]{:S(2)}) async-start(bf16[4,192,1024]{2,1,0:T(8,128)(2,1)} %copy.195), calls=%async_computation.3 | async-start | bytes 3145728 | tf_op jit(solution)/shard_map/all_to_all | solution.py:483
  443.7 49.0 %collective-permute-start.34 = (bf16[256,1024]{1,0:T(8,128)(2,1)}, bf16[256,1024]{1,0:T(8,128)(2,1)}, u32[]{:S(2)}, u32[]{:S(2)}) collective-permute-start(bf16[256,1024]{1,0:T(8,128)(2,1)} %get-tuple-element.101), channel_id=1, source_target_pairs={{0,24},{8,0},{16,8},{24,16},{1,25},{9,1},{17,9},{25,17},{2,26},{10... | collective-permute-start | bytes 1572872 | tf_op jit(solution)/shard_map/ppermute | solution.py:57
  448.2 41.5 %collective-permute-start.36 = (bf16[4,64,1024]{2,1,0:T(8,128)(2,1)}, bf16[4,64,1024]{2,1,0:T(8,128)(2,1)}, u32[]{:S(2)}, u32[]{:S(2)}) collective-permute-start(bf16[4,64,1024]{2,1,0:T(8,128)(2,1)} %dynamic-slice_bitcast_fusion.10), channel_id=1, source_target_pairs={{0,4},{4,0},{1,5},{5,1},{2,6},{6,2},{3,7},{7,3},{8,12},{12,8},{9,1... | collective-permute-start | bytes 1572872 | tf_op jit(solution)/shard_map/ppermute | solution.py:57
  464.0 25.8 %collective-permute-start.37 = (bf16[4,64,1024]{2,1,0:T(8,128)(2,1)S(1)}, bf16[4,64,1024]{2,1,0:T(8,128)(2,1)S(1)}, u32[]{:S(2)}, u32[]{:S(2)}) collective-permute-start(bf16[4,64,1024]{2,1,0:T(8,128)(2,1)S(1)} %copy-done.27), channel_id=1, source_target_pairs={{0,4},{4,0},{1,5},{5,1},{2,6},{6,2},{3,7},{7,3},{8,12},{12,8},{9,1... | collective-permute-start | bytes 1572872 | tf_op jit(solution)/shard_map/ppermute | solution.py:57
  466.2 21.6 %collective-permute-start.38 = (bf16[4,32,1024]{2,1,0:T(8,128)(2,1)S(1)}, bf16[4,32,1024]{2,1,0:T(8,128)(2,1)S(1)}, u32[]{:S(2)}, u32[]{:S(2)}) collective-permute-start(bf16[4,32,1024]{2,1,0:T(8,128)(2,1)S(1)} %copy-done.30), channel_id=1, source_target_pairs={{0,4},{4,0},{1,5},{5,1},{2,6},{6,2},{3,7},{7,3},{8,12},{12,8},{9,1... | collective-permute-start | bytes 786440 | tf_op jit(solution)/shard_map/ppermute | solution.py:57
  468.1 13.1 %collective-permute-start.51 = (f32[2,256]{1,0:T(2,128)S(1)}, f32[2,256]{1,0:T(2,128)S(1)}, u32[]{:S(2)}, u32[]{:S(2)}) collective-permute-start(f32[2,256]{1,0:T(2,128)S(1)} %fusion.97), channel_id=1, source_target_pairs={{0,4},{4,0},{1,5},{5,1},{2,6},{6,2},{3,7},{7,3},{8,12},{12,8},{9,1... | collective-permute-start | bytes 6152 | tf_op jit(solution)/shard_map/ppermute | solution.py:57
  484.9 33.1 %collective-permute-start.33 = (bf16[256,1024]{1,0:T(8,128)(2,1)S(1)}, bf16[256,1024]{1,0:T(8,128)(2,1)S(1)}, u32[]{:S(2)}, u32[]{:S(2)}) collective-permute-start(bf16[256,1024]{1,0:T(8,128)(2,1)S(1)} %copy-done.26), channel_id=1, source_target_pairs={{0,16},{8,24},{16,0},{24,8},{1,17},{9,25},{17,1},{25,9},{2,18},{10... | collective-permute-start | bytes 1572872 | tf_op jit(solution)/shard_map/ppermute | solution.py:57
  487.8 30.2 %collective-permute-start.32 = (bf16[256,1024]{1,0:T(8,128)(2,1)S(1)}, bf16[256,1024]{1,0:T(8,128)(2,1)S(1)}, u32[]{:S(2)}, u32[]{:S(2)}) collective-permute-start(bf16[256,1024]{1,0:T(8,128)(2,1)S(1)} %copy-done.25), channel_id=1, source_target_pairs={{0,8},{8,16},{16,24},{24,0},{1,9},{9,17},{17,25},{25,1},{2,10},{10... | collective-permute-start | bytes 1572872 | tf_op jit(solution)/shard_map/ppermute | solution.py:57
  489.7 29.8 %collective-permute-start.39 = (bf16[4,4,32,896]{3,2,0,1:T(8,128)(2,1)S(1)}, bf16[4,4,32,896]{3,2,0,1:T(8,128)(2,1)S(1)}, u32[]{:S(2)}, u32[]{:S(2)}) collective-permute-start(bf16[4,4,32,896]{3,2,0,1:T(8,128)(2,1)S(1)} %dynamic-slice_bitcast_fusion.8), channel_id=1, source_target_pairs={{0,1},{1,0},{2,3},{3,2},{4,5},{5,4},{6,7},{7,6},{8,9},{9,8},{10,11... | collective-permute-start | bytes 2752520 | tf_op jit(solution)/shard_map/ppermute | solution.py:57
  489.8 31.4 %collective-permute-start.35 = (bf16[4,64,2048]{2,1,0:T(8,128)(2,1)S(1)}, bf16[4,64,2048]{2,1,0:T(8,128)(2,1)S(1)}, u32[]{:S(2)}, u32[]{:S(2)}) collective-permute-start(bf16[4,64,2048]{2,1,0:T(8,128)(2,1)S(1)} %copy-done.23), channel_id=1, source_target_pairs={{0,2},{2,0},{1,3},{3,1},{4,6},{6,4},{5,7},{7,5},{8,10},{10,8},{9,1... | collective-permute-start | bytes 3145736 | tf_op jit(solution)/shard_map/ppermute | solution.py:57
  520.0 45.8 %collective-permute-start.40 = (bf16[2,4,32,896]{3,2,1,0:T(8,128)(2,1)S(1)}, bf16[2,4,32,896]{3,2,1,0:T(8,128)(2,1)S(1)}, u32[]{:S(2)}, u32[]{:S(2)}) collective-permute-start(bf16[2,4,32,896]{3,2,1,0:T(8,128)(2,1)S(1)} %dynamic-slice_bitcast_fusion.15), channel_id=1, source_target_pairs={{0,4},{4,0},{1,5},{5,1},{2,6},{6,2},{3,7},{7,3},{8,12},{12,8},{9,1... | collective-permute-start | bytes 1376264 | tf_op jit(solution)/shard_map/ppermute | solution.py:57
  522.4 8.7 %collective-permute-start.46 = (bf16[32,1024]{1,0:T(8,128)(2,1)S(1)}, bf16[32,1024]{1,0:T(8,128)(2,1)S(1)}, u32[]{:S(2)}, u32[]{:S(2)}) collective-permute-start(bf16[32,1024]{1,0:T(8,128)(2,1)S(1)} %get-tuple-element.120), channel_id=1, source_target_pairs={{0,16},{8,24},{16,0},{24,8},{1,17},{9,25},{17,1},{25,9},{2,18},{10... | collective-permute-start | bytes 196616 | tf_op jit(solution)/shard_map/ppermute | solution.py:57
  526.7 40.6 %collective-permute-start.55 = (bf16[64,2048]{1,0:T(8,128)(2,1)S(1)}, bf16[64,2048]{1,0:T(8,128)(2,1)S(1)}, u32[]{:S(2)}, u32[]{:S(2)}) collective-permute-start(bf16[64,2048]{1,0:T(8,128)(2,1)S(1)} %get-tuple-element.106), channel_id=1, source_target_pairs={{0,24},{8,0},{16,8},{24,16},{1,25},{9,1},{17,9},{25,17},{2,26},{10... | collective-permute-start | bytes 786440 | tf_op jit(solution)/shard_map/ppermute | solution.py:57
  529.8 11.4 %collective-permute-start.62 = (bf16[64,1024]{1,0:T(8,128)(2,1)S(1)}, bf16[64,1024]{1,0:T(8,128)(2,1)S(1)}, u32[]{:S(2)}, u32[]{:S(2)}) collective-permute-start(bf16[64,1024]{1,0:T(8,128)(2,1)S(1)} %get-tuple-element.113), channel_id=1, source_target_pairs={{0,24},{8,0},{16,8},{24,16},{1,25},{9,1},{17,9},{25,17},{2,26},{10... | collective-permute-start | bytes 393224 | tf_op jit(solution)/shard_map/ppermute | solution.py:57
  531.1 17.1 %collective-permute-start.61 = (bf16[64,1024]{1,0:T(8,128)(2,1)S(1)}, bf16[64,1024]{1,0:T(8,128)(2,1)S(1)}, u32[]{:S(2)}, u32[]{:S(2)}) collective-permute-start(bf16[64,1024]{1,0:T(8,128)(2,1)S(1)} %get-tuple-element.114), channel_id=1, source_target_pairs={{0,16},{8,24},{16,0},{24,8},{1,17},{9,25},{17,1},{25,9},{2,18},{10... | collective-permute-start | bytes 393224 | tf_op jit(solution)/shard_map/ppermute | solution.py:57
  531.5 16.6 %collective-permute-start.60 = (bf16[64,1024]{1,0:T(8,128)(2,1)S(1)}, bf16[64,1024]{1,0:T(8,128)(2,1)S(1)}, u32[]{:S(2)}, u32[]{:S(2)}) collective-permute-start(bf16[64,1024]{1,0:T(8,128)(2,1)S(1)} %get-tuple-element.112), channel_id=1, source_target_pairs={{0,8},{8,16},{16,24},{24,0},{1,9},{9,17},{17,25},{25,1},{2,10},{10... | collective-permute-start | bytes 393224 | tf_op jit(solution)/shard_map/ppermute | solution.py:57
  541.2 11.8 %collective-permute-start.59 = (bf16[64,1024]{1,0:T(8,128)(2,1)S(1)}, bf16[64,1024]{1,0:T(8,128)(2,1)S(1)}, u32[]{:S(2)}, u32[]{:S(2)}) collective-permute-start(bf16[64,1024]{1,0:T(8,128)(2,1)S(1)} %get-tuple-element.110), channel_id=1, source_target_pairs={{0,24},{8,0},{16,8},{24,16},{1,25},{9,1},{17,9},{25,17},{2,26},{10... | collective-permute-start | bytes 393224 | tf_op jit(solution)/shard_map/ppermute | solution.py:57
  548.1 16.7 %collective-permute-start.58 = (bf16[64,1024]{1,0:T(8,128)(2,1)S(1)}, bf16[64,1024]{1,0:T(8,128)(2,1)S(1)}, u32[]{:S(2)}, u32[]{:S(2)}) collective-permute-start(bf16[64,1024]{1,0:T(8,128)(2,1)S(1)} %get-tuple-element.111), channel_id=1, source_target_pairs={{0,16},{8,24},{16,0},{24,8},{1,17},{9,25},{17,1},{25,9},{2,18},{10... | collective-permute-start | bytes 393224 | tf_op jit(solution)/shard_map/ppermute | solution.py:57
  548.1 16.7 %collective-permute-start.57 = (bf16[64,1024]{1,0:T(8,128)(2,1)S(1)}, bf16[64,1024]{1,0:T(8,128)(2,1)S(1)}, u32[]{:S(2)}, u32[]{:S(2)}) collective-permute-start(bf16[64,1024]{1,0:T(8,128)(2,1)S(1)} %get-tuple-element.109), channel_id=1, source_target_pairs={{0,8},{8,16},{16,24},{24,0},{1,9},{9,17},{17,25},{25,1},{2,10},{10... | collective-permute-start | bytes 393224 | tf_op jit(solution)/shard_map/ppermute | solution.py:57
  553.0 23.0 %collective-permute-start.54 = (bf16[64,2048]{1,0:T(8,128)(2,1)S(1)}, bf16[64,2048]{1,0:T(8,128)(2,1)S(1)}, u32[]{:S(2)}, u32[]{:S(2)}) collective-permute-start(bf16[64,2048]{1,0:T(8,128)(2,1)S(1)} %get-tuple-element.107), channel_id=1, source_target_pairs={{0,16},{8,24},{16,0},{24,8},{1,17},{9,25},{17,1},{25,9},{2,18},{10... | collective-permute-start | bytes 786440 | tf_op jit(solution)/shard_map/ppermute | solution.py:57
  564.8 11.1 %collective-permute-start.53 = (bf16[64,2048]{1,0:T(8,128)(2,1)S(1)}, bf16[64,2048]{1,0:T(8,128)(2,1)S(1)}, u32[]{:S(2)}, u32[]{:S(2)}) collective-permute-start(bf16[64,2048]{1,0:T(8,128)(2,1)S(1)} %get-tuple-element.105), channel_id=1, source_target_pairs={{0,8},{8,16},{16,24},{24,0},{1,9},{9,17},{17,25},{25,1},{2,10},{10... | collective-permute-start | bytes 786440 | tf_op jit(solution)/shard_map/ppermute | solution.py:57
  565.9 10.4 %collective-permute-start.41 = (bf16[4,32,896]{2,1,0:T(8,128)(2,1)S(1)}, bf16[4,32,896]{2,1,0:T(8,128)(2,1)S(1)}, u32[]{:S(2)}, u32[]{:S(2)}) collective-permute-start(bf16[4,32,896]{2,1,0:T(8,128)(2,1)S(1)} %dynamic-slice_bitcast_fusion.20), channel_id=1, source_target_pairs={{0,2},{2,0},{1,3},{3,1},{4,6},{6,4},{5,7},{7,5},{8,10},{10,8},{9,1... | collective-permute-start | bytes 688136 | tf_op jit(solution)/shard_map/ppermute | solution.py:57
  (70 other events, 556.7 us)
Sparse Core Ops, SparseCore 0:
  12.5 164.2 all-gather.1

commit v3 on v2

--- a/solution.py
+++ b/solution.py
@@ -100,16 +100,24 @@
     return put(out, third, jnp.where(me == 0, 3, jnp.where(me == 3, 0, jnp.where(me == 1, 0, 3))))
 
 
-def reduce_axis(x, axis):
+def reduce_begin(x, axis):
     n = lax.axis_size(axis)
     if n == 1:
-        return x[0].astype(f32)
+        return [x[0]]
     me = lax.axis_index(axis)
-    total = lax.dynamic_index_in_dim(x, me, 0, keepdims=False).astype(f32)
-    for k in range(1, n):
-        piece = lax.dynamic_index_in_dim(x, (me + k) % n, 0, keepdims=False)
-        total = total + shifted(piece, axis, k).astype(f32)
+    pieces = [lax.dynamic_index_in_dim(x, (me + k) % n, 0, keepdims=False) for k in range(n)]
+    return pieces[:1] + [shifted(pieces[k], axis, k) for k in range(1, n)]
+
+
+def reduce_end(pieces):
+    total = pieces[0].astype(f32)
+    for piece in pieces[1:]:
+        total = total + piece.astype(f32)
     return total
+
+
+def reduce_axis(x, axis):
+    return reduce_end(reduce_begin(x, axis))
 
 
 def exchange_axis(x, axis):
@@ -130,20 +138,35 @@
     return (t >= starts) & (t <= pos)
 
 
-def lay_rows(kv_ref, rows_ref):
-    def lay(i, _):
-        rows_ref[pl.ds(pl.multiple_of(i * BLOCK_K, BLOCK_K), BLOCK_K), :] = kv_ref[i].T
+def lay_rows(me, own_ref, far_ref, rows_ref, cols_ref, first):
+    hb, _, block_rows = own_ref.shape
+    n_rest = far_ref.shape[0] + 1
+    subs = block_rows // BLOCK_K
+
+    def lay(read, b, rest):
+        for sub in range(subs):
+            kb = (b * n_rest + rest) * subs + sub
+            block = read(b)[:, sub * BLOCK_K : (sub + 1) * BLOCK_K]
+            rows_ref[pl.ds(pl.multiple_of(kb * BLOCK_K, BLOCK_K), BLOCK_K), :] = block[HEAD_DIM:].T
+            cols_ref[kb] = block[first : first + HEAD_DIM]
+
+    def each(b, _):
+        lay(lambda b: own_ref[b], b, me)
+        for k in range(1, n_rest):
+            lay(lambda b: far_ref[k - 1, b], b, (me - k) % n_rest)
         return 0
 
-    lax.fori_loop(0, kv_ref.shape[0], lay, 0)
-
-
-def forward_kernel(lo_ref, mid_ref, q0_ref, q_ref, kv_ref, start_ref, o_ref, wide_ref, lse_ref, rows_ref):
+    lax.fori_loop(0, hb, each, 0)
+
+
+def forward_kernel(
+    lo_ref, mid_ref, q0_ref, me_ref, q_ref, own_ref, far_ref, start_ref, o_ref, wide_ref, lse_ref, rows_ref, cols_ref
+):
     step = pl.program_id(0)
 
     @pl.when(step == 0)
     def _():
-        lay_rows(kv_ref, rows_ref)
+        lay_rows(me_ref[0], own_ref, far_ref, rows_ref, cols_ref, 2 * HEAD_DIM)
 
     first = q0_ref[step]
     q = q_ref[0] * jnp.asarray(SCALE, bf16)
@@ -160,7 +183,7 @@
         new_top = jnp.maximum(top, jnp.max(s, axis=0, keepdims=True))
         p = jnp.exp(s - new_top)
         factor = jnp.exp(top - new_top)
-        values = kv_ref[kb, HEAD_DIM:, :]
+        values = cols_ref[kb]
         acc = acc * factor + jnp.dot(values, p.astype(bf16), preferred_element_type=f32)
         return (new_top, total * factor + jnp.sum(p, axis=0, keepdims=True), acc)
 
@@ -185,13 +208,29 @@
 
 
 def backward_kernel(
-    n_steps, lo_ref, mid_ref, q0_ref, q_ref, kv_ref, start_ref, do_ref, wide_ref, lse_ref, dq_ref, dkv_ref, rows_ref, acc_ref
+    n_steps,
+    lo_ref,
+    mid_ref,
+    q0_ref,
+    me_ref,
+    q_ref,
+    own_ref,
+    far_ref,
+    start_ref,
+    do_ref,
+    wide_ref,
+    lse_ref,
+    dq_ref,
+    dkv_ref,
+    rows_ref,
+    cols_ref,
+    acc_ref,
 ):
     step = pl.program_id(0)
 
     @pl.when(step == 0)
     def _():
-        lay_rows(kv_ref, rows_ref)
+        lay_rows(me_ref[0], own_ref, far_ref, rows_ref, cols_ref, HEAD_DIM)
         acc_ref[...] = jnp.zeros_like(acc_ref)
 
     @pl.when(step < n_steps)
@@ -221,7 +260,7 @@
             acc_ref[at, :] += jnp.dot(p.astype(bf16), do_rows, preferred_element_type=f32) + jnp.dot(
                 ds, q_rows, preferred_element_type=f32
             )
-            return dq + jnp.dot(kv_ref[kb, :HEAD_DIM, :], ds, preferred_element_type=f32)
+            return dq + jnp.dot(cols_ref[kb], ds, preferred_element_type=f32)
 
         diagonal = first // BLOCK_K
         mid = jnp.minimum(mid_ref[step], diagonal)
@@ -236,13 +275,13 @@
     def _():
         kb = jnp.maximum(step - n_steps, 0)
         at = pl.ds(pl.multiple_of(kb * BLOCK_K, BLOCK_K), BLOCK_K)
-        dkv_ref[0] = acc_ref[at, :].astype(bf16).T
-
-
-def attention_specs(block_rows, tok_rows, keys):
+        dkv_ref[0, 0] = acc_ref[at, :].astype(bf16).T
+
+
+def attention_specs(qkv, far, tok_rows):
+    hb, depth, block_rows = qkv.shape
     subs = block_rows // BLOCK_Q
     pieces = BLOCK_Q // tok_rows
-    n_kb = keys // BLOCK_K
 
     def wrap(index):
         return lambda i, *_: index(i)
@@ -252,26 +291,33 @@
     piece_spec = lambda cap: pl.BlockSpec(
         (pieces, 1, HEAD_DIM, tok_rows), wrap(lambda i: (cap(i) % subs, cap(i) // subs, 0, 0))
     )
-    kv_spec = pl.BlockSpec(
-        (n_kb, 2 * HEAD_DIM, BLOCK_K), wrap(lambda i: (0, 0, 0)), pipeline_mode=pl.Buffered(1)
-    )
-    return q_spec, row_spec, piece_spec, kv_spec
-
-
-def attention_forward(bounds, qkv, kv, starts, n_head, tok_rows):
+    own_spec = pl.BlockSpec((hb, depth, block_rows), wrap(lambda i: (0, 0, 0)), pipeline_mode=pl.Buffered(1))
+    far_spec = pl.BlockSpec(far.shape, wrap(lambda i: (0, 0, 0, 0)), pipeline_mode=pl.Buffered(1))
+    return q_spec, row_spec, piece_spec, own_spec, far_spec
+
+
+def padded_cost(products, queries, keys):
+    pairs = queries * keys // 2
+    return pl.CostEstimate(flops=products * 2 * 256 * pairs, transcendentals=pairs, bytes_accessed=8 * keys * HEAD_DIM)
+
+
+def attention_forward(bounds, qkv, far, starts, n_head, tok_rows):
     hb, _, block_rows = qkv.shape
-    keys = kv.shape[0] * BLOCK_K
-    n_steps = hb * block_rows // BLOCK_Q
-    q_spec, row_spec, piece_spec, kv_spec = attention_specs(block_rows, tok_rows, keys)
+    queries = hb * block_rows
+    keys = queries * (far.shape[0] + 1)
+    q_spec, row_spec, piece_spec, own_spec, far_spec = attention_specs(qkv, far, tok_rows)
     same = lambda i: i
     return pl.pallas_call(
         forward_kernel,
         grid_spec=pltpu.PrefetchScalarGridSpec(
-            num_scalar_prefetch=3,
-            grid=(n_steps,),
-            in_specs=[q_spec(same), kv_spec, row_spec(same)],
+            num_scalar_prefetch=4,
+            grid=(queries // BLOCK_Q,),
+            in_specs=[q_spec(same), own_spec, far_spec, row_spec(same)],
             out_specs=[piece_spec(same), q_spec(same), row_spec(same)],
-            scratch_shapes=[pltpu.VMEM((keys, 2 * HEAD_DIM), bf16)],
+            scratch_shapes=[
+                pltpu.VMEM((keys, 2 * HEAD_DIM), bf16),
+                pltpu.VMEM((keys // BLOCK_K, HEAD_DIM, BLOCK_K), bf16),
+            ],
         ),
         out_shape=[
             jax.ShapeDtypeStruct((n_head, hb, HEAD_DIM, tok_rows), bf16),
@@ -279,36 +325,47 @@
             jax.ShapeDtypeStruct((hb, 1, block_rows), f32),
         ],
         compiler_params=pltpu.CompilerParams(vmem_limit_bytes=VMEM_BYTES),
+        cost_estimate=padded_cost(2, queries, keys),
         name="attention_forward",
-    )(*bounds, qkv, kv, starts)
-
-
-def attention_backward(bounds, qkv, kv, starts, do, wide, lse):
+    )(*bounds, qkv, qkv, far, starts)
+
+
+def attention_backward(bounds, qkv, far, starts, do, wide, lse):
     hb, _, block_rows = qkv.shape
-    n_kb = kv.shape[0]
-    keys = n_kb * BLOCK_K
-    n_steps = hb * block_rows // BLOCK_Q
-    q_spec, row_spec, piece_spec, kv_spec = attention_specs(block_rows, do.shape[3], keys)
+    n_rest = far.shape[0] + 1
+    queries = hb * block_rows
+    keys = queries * n_rest
+    n_kb = keys // BLOCK_K
+    subs = block_rows // BLOCK_K
+    n_steps = queries // BLOCK_Q
+    q_spec, row_spec, piece_spec, own_spec, far_spec = attention_specs(qkv, far, do.shape[3])
     cap = lambda i: jnp.minimum(i, n_steps - 1)
+
+    def place(i, *_):
+        kb = jnp.maximum(i - n_steps, 0)
+        return (kb // subs % n_rest, kb // subs // n_rest, 0, kb % subs)
+
     return pl.pallas_call(
         functools.partial(backward_kernel, n_steps),
         grid_spec=pltpu.PrefetchScalarGridSpec(
-            num_scalar_prefetch=3,
+            num_scalar_prefetch=4,
             grid=(n_steps + n_kb,),
-            in_specs=[q_spec(cap), kv_spec, row_spec(cap), piece_spec(cap), q_spec(cap), row_spec(cap)],
-            out_specs=[
-                q_spec(cap),
-                pl.BlockSpec((1, 2 * HEAD_DIM, BLOCK_K), lambda i, *_: (jnp.maximum(i - n_steps, 0), 0, 0)),
+            in_specs=[q_spec(cap), own_spec, far_spec, row_spec(cap), piece_spec(cap), q_spec(cap), row_spec(cap)],
+            out_specs=[q_spec(cap), pl.BlockSpec((1, 1, 2 * HEAD_DIM, BLOCK_K), place)],
+            scratch_shapes=[
+                pltpu.VMEM((keys, 2 * HEAD_DIM), bf16),
+                pltpu.VMEM((n_kb, HEAD_DIM, BLOCK_K), bf16),
+                pltpu.VMEM((keys, 2 * HEAD_DIM), f32),
             ],
-            scratch_shapes=[pltpu.VMEM((keys, 2 * HEAD_DIM), bf16), pltpu.VMEM((keys, 2 * HEAD_DIM), f32)],
         ),
         out_shape=[
             jax.ShapeDtypeStruct((hb, HEAD_DIM, block_rows), bf16),
-            jax.ShapeDtypeStruct((n_kb, 2 * HEAD_DIM, BLOCK_K), bf16),
+            jax.ShapeDtypeStruct((n_rest, hb, 2 * HEAD_DIM, block_rows), bf16),
         ],
         compiler_params=pltpu.CompilerParams(vmem_limit_bytes=VMEM_BYTES),
+        cost_estimate=padded_cost(5, queries, keys),
         name="attention_backward",
-    )(*bounds, qkv, kv, starts, do, wide, lse)
+    )(*bounds, qkv, qkv, far, starts, do, wide, lse)
 
 
 def on_device(
@@ -349,6 +406,27 @@
     out_rows = gather_axis(out_weight, "rest").reshape(n_rest * w_rows, width)
     down_rows = down_weight.reshape(2, f_rows, width)
     f_half = chips * f_rows
+
+    parts = [norm_gain, norm_shift, query_bias, value_bias, out_bias, post_gain, post_shift, down_bias, up_bias]
+    packed = [jnp.concatenate(parts).reshape(1, -1)]
+
+    cols = in_weight.reshape(w_rows, 3, n_head, hb, HEAD_DIM).transpose(2, 0, 3, 1, 4).reshape(n_head, w_rows, group)
+    w_in = [cols]
+
+    def chain_one():
+        for axis in ("rest", "v"):
+            packed[0] = gather_axis(packed[0], axis)
+        w_in[0] = exchange_axis(w_in[0], "head")
+        return (packed[0], w_in[0])
+
+    def chain_two():
+        for axis in ("u", "head"):
+            packed[0] = gather_axis(packed[0], axis)
+        w_in[0] = gather_axis(w_in[0], "v")
+        return (packed[0], w_in[0])
+
+    rows_all = gather_line(tokens, "head", [chain_one, chain_two, None]).reshape(block_rows, width).astype(f32)
+    rows_all, up_cols, down_rows, out_rows = lax.optimization_barrier((rows_all, up_cols, down_rows, out_rows))
     if f_rows == n_rest * w_rows:
         joint = jnp.concatenate([up_cols, down_rows[0], down_rows[1], out_rows], axis=1)
         joint = lax.all_gather(joint, ("head", "u", "v"), axis=0, tiled=True)
@@ -362,25 +440,6 @@
         )
         w_down = w_down_a, w_down_b
 
-    parts = [norm_gain, norm_shift, query_bias, value_bias, out_bias, post_gain, post_shift, down_bias, up_bias]
-    packed = [jnp.concatenate(parts).reshape(1, -1)]
-
-    cols = in_weight.reshape(w_rows, 3, n_head, hb, HEAD_DIM).transpose(2, 0, 3, 1, 4).reshape(n_head, w_rows, group)
-    w_in = [cols]
-
-    def chain_one():
-        for axis in ("rest", "v"):
-            packed[0] = gather_axis(packed[0], axis)
-        w_in[0] = exchange_axis(w_in[0], "head")
-        return (packed[0], w_in[0])
-
-    def chain_two():
-        for axis in ("u", "head"):
-            packed[0] = gather_axis(packed[0], axis)
-        w_in[0] = gather_axis(w_in[0], "v")
-        return (packed[0], w_in[0])
-
-    rows_all = gather_line(tokens, "head", [chain_one, chain_two, None]).reshape(block_rows, width).astype(f32)
     packed = packed[0].reshape(n_all, -1)
     vectors, at = [], 0
     for part in parts:
@@ -400,10 +459,8 @@
     qkv = lax.all_to_all(
         projected.reshape(hb, 3 * HEAD_DIM, block_rows), ("u", "v"), split_axis=0, concat_axis=0, tiled=True
     )
-    subs_k = block_rows // BLOCK_K
-    kv = gather_axis(qkv[:, HEAD_DIM:], "rest")
-    kv = kv.reshape(n_rest, hb, 2 * HEAD_DIM, subs_k, BLOCK_K).transpose(1, 0, 3, 2, 4)
-    kv = kv.reshape(n_blk * subs_k, 2 * HEAD_DIM, BLOCK_K)
+    far = [shifted(qkv, "rest", k) for k in range(1, n_rest)]
+    far = jnp.stack(far) if n_rest > 2 else far[0][None]
 
     doc_start = jnp.zeros_like(segment)
     for doc in range(1, DOCS):
@@ -415,10 +472,10 @@
     mid = (starts_q[:, -1] + BLOCK_K - 1) // BLOCK_K
     q_first = (jnp.arange(hb, dtype=jnp.int32)[:, None] * n_rest + me_rest) * block_rows
     q_first = (q_first + jnp.arange(block_rows // BLOCK_Q, dtype=jnp.int32)[None] * BLOCK_Q).reshape(-1)
-    bounds = (lo, mid, q_first)
+    bounds = (lo, mid, q_first, me_rest.astype(jnp.int32).reshape(1))
     starts = starts.reshape(hb, 1, block_rows)
 
-    attended, wide, lse = attention_forward(bounds, qkv, kv, starts, n_head, tok_rows)
+    attended, wide, lse = attention_forward(bounds, qkv, far, starts, n_head, tok_rows)
     back = lax.all_to_all(
         attended.reshape(HEADS, HEAD_DIM, tok_rows), ("head", "u", "v"), split_axis=0, concat_axis=0, tiled=True
     ).reshape(width, tok_rows)
@@ -460,8 +517,9 @@
     out_grad = out_grad.reshape(chips, n_rest, w_rows, width).transpose(1, 0, 2, 3)
     out_grad = reduce_axis(out_grad, "rest").astype(bf16)
     plane = lambda x: x.reshape(n_head, n_u, n_v, -1, x.shape[-1])
-    by_u = [plane(up_grad).transpose(1, 2, 0, 3, 4)]
-    by_v = [plane(x).transpose(2, 1, 0, 3, 4) for x in (*down_grads, out_grad)]
+    up_grad = plane(up_grad).transpose(1, 2, 0, 3, 4)
+    down_a, out_grad = (plane(x).transpose(2, 1, 0, 3, 4) for x in (down_grads[0], out_grad))
+    down_b = plane(down_grads[1])
     sums = [
         jnp.sum(grad_branch.astype(f32), axis=0),
         jnp.sum(grad_hidden * unit_mid, axis=0),
@@ -473,31 +531,39 @@
     unit_sum = jnp.sum(grad_pre.astype(f32), axis=0).reshape(2, chips, f_rows).transpose(1, 0, 2).reshape(chips, -1)
     small = jnp.concatenate([small, unit_sum], axis=1).reshape(n_head, n_u, n_v, -1)
 
-    grad_heads, by_u, by_v, small = lax.optimization_barrier((grad_heads, by_u, by_v, small))
-    by_u = [reduce_axis(x, "u").astype(bf16) for x in by_u]
-    by_v = [reduce_axis(x, "v").astype(bf16) for x in by_v]
-
-    dq, dkv = attention_backward(bounds, qkv, kv, starts, grad_heads, wide, lse)
-    dkv = dkv.reshape(hb, n_rest, subs_k, 2 * HEAD_DIM, BLOCK_K).transpose(1, 0, 3, 2, 4)
-    dkv = reduce_axis(dkv.reshape(n_rest, hb, 2 * HEAD_DIM, block_rows), "rest").astype(bf16)
+    grad_heads, up_grad, down_a, out_grad, down_b, small = lax.optimization_barrier(
+        (grad_heads, up_grad, down_a, out_grad, down_b, small)
+    )
+    begun = [reduce_begin(up_grad, "u"), reduce_begin(down_a, "v"), reduce_begin(out_grad, "v")]
+    begun.append(reduce_begin(down_b, "head"))
+
+    dq, dkv = attention_backward(bounds, qkv, far, starts, grad_heads, wide, lse)
+    dq, dkv, begun = lax.optimization_barrier((dq, dkv, begun))
+    up_grad, down_a, out_grad, down_b = (reduce_end(x).astype(bf16) for x in begun)
+    dkv = reduce_axis(dkv, "rest").astype(bf16)
     grad_proj = lax.all_to_all(
         jnp.concatenate([dq, dkv], axis=1), ("u", "v"), split_axis=0, concat_axis=0, tiled=True
     ).reshape(group, block_rows)
 
-    grad_proj, by_u, by_v, small = lax.optimization_barrier((grad_proj, by_u, by_v, small))
-    by_u = [reduce_axis(x, "v").astype(bf16) for x in by_u]
-    by_v = [reduce_axis(x, "u").astype(bf16) for x in by_v]
+    grad_proj, up_grad, down_a, out_grad, down_b, small = lax.optimization_barrier(
+        (grad_proj, up_grad, down_a, out_grad, down_b, small)
+    )
+    up_grad = reduce_axis(up_grad, "v").astype(bf16)
+    down_a, out_grad, down_b = (reduce_axis(x, "u").astype(bf16) for x in (down_a, out_grad, down_b))
     small = reduce_axis(reduce_axis(small, "head"), "u")
     small = reduce_axis(small, "v")
 
     grad_normed = lax.dot_general(grad_proj, w_in, (((0,), (1,)), ((), ())), preferred_element_type=f32)
     grad_tokens = reduce_axis(grad_normed.astype(bf16).reshape(n_head, tok_rows, width), "head")
-    grad_tokens, by_u, by_v = lax.optimization_barrier((grad_tokens, by_u, by_v))
-    up_weight_grad = reduce_axis(by_u[0], "head").astype(bf16).reshape(n_rest, w_rows, -1)
+    grad_tokens, up_grad, down_a, out_grad, down_b = lax.optimization_barrier(
+        (grad_tokens, up_grad, down_a, out_grad, down_b)
+    )
+    up_weight_grad = reduce_axis(up_grad, "head").astype(bf16).reshape(n_rest, w_rows, -1)
     up_weight_grad = exchange_axis(up_weight_grad, "rest").astype(f32)
     up_weight_grad = up_weight_grad.reshape(n_rest, w_rows, 2, chips, f_rows).transpose(1, 3, 0, 2, 4)
     up_weight_grad = up_weight_grad.reshape(w_rows, -1)
-    down_a, down_b, out_weight_grad = (reduce_axis(x, "head") for x in by_v)
+    down_a, out_weight_grad = (reduce_axis(x, "head") for x in (down_a, out_grad))
+    down_b = reduce_axis(down_b, "v")
     down_weight_grad = jnp.concatenate([down_a, down_b], axis=0)
     size = width // n_all
     out_bias_grad, post_gain_grad, post_shift_grad, down_bias_grad = (

time: 606 us -> 567 us (0.936)
  waiting for transfers between devices: 219 us -> 180 us
  blocking collectives: 0 us -> 34.1 us
  local copies, waits for them, and re-layouts: 77 us -> 55.9 us
  starting transfers between devices: 109 us -> 97.2 us
    ppermute x57, waiting for transfers between devices: 141 us -> 97.8 us  [shifted(): return lax.ppermute(x, axis, [(i, (i + k) % n) for i in range(n)])]
    all_to_all x0 -> x1, blocking collectives: none -> 34.1 us  [on_device(): lax.all_to_all(projected.reshape(hb, 3 * HEAD_DIM, block_rows), ('u', 'v'...]
    all_gather x1, waiting for transfers between devices: 0.01 us -> 24.7 us  [on_device(): joint = lax.all_gather(joint, ('head', 'u', 'v'), axis=0, tiled=True)]
    ppermute x3, waiting for transfers between devices: 33 us -> 11.1 us  [gather_line(): right.append(lax.ppermute(right[-1], axis, down))]
    all_to_all x1 -> x0, waiting for transfers between devices: 12.5 us -> none  [on_device(): lax.all_to_all(projected.reshape(hb, 3 * HEAD_DIM, block_rows), ('u', 'v'...]
    ppermute x57, starting transfers between devices: 71.2 us -> 61.1 us  [shifted(): return lax.ppermute(x, axis, [(i, (i + k) % n) for i in range(n)])]
    all_to_all x1, waiting for transfers between devices: 8.4 us -> 18.2 us  [on_device(): lax.all_to_all(attended.reshape(HEADS, HEAD_DIM, tok_rows), ('head', 'u',...]
    all_to_all x1, waiting for transfers between devices: 4.26 us -> 12.4 us  [on_device(): lax.all_to_all(jnp.concatenate([dq, dkv], axis=1), ('u', 'v'), split_axis...]
  transfers between devices with their start and end apart: 68 -> 67, of which waited for: 28 -> 27; matrix products, arithmetic and copies ran while one was open for 22% -> 18% of each run, Pallas kernels for 6% -> 15%
where the time goes in v3:
time: 567 us; the launch traced here: 558 us
  waiting for transfers between devices  180 us (32%)
  starting transfers between devices  97.2 us (17%)
  Pallas kernels  84.9 us (15%)
  local copies, waits for them, and re-layouts  55.9 us (10%)
  matrix products  48.4 us (9%)
  other arithmetic  41.9 us (7%)
  blocking collectives  34.1 us (6%)
  between operations  15.8 us (3%)
    ppermute x57, waiting for transfers between devices, shifted(): return lax.ppermute(x, axis, [(i, (i + k) % n) for i in range(n)])  97.8 us
    ppermute x57, starting transfers between devices, shifted(): return lax.ppermute(x, axis, [(i, (i + k) % n) for i in range(n)])  61.1 us
    pallas_call x1, Pallas kernels, attention_backward(): pl.pallas_call(functools.partial(backward_kernel, n_steps), grid_spec=plt...  48.5 us
    pallas_call x1, Pallas kernels, attention_forward(): pl.pallas_call(forward_kernel, grid_spec=pltpu.PrefetchScalarGridSpec(num...  36.4 us
    all_to_all x1, blocking collectives, on_device(): lax.all_to_all(projected.reshape(hb, 3 * HEAD_DIM, block_rows), ('u', 'v'...  34.1 us
    all_gather x1, waiting for transfers between devices, on_device(): joint = lax.all_gather(joint, ('head', 'u', 'v'), axis=0, tiled=True)  24.7 us
    all_to_all x1, waiting for transfers between devices, on_device(): lax.all_to_all(attended.reshape(HEADS, HEAD_DIM, tok_rows), ('head', 'u',...  18.2 us
    ppermute x3, starting transfers between devices, gather_line(): left.append(lax.ppermute(left[-1], axis, up))  13.6 us
  transfers between devices with their start and end apart: 67, of which 27 were waited for; matrix products, arithmetic and copies ran while one was open for 18% of the time, Pallas kernels for 15%

profile of v3, /device:TPU:0, one launch (start us, length us, event | category | flops | bytes accessed | tf_op | source)
XLA Modules:
  0.0 557.9 jit_solution(5148463812085508729)
XLA Ops:
  7.2 5.7 %collective-permute-start.6 = (bf16[256,1024]{1,0:T(8,128)(2,1)}, bf16[256,1024]{1,0:T(8,128)(2,1)}, u32[]{:S(2)}, u32[]{:S(2)}) collective-permute-start(bf16[256,1024]{1,0:T(8,128)(2,1)} %param.16), channel_id=1, source_target_pairs={{0,8},{8,16},{16,24},{1,9},{9,17},{17,25},{2,10},{10,18},{18,26},{... | collective-permute-start | bytes 1572872 | tf_op jit(solution)/shard_map/ppermute | solution.py:87
  14.3 6.1 %concatenate.28 = bf16[384]{0:T(512)(128)(2,1)S(1)} concatenate(bf16[32]{0:T(256)(128)(2,1)} %param.19, bf16[32]{0:T(256)(128)(2,1)} %param.20, bf16[32]{0:T(256)(128)(2,1)} %param.22, bf16[32]{0:T(256)(128)(2,1)} %param.23, bf16[32]{0:T(256)(128)(2,1)} %param.25, bf16[32]{0:T(256)(128)(2,1)} %param.26, bf16[32]{0:T(256)(128)(2,1)} %param.27, bf16[32]{0:T(256)(128)(2,1)} %param.31, ...), dimensions={0} | concatenate | bytes 1536 | tf_op jit(solution)/shard_map/concatenate | solution.py:411
  23.7 2.6 collective-permute-start
  39.0 4.6 collective-permute-done.13
  44.4 3.7 collective-permute-done.14
  48.6 3.1 collective-permute-done.15
  61.6 3.3 collective-permute-start.10
  66.9 8.4 %collective-permute-done.10 = bf16[256,1024]{1,0:T(8,128)(2,1)S(1)} collective-permute-done((bf16[256,1024]{1,0:T(8,128)(2,1)}, bf16[256,1024]{1,0:T(8,128)(2,1)S(1)}, u32[]{:S(2)}, u32[]{:S(2)}) %collective-permute-start.10) | collective-permute-done | bytes 524320 | tf_op jit(solution)/shard_map/ppermute | solution.py:87
  75.3 4.0 collective-permute-done.11
  80.6 4.6 collective-permute-start.17
  86.7 7.1 %collective-permute-done.16 = bf16[256,1024]{1,0:T(8,128)(2,1)S(1)} collective-permute-done((bf16[256,1024]{1,0:T(8,128)(2,1)S(1)}, bf16[256,1024]{1,0:T(8,128)(2,1)S(1)}, u32[]{:S(2)}, u32[]{:S(2)}) %collective-permute-start.16) | collective-permute-done | bytes 524320 | tf_op jit(solution)/shard_map/ppermute | solution.py:88
  96.4 2.6 bitcast_convert_fusion
  101.7 6.9 %collective-permute-done.4 = bf16[2,4,32,768]{3,2,0,1:T(8,128)(2,1)S(1)} collective-permute-done((bf16[2,4,32,768]{3,2,0,1:T(8,128)(2,1)S(1)}, bf16[2,4,32,768]{3,2,0,1:T(8,128)(2,1)S(1)}, u32[]{:S(2)}, u32[]{:S(2)}) %collective-permute-start.4) | collective-permute-done | bytes 393248 | tf_op jit(solution)/shard_map/ppermute | solution.py:57
  112.6 2.4 reduce_sum.183
  115.1 2.9 multiply_reduce_fusion.1
  119.0 4.5 add_convert_fusion.2
  123.5 34.1 %all_to_all.20.q_ref.own_ref = bf16[4,192,1024]{2,1,0:T(8,128)(2,1)S(1)} all-to-all(bf16[4,192,1024]{2,1,0:T(8,128)(2,1)S(1)} %bitcast.371), channel_id=1, replica_groups=mesh['head'=4,'u'=2,'v'=2,'rest'=2] {'u','v'}, dimensions={0} | all-to-all | bytes 3145728 | tf_op jit(solution)/shard_map/all_to_all | solution.py:459
  162.4 36.4 %attention_forward.1 = (bf16[4,4,64,256]{3,2,1,0:T(8,128)(2,1)}, f32[4,64,1024]{2,1,0:T(8,128)}, f32[4,1,1024]{2,1,0:T(1,128)}) custom-call(s32[8]{0:T(128)} %get-tuple-element.192.lo_ref, s32[8]{0:T(128)} %get-tuple-element.191.mid_ref, s32[8]{0:T(128)} %add.650.q0_ref, s32[1]{0:T(128)} %bitcast.me_ref, bf16[4,192,1024]{2,1,0:T(8,128)(2,1)} %copy-done.20, ...), custom_call_target="tpu_custom_call" | custom-call | flops 17179869184 | bytes 4194304 | tf_op jit(solution)/shard_map/attention_forward/pallas_call | solution.py:310
  198.8 8.8 %all-to-all-start.1 = ((bf16[16,64,256]{2,1,0:T(8,128)(2,1)}), bf16[16,64,256]{2,1,0:T(8,128)(2,1)S(1)}, u32[]{:S(2)}, u32[]{:S(2)}) async-start(bf16[16,64,256]{2,1,0:T(8,128)(2,1)} %bitcast.378), calls=%async_computation.1 | async-start | bytes 1048576 | tf_op jit(solution)/shard_map/all_to_all | solution.py:479
  212.4 18.2 %all-to-all-done.1 = bf16[16,64,256]{2,1,0:T(8,128)(2,1)S(1)} async-done(((bf16[16,64,256]{2,1,0:T(8,128)(2,1)}), bf16[16,64,256]{2,1,0:T(8,128)(2,1)S(1)}, u32[]{:S(2)}, u32[]{:S(2)}) %all-to-all-start.1) | async-done | bytes 524320 | tf_op jit(solution)/shard_map/all_to_all | solution.py:479
  230.6 24.7 %all-gather.2.cloned.1.call-done = bf16[1024,5120]{1,0:T(8,128)(2,1)} async-done(((bf16[64,5120]{1,0:T(8,128)(2,1)}), bf16[1024,5120]{1,0:T(8,128)(2,1)}) %all-gather.2.cloned.1.call-update) | async-done | bytes 10485776 | tf_op jit(solution)/shard_map/all_gather | solution.py:432
  255.3 2.4 fusion.90
  258.5 3.3 fusion.17
  263.1 2.5 fusion.21
  265.6 6.2 %convert_reduce_fusion = (f32[2048]{0:T(1024)S(1)}, bf16[512,2048]{1,0:T(8,128)(2,1)S(1)}, bf16[512,2048]{1,0:T(8,128)(2,1)S(1)}) fusion(f32[2048]{0:T(1024)S(1)} %add.694, f32[512,1024]{1,0:T(8,128)S(1)} %fusion.17, f32[512,1024]{1,0:T(8,128)S(1)} %fusion.21, bf16[512,1024]{1,0:T(8,128)(2,1)S(1)} %bitcast.374, bf16[1024,5120]{1,0:T(8,128)(2,1)S(1)} %copy-done.31), kind=kOutput, calls=%fused_computation.14 | convolution fusion | flops 2173696000 | bytes 13647872 | tf_op jit(solution)/shard_map/dot_general | solution.py:492
  271.9 2.4 fusion.9
  277.6 4.4 convolution_convert_fusion
  282.0 3.9 convolution_convert_fusion.3
  291.4 5.2 all-to-all-start.2
  297.5 4.3 convolution_convert_fusion.1
  306.0 6.2 %all-to-all-done.2 = bf16[16,64,256]{2,1,0:T(8,128)(2,1)} async-done(((bf16[16,64,256]{2,1,0:T(8,128)(2,1)}), bf16[16,64,256]{2,1,0:T(8,128)(2,1)}, u32[]{:S(2)}, u32[]{:S(2)}) %all-to-all-start.2) | async-done | bytes 524320 | tf_op jit(solution)/shard_map/all_to_all | solution.py:510
  312.9 4.2 dynamic-slice_bitcast_fusion
  329.0 48.5 %attention_backward.1 = (bf16[4,64,1024]{2,1,0:T(8,128)(2,1)}, bf16[2,4,128,1024]{3,2,1,0:T(8,128)(2,1)}) custom-call(s32[8]{0:T(128)} %get-tuple-element.192.lo_ref, s32[8]{0:T(128)} %get-tuple-element.191.mid_ref, s32[8]{0:T(128)} %add.650.q0_ref, s32[1]{0:T(128)} %bitcast.me_ref, bf16[4,192,1024]{2,1,0:T(8,128)(2,1)} %copy-done.20, ...), custom_call_target="tpu_custom_call" | custom-call | flops 42949672960 | bytes 4194304 | tf_op jit(solution)/shard_map/attention_backward/pallas_call | solution.py:348
  380.7 3.0 collective-permute-done.33
  386.9 4.5 all-to-all-start.3
  391.5 2.6 add_convert_fusion.4
  396.6 2.4 add_convert_fusion
  399.0 12.4 %all-to-all-done.3 = bf16[4,192,1024]{2,1,0:T(8,128)(2,1)} async-done(((bf16[4,192,1024]{2,1,0:T(8,128)(2,1)}), bf16[4,192,1024]{2,1,0:T(8,128)(2,1)}, u32[]{:S(2)}, u32[]{:S(2)}) %all-to-all-start.3) | async-done | bytes 1572896 | tf_op jit(solution)/shard_map/all_to_all | solution.py:544
  411.4 5.2 multiply_reduce_fusion
  416.5 2.4 convert_reduce_fusion.1
  419.0 4.5 convolution_convert_fusion.4
  434.0 4.2 collective-permute-done.52
  443.4 8.1 %collective-permute-done.53 = f32[2,256]{1,0:T(2,128)S(1)} collective-permute-done((f32[2,256]{1,0:T(2,128)S(1)}, f32[2,256]{1,0:T(2,128)S(1)}, u32[]{:S(2)}, u32[]{:S(2)}) %collective-permute-start.53) | collective-permute-done | bytes 2080 | tf_op jit(solution)/shard_map/ppermute | solution.py:57
  461.9 27.6 %collective-permute-done.35 = bf16[256,1024]{1,0:T(8,128)(2,1)S(1)} collective-permute-done((bf16[256,1024]{1,0:T(8,128)(2,1)S(1)}, bf16[256,1024]{1,0:T(8,128)(2,1)S(1)}, u32[]{:S(2)}, u32[]{:S(2)}) %collective-permute-start.35) | collective-permute-done | bytes 524320 | tf_op jit(solution)/shard_map/ppermute | solution.py:57
  502.8 8.2 %collective-permute-start.60 = (bf16[64,1024]{1,0:T(8,128)(2,1)S(1)}, bf16[64,1024]{1,0:T(8,128)(2,1)S(1)}, u32[]{:S(2)}, u32[]{:S(2)}) collective-permute-start(bf16[64,1024]{1,0:T(8,128)(2,1)S(1)} %get-tuple-element.150), channel_id=1, source_target_pairs={{0,16},{8,24},{16,0},{24,8},{1,17},{9,25},{17,1},{25,9},{2,18},{10... | collective-permute-start | bytes 393224 | tf_op jit(solution)/shard_map/ppermute | solution.py:57
  512.8 13.1 %collective-permute-done.60 = bf16[64,1024]{1,0:T(8,128)(2,1)S(1)} collective-permute-done((bf16[64,1024]{1,0:T(8,128)(2,1)S(1)}, bf16[64,1024]{1,0:T(8,128)(2,1)S(1)}, u32[]{:S(2)}, u32[]{:S(2)}) %collective-permute-start.60) | collective-permute-done | bytes 131104 | tf_op jit(solution)/shard_map/ppermute | solution.py:57
  528.9 8.2 %collective-permute-done.56 = bf16[64,2048]{1,0:T(8,128)(2,1)S(1)} collective-permute-done((bf16[64,2048]{1,0:T(8,128)(2,1)S(1)}, bf16[64,2048]{1,0:T(8,128)(2,1)S(1)}, u32[]{:S(2)}, u32[]{:S(2)}) %collective-permute-start.56) | collective-permute-done | bytes 262176 | tf_op jit(solution)/shard_map/ppermute | solution.py:57
  544.3 3.4 collective-permute-done.45
  (378 shorter events, 144.1 us)
Async XLA Ops:
  7.2 248.1 %all-gather.2.cloned.1.call-start = ((), (), s32[]{:S(2)}) async-start(), calls=%async_computation.4 | async-start | bytes 11141120 | tf_op jit(solution)/shard_map/all_gather | solution.py:432
  7.2 54.4 %collective-permute-start.6 = (bf16[256,1024]{1,0:T(8,128)(2,1)}, bf16[256,1024]{1,0:T(8,128)(2,1)}, u32[]{:S(2)}, u32[]{:S(2)}) collective-permute-start(bf16[256,1024]{1,0:T(8,128)(2,1)} %param.16), channel_id=1, source_target_pairs={{0,8},{8,16},{16,24},{1,9},{9,17},{17,25},{2,10},{10,18},{18,26},{... | collective-permute-start | bytes 1572872 | tf_op jit(solution)/shard_map/ppermute | solution.py:87
  13.0 48.6 %collective-permute-start.7 = (bf16[256,1024]{1,0:T(8,128)(2,1)}, bf16[256,1024]{1,0:T(8,128)(2,1)}, u32[]{:S(2)}, u32[]{:S(2)}) collective-permute-start(bf16[256,1024]{1,0:T(8,128)(2,1)} %param.16), channel_id=1, source_target_pairs={{8,0},{16,8},{24,16},{9,1},{17,9},{25,17},{10,2},{18,10},{26,18},{... | collective-permute-start | bytes 1572872 | tf_op jit(solution)/shard_map/ppermute | solution.py:88
  20.4 10.5 %collective-permute-start.8 = (bf16[1,384]{1,0:T(2,128)(2,1)S(1)}, bf16[1,384]{1,0:T(2,128)(2,1)S(1)}, u32[]{:S(2)}, u32[]{:S(2)}) collective-permute-start(bf16[1,384]{1,0:T(2,128)(2,1)S(1)} %reshape.398), channel_id=1, source_target_pairs={{0,1},{1,0},{2,3},{3,2},{4,5},{5,4},{6,7},{7,6},{8,9},{9,8},{10,11... | collective-permute-start | bytes 2312 | tf_op jit(solution)/shard_map/ppermute | solution.py:57
  23.7 28.8 %collective-permute-start = (bf16[32,768]{1,0:T(8,128)(2,1)}, bf16[32,768]{1,0:T(8,128)(2,1)}, u32[]{:S(2)}, u32[]{:S(2)}) collective-permute-start(bf16[32,768]{1,0:T(8,128)(2,1)} %get-tuple-element.167), channel_id=1, source_target_pairs={{0,8},{8,16},{16,24},{24,0},{1,9},{9,17},{17,25},{25,1},{2,10},{10... | collective-permute-start | bytes 147464 | tf_op jit(solution)/shard_map/ppermute | solution.py:57
  26.3 34.4 %collective-permute-start.19 = (bf16[32,1024]{1,0:T(8,128)(2,1)}, bf16[32,1024]{1,0:T(8,128)(2,1)}, u32[]{:S(2)}, u32[]{:S(2)}) collective-permute-start(bf16[32,1024]{1,0:T(8,128)(2,1)} %param.24), channel_id=1, source_target_pairs={{0,1},{1,0},{2,3},{3,2},{4,5},{5,4},{6,7},{7,6},{8,9},{9,8},{10,11... | collective-permute-start | bytes 196616 | tf_op jit(solution)/shard_map/ppermute | solution.py:57
  57.0 9.3 %collective-permute-start.18 = (bf16[32,2048]{1,0:T(8,128)(2,1)S(1)}, bf16[32,2048]{1,0:T(8,128)(2,1)S(1)}, u32[]{:S(2)}, u32[]{:S(2)}) collective-permute-start(bf16[32,2048]{1,0:T(8,128)(2,1)S(1)} %get-tuple-element.159), channel_id=1, source_target_pairs={{0,1},{1,0},{2,3},{3,2},{4,5},{5,4},{6,7},{7,6},{8,9},{9,8},{10,11... | collective-permute-start | bytes 393224 | tf_op jit(solution)/shard_map/ppermute | solution.py:57
  58.2 8.7 %collective-permute-start.3 = (bf16[4,32,768]{2,1,0:T(8,128)(2,1)}, bf16[4,32,768]{2,1,0:T(8,128)(2,1)S(1)}, u32[]{:S(2)}, u32[]{:S(2)}) collective-permute-start(bf16[4,32,768]{2,1,0:T(8,128)(2,1)} %bitcast_dynamic-update-slice_fusion.21), channel_id=1, source_target_pairs={{0,2},{2,0},{1,3},{3,1},{4,6},{6,4},{5,7},{7,5},{8,10},{10,8},{9,1... | collective-permute-start | bytes 589832 | tf_op jit(solution)/shard_map/ppermute | solution.py:57
  61.6 13.7 %collective-permute-start.10 = (bf16[256,1024]{1,0:T(8,128)(2,1)}, bf16[256,1024]{1,0:T(8,128)(2,1)S(1)}, u32[]{:S(2)}, u32[]{:S(2)}) collective-permute-start(bf16[256,1024]{1,0:T(8,128)(2,1)} %collective-permute-done.6), channel_id=1, source_target_pairs={{0,8},{8,16},{16,24},{1,9},{9,17},{17,25},{2,10},{10,18},{18,26},{... | collective-permute-start | bytes 1572872 | tf_op jit(solution)/shard_map/ppermute | solution.py:87
  64.9 14.4 %collective-permute-start.11 = (bf16[256,1024]{1,0:T(8,128)(2,1)}, bf16[256,1024]{1,0:T(8,128)(2,1)S(1)}, u32[]{:S(2)}, u32[]{:S(2)}) collective-permute-start(bf16[256,1024]{1,0:T(8,128)(2,1)} %collective-permute-done.7), channel_id=1, source_target_pairs={{8,0},{16,8},{24,16},{9,1},{17,9},{25,17},{10,2},{18,10},{26,18},{... | collective-permute-start | bytes 1572872 | tf_op jit(solution)/shard_map/ppermute | solution.py:88
  79.3 14.4 %collective-permute-start.16 = (bf16[256,1024]{1,0:T(8,128)(2,1)S(1)}, bf16[256,1024]{1,0:T(8,128)(2,1)S(1)}, u32[]{:S(2)}, u32[]{:S(2)}) collective-permute-start(bf16[256,1024]{1,0:T(8,128)(2,1)S(1)} %collective-permute-done.11), channel_id=1, source_target_pairs={{8,0},{16,8},{24,16},{9,1},{17,9},{25,17},{10,2},{18,10},{26,18},{... | collective-permute-start | bytes 1572872 | tf_op jit(solution)/shard_map/ppermute | solution.py:88
  80.6 14.3 %collective-permute-start.17 = (bf16[256,1024]{1,0:T(8,128)(2,1)S(1)}, bf16[256,1024]{1,0:T(8,128)(2,1)S(1)}, u32[]{:S(2)}, u32[]{:S(2)}) collective-permute-start(bf16[256,1024]{1,0:T(8,128)(2,1)S(1)} %collective-permute-done.10), channel_id=1, source_target_pairs={{0,8},{8,16},{16,24},{1,9},{9,17},{17,25},{2,10},{10,18},{18,26},{... | collective-permute-start | bytes 1572872 | tf_op jit(solution)/shard_map/ppermute | solution.py:87
  100.0 8.6 %collective-permute-start.4 = (bf16[2,4,32,768]{3,2,0,1:T(8,128)(2,1)S(1)}, bf16[2,4,32,768]{3,2,0,1:T(8,128)(2,1)S(1)}, u32[]{:S(2)}, u32[]{:S(2)}) collective-permute-start(bf16[2,4,32,768]{3,2,0,1:T(8,128)(2,1)S(1)} %bitcast_dynamic-update-slice_fusion.13), channel_id=1, source_target_pairs={{0,4},{4,0},{1,5},{5,1},{2,6},{6,2},{3,7},{7,3},{8,12},{12,8},{9,1... | collective-permute-start | bytes 1179656 | tf_op jit(solution)/shard_map/ppermute | solution.py:57
  198.8 31.9 %all-to-all-start.1 = ((bf16[16,64,256]{2,1,0:T(8,128)(2,1)}), bf16[16,64,256]{2,1,0:T(8,128)(2,1)S(1)}, u32[]{:S(2)}, u32[]{:S(2)}) async-start(bf16[16,64,256]{2,1,0:T(8,128)(2,1)} %bitcast.378), calls=%async_computation.1 | async-start | bytes 1048576 | tf_op jit(solution)/shard_map/all_to_all | solution.py:479
  258.4 7.2 %collective-permute-start.21 = (bf16[256,1024]{1,0:T(8,128)(2,1)S(1)}, bf16[256,1024]{1,0:T(8,128)(2,1)S(1)}, u32[]{:S(2)}, u32[]{:S(2)}) collective-permute-start(bf16[256,1024]{1,0:T(8,128)(2,1)S(1)} %get-tuple-element.124), channel_id=1, source_target_pairs={{0,1},{1,0},{2,3},{3,2},{4,5},{5,4},{6,7},{7,6},{8,9},{9,8},{10,11... | collective-permute-start | bytes 1572872 | tf_op jit(solution)/shard_map/ppermute | solution.py:57
  274.4 11.6 %collective-permute-start.24 = (f32[256,1024]{1,0:T(8,128)S(1)}, f32[256,1024]{1,0:T(8,128)S(1)}, u32[]{:S(2)}, u32[]{:S(2)}) collective-permute-start(f32[256,1024]{1,0:T(8,128)S(1)} %dynamic-slice_bitcast_fusion.5), channel_id=1, source_target_pairs={{0,1},{1,0},{2,3},{3,2},{4,5},{5,4},{6,7},{7,6},{8,9},{9,8},{10,11... | collective-permute-start | bytes 3145736 | tf_op jit(solution)/shard_map/ppermute | solution.py:57
  277.1 9.5 %collective-permute-start.22 = (f32[256,1024]{1,0:T(8,128)S(1)}, f32[256,1024]{1,0:T(8,128)S(1)}, u32[]{:S(2)}, u32[]{:S(2)}) collective-permute-start(f32[256,1024]{1,0:T(8,128)S(1)} %dynamic-slice_bitcast_fusion.6), channel_id=1, source_target_pairs={{0,1},{1,0},{2,3},{3,2},{4,5},{5,4},{6,7},{7,6},{8,9},{9,8},{10,11... | collective-permute-start | bytes 3145736 | tf_op jit(solution)/shard_map/ppermute | solution.py:57
  289.9 14.4 %collective-permute-start.25 = (bf16[16,32,1024]{2,1,0:T(8,128)(2,1)}, bf16[16,32,1024]{2,1,0:T(8,128)(2,1)}, u32[]{:S(2)}, u32[]{:S(2)}) collective-permute-start(bf16[16,32,1024]{2,1,0:T(8,128)(2,1)} %dynamic-slice_bitcast_fusion.4), channel_id=1, source_target_pairs={{0,1},{1,0},{2,3},{3,2},{4,5},{5,4},{6,7},{7,6},{8,9},{9,8},{10,11... | collective-permute-start | bytes 3145736 | tf_op jit(solution)/shard_map/ppermute | solution.py:57
  291.4 20.8 %all-to-all-start.2 = ((bf16[16,64,256]{2,1,0:T(8,128)(2,1)}), bf16[16,64,256]{2,1,0:T(8,128)(2,1)}, u32[]{:S(2)}, u32[]{:S(2)}) async-start(bf16[16,64,256]{2,1,0:T(8,128)(2,1)} %bitcast.379), calls=%async_computation.2 | async-start | bytes 1048576 | tf_op jit(solution)/shard_map/all_to_all | solution.py:510
  312.3 14.9 %collective-permute-start.29 = (bf16[2,4,32,1024]{3,2,1,0:T(8,128)(2,1)S(1)}, bf16[2,4,32,1024]{3,2,1,0:T(8,128)(2,1)S(1)}, u32[]{:S(2)}, u32[]{:S(2)}) collective-permute-start(bf16[2,4,32,1024]{3,2,1,0:T(8,128)(2,1)S(1)} %get-tuple-element.145), channel_id=1, source_target_pairs={{0,2},{2,0},{1,3},{3,1},{4,6},{6,4},{5,7},{7,5},{8,10},{10,8},{9,1... | collective-permute-start | bytes 1572872 | tf_op jit(solution)/shard_map/ppermute | solution.py:57
  317.1 60.7 %collective-permute-start.27 = (bf16[2,4,64,2048]{3,2,1,0:T(8,128)(2,1)S(1)}, bf16[2,4,64,2048]{3,2,1,0:T(8,128)(2,1)}, u32[]{:S(2)}, u32[]{:S(2)}) collective-permute-start(bf16[2,4,64,2048]{3,2,1,0:T(8,128)(2,1)S(1)} %get-tuple-element.129), channel_id=1, source_target_pairs={{0,4},{4,0},{1,5},{5,1},{2,6},{6,2},{3,7},{7,3},{8,12},{12,8},{9,1... | collective-permute-start | bytes 6291464 | tf_op jit(solution)/shard_map/ppermute | solution.py:57
  319.6 58.1 %collective-permute-start.28 = (bf16[2,4,64,1024]{3,2,1,0:T(8,128)(2,1)}, bf16[2,4,64,1024]{3,2,1,0:T(8,128)(2,1)S(1)}, u32[]{:S(2)}, u32[]{:S(2)}) collective-permute-start(bf16[2,4,64,1024]{3,2,1,0:T(8,128)(2,1)} %bitcast.336), channel_id=1, source_target_pairs={{0,2},{2,0},{1,3},{3,1},{4,6},{6,4},{5,7},{7,5},{8,10},{10,8},{9,1... | collective-permute-start | bytes 3145736 | tf_op jit(solution)/shard_map/ppermute | solution.py:57
  322.3 55.4 %collective-permute-start.30 = (bf16[2,2,64,1024]{3,2,1,0:T(8,128)(2,1)}, bf16[2,2,64,1024]{3,2,1,0:T(8,128)(2,1)}, u32[]{:S(2)}, u32[]{:S(2)}) collective-permute-start(bf16[2,2,64,1024]{3,2,1,0:T(8,128)(2,1)} %get-tuple-element.136), channel_id=1, source_target_pairs={{0,8},{8,16},{16,24},{24,0},{1,9},{9,17},{17,25},{25,1},{2,10},{10... | collective-permute-start | bytes 1572872 | tf_op jit(solution)/shard_map/ppermute | solution.py:57
  323.5 54.2 %collective-permute-start.31 = (bf16[2,2,64,1024]{3,2,1,0:T(8,128)(2,1)}, bf16[2,2,64,1024]{3,2,1,0:T(8,128)(2,1)}, u32[]{:S(2)}, u32[]{:S(2)}) collective-permute-start(bf16[2,2,64,1024]{3,2,1,0:T(8,128)(2,1)} %get-tuple-element.135), channel_id=1, source_target_pairs={{0,16},{8,24},{16,0},{24,8},{1,17},{9,25},{17,1},{25,9},{2,18},{10... | collective-permute-start | bytes 1572872 | tf_op jit(solution)/shard_map/ppermute | solution.py:57
  327.2 50.5 %collective-permute-start.32 = (bf16[2,2,64,1024]{3,2,1,0:T(8,128)(2,1)}, bf16[2,2,64,1024]{3,2,1,0:T(8,128)(2,1)}, u32[]{:S(2)}, u32[]{:S(2)}) collective-permute-start(bf16[2,2,64,1024]{3,2,1,0:T(8,128)(2,1)} %get-tuple-element.134), channel_id=1, source_target_pairs={{0,24},{8,0},{16,8},{24,16},{1,25},{9,1},{17,9},{25,17},{2,26},{10... | collective-permute-start | bytes 1572872 | tf_op jit(solution)/shard_map/ppermute | solution.py:57
  386.9 24.4 %all-to-all-start.3 = ((bf16[4,192,1024]{2,1,0:T(8,128)(2,1)}), bf16[4,192,1024]{2,1,0:T(8,128)(2,1)}, u32[]{:S(2)}, u32[]{:S(2)}) async-start(bf16[4,192,1024]{2,1,0:T(8,128)(2,1)} %pad_maximum_fusion), calls=%async_computation.3 | async-start | bytes 3145728 | tf_op jit(solution)/shard_map/all_to_all | solution.py:544
  424.6 37.2 %collective-permute-start.36 = (bf16[256,1024]{1,0:T(8,128)(2,1)}, bf16[256,1024]{1,0:T(8,128)(2,1)}, u32[]{:S(2)}, u32[]{:S(2)}) collective-permute-start(bf16[256,1024]{1,0:T(8,128)(2,1)} %get-tuple-element.132), channel_id=1, source_target_pairs={{0,24},{8,0},{16,8},{24,16},{1,25},{9,1},{17,9},{25,17},{2,26},{10... | collective-permute-start | bytes 1572872 | tf_op jit(solution)/shard_map/ppermute | solution.py:57
  427.2 31.9 %collective-permute-start.38 = (bf16[4,64,1024]{2,1,0:T(8,128)(2,1)}, bf16[4,64,1024]{2,1,0:T(8,128)(2,1)}, u32[]{:S(2)}, u32[]{:S(2)}) collective-permute-start(bf16[4,64,1024]{2,1,0:T(8,128)(2,1)} %dynamic-slice_bitcast_fusion.7), channel_id=1, source_target_pairs={{0,4},{4,0},{1,5},{5,1},{2,6},{6,2},{3,7},{7,3},{8,12},{12,8},{9,1... | collective-permute-start | bytes 1572872 | tf_op jit(solution)/shard_map/ppermute | solution.py:57
  430.5 7.7 %collective-permute-start.52 = (f32[2,2,256]{2,1,0:T(2,128)S(1)}, f32[2,2,256]{2,1,0:T(2,128)S(1)}, u32[]{:S(2)}, u32[]{:S(2)}) collective-permute-start(f32[2,2,256]{2,1,0:T(2,128)S(1)} %get-tuple-element.178), channel_id=1, source_target_pairs={{0,24},{8,0},{16,8},{24,16},{1,25},{9,1},{17,9},{25,17},{2,26},{10... | collective-permute-start | bytes 12296 | tf_op jit(solution)/shard_map/ppermute | solution.py:57
  432.6 7.2 %collective-permute-start.51 = (f32[2,2,256]{2,1,0:T(2,128)S(1)}, f32[2,2,256]{2,1,0:T(2,128)S(1)}, u32[]{:S(2)}, u32[]{:S(2)}) collective-permute-start(f32[2,2,256]{2,1,0:T(2,128)S(1)} %get-tuple-element.179), channel_id=1, source_target_pairs={{0,16},{8,24},{16,0},{24,8},{1,17},{9,25},{17,1},{25,9},{2,18},{10... | collective-permute-start | bytes 12296 | tf_op jit(solution)/shard_map/ppermute | solution.py:57
  438.3 19.1 %collective-permute-start.39 = (bf16[4,32,1024]{2,1,0:T(8,128)(2,1)}, bf16[4,32,1024]{2,1,0:T(8,128)(2,1)S(1)}, u32[]{:S(2)}, u32[]{:S(2)}) collective-permute-start(bf16[4,32,1024]{2,1,0:T(8,128)(2,1)} %dynamic-slice_bitcast_fusion.22), channel_id=1, source_target_pairs={{0,4},{4,0},{1,5},{5,1},{2,6},{6,2},{3,7},{7,3},{8,12},{12,8},{9,1... | collective-permute-start | bytes 786440 | tf_op jit(solution)/shard_map/ppermute | solution.py:57
  439.7 19.2 %collective-permute-start.40 = (bf16[2,64,1024]{2,1,0:T(8,128)(2,1)}, bf16[2,64,1024]{2,1,0:T(8,128)(2,1)S(1)}, u32[]{:S(2)}, u32[]{:S(2)}) collective-permute-start(bf16[2,64,1024]{2,1,0:T(8,128)(2,1)} %dynamic-slice_bitcast_fusion.21), channel_id=1, source_target_pairs={{0,4},{4,0},{1,5},{5,1},{2,6},{6,2},{3,7},{7,3},{8,12},{12,8},{9,1... | collective-permute-start | bytes 786440 | tf_op jit(solution)/shard_map/ppermute | solution.py:57
  440.3 11.2 %collective-permute-start.53 = (f32[2,256]{1,0:T(2,128)S(1)}, f32[2,256]{1,0:T(2,128)S(1)}, u32[]{:S(2)}, u32[]{:S(2)}) collective-permute-start(f32[2,256]{1,0:T(2,128)S(1)} %fusion.84), channel_id=1, source_target_pairs={{0,4},{4,0},{1,5},{5,1},{2,6},{6,2},{3,7},{7,3},{8,12},{12,8},{9,1... | collective-permute-start | bytes 6152 | tf_op jit(solution)/shard_map/ppermute | solution.py:57
  455.2 34.3 %collective-permute-start.35 = (bf16[256,1024]{1,0:T(8,128)(2,1)S(1)}, bf16[256,1024]{1,0:T(8,128)(2,1)S(1)}, u32[]{:S(2)}, u32[]{:S(2)}) collective-permute-start(bf16[256,1024]{1,0:T(8,128)(2,1)S(1)} %copy-done.27), channel_id=1, source_target_pairs={{0,16},{8,24},{16,0},{24,8},{1,17},{9,25},{17,1},{25,9},{2,18},{10... | collective-permute-start | bytes 1572872 | tf_op jit(solution)/shard_map/ppermute | solution.py:57
  457.3 32.2 %collective-permute-start.34 = (bf16[256,1024]{1,0:T(8,128)(2,1)S(1)}, bf16[256,1024]{1,0:T(8,128)(2,1)S(1)}, u32[]{:S(2)}, u32[]{:S(2)}) collective-permute-start(bf16[256,1024]{1,0:T(8,128)(2,1)S(1)} %copy-done.26), channel_id=1, source_target_pairs={{0,8},{8,16},{16,24},{24,0},{1,9},{9,17},{17,25},{25,1},{2,10},{10... | collective-permute-start | bytes 1572872 | tf_op jit(solution)/shard_map/ppermute | solution.py:57
  458.9 32.1 %collective-permute-start.41 = (bf16[4,4,32,896]{3,2,1,0:T(8,128)(2,1)S(1)}, bf16[4,4,32,896]{3,2,1,0:T(8,128)(2,1)S(1)}, u32[]{:S(2)}, u32[]{:S(2)}) collective-permute-start(bf16[4,4,32,896]{3,2,1,0:T(8,128)(2,1)S(1)} %bitcast.376), channel_id=1, source_target_pairs={{0,1},{1,0},{2,3},{3,2},{4,5},{5,4},{6,7},{7,6},{8,9},{9,8},{10,11... | collective-permute-start | bytes 2752520 | tf_op jit(solution)/shard_map/ppermute | solution.py:57
  459.0 33.8 %collective-permute-start.37 = (bf16[4,64,2048]{2,1,0:T(8,128)(2,1)S(1)}, bf16[4,64,2048]{2,1,0:T(8,128)(2,1)S(1)}, u32[]{:S(2)}, u32[]{:S(2)}) collective-permute-start(bf16[4,64,2048]{2,1,0:T(8,128)(2,1)S(1)} %copy-done.23), channel_id=1, source_target_pairs={{0,2},{2,0},{1,3},{3,1},{4,6},{6,4},{5,7},{7,5},{8,10},{10,8},{9,1... | collective-permute-start | bytes 3145736 | tf_op jit(solution)/shard_map/ppermute | solution.py:57
  491.4 35.7 %collective-permute-start.42 = (bf16[2,4,32,896]{3,2,1,0:T(8,128)(2,1)S(1)}, bf16[2,4,32,896]{3,2,1,0:T(8,128)(2,1)S(1)}, u32[]{:S(2)}, u32[]{:S(2)}) collective-permute-start(bf16[2,4,32,896]{3,2,1,0:T(8,128)(2,1)S(1)} %dynamic-slice_bitcast_fusion.17), channel_id=1, source_target_pairs={{0,4},{4,0},{1,5},{5,1},{2,6},{6,2},{3,7},{7,3},{8,12},{12,8},{9,1... | collective-permute-start | bytes 1376264 | tf_op jit(solution)/shard_map/ppermute | solution.py:57
  493.7 8.0 %collective-permute-start.48 = (bf16[32,1024]{1,0:T(8,128)(2,1)S(1)}, bf16[32,1024]{1,0:T(8,128)(2,1)S(1)}, u32[]{:S(2)}, u32[]{:S(2)}) collective-permute-start(bf16[32,1024]{1,0:T(8,128)(2,1)S(1)} %get-tuple-element.156), channel_id=1, source_target_pairs={{0,16},{8,24},{16,0},{24,8},{1,17},{9,25},{17,1},{25,9},{2,18},{10... | collective-permute-start | bytes 196616 | tf_op jit(solution)/shard_map/ppermute | solution.py:57
  494.4 8.4 %collective-permute-start.47 = (bf16[32,1024]{1,0:T(8,128)(2,1)S(1)}, bf16[32,1024]{1,0:T(8,128)(2,1)S(1)}, u32[]{:S(2)}, u32[]{:S(2)}) collective-permute-start(bf16[32,1024]{1,0:T(8,128)(2,1)S(1)} %get-tuple-element.154), channel_id=1, source_target_pairs={{0,8},{8,16},{16,24},{24,0},{1,9},{9,17},{17,25},{25,1},{2,10},{10... | collective-permute-start | bytes 196616 | tf_op jit(solution)/shard_map/ppermute | solution.py:57
  496.4 32.4 %collective-permute-start.57 = (bf16[64,2048]{1,0:T(8,128)(2,1)S(1)}, bf16[64,2048]{1,0:T(8,128)(2,1)S(1)}, u32[]{:S(2)}, u32[]{:S(2)}) collective-permute-start(bf16[64,2048]{1,0:T(8,128)(2,1)S(1)} %get-tuple-element.143), channel_id=1, source_target_pairs={{0,24},{8,0},{16,8},{24,16},{1,25},{9,1},{17,9},{25,17},{2,26},{10... | collective-permute-start | bytes 786440 | tf_op jit(solution)/shard_map/ppermute | solution.py:57
  499.5 12.2 %collective-permute-start.62 = (bf16[64,1024]{1,0:T(8,128)(2,1)S(1)}, bf16[64,1024]{1,0:T(8,128)(2,1)S(1)}, u32[]{:S(2)}, u32[]{:S(2)}) collective-permute-start(bf16[64,1024]{1,0:T(8,128)(2,1)S(1)} %dynamic-slice_bitcast_fusion.24), channel_id=1, source_target_pairs={{0,2},{2,0},{1,3},{3,1},{4,6},{6,4},{5,7},{7,5},{8,10},{10,8},{9,1... | collective-permute-start | bytes 393224 | tf_op jit(solution)/shard_map/ppermute | solution.py:57
  501.7 10.8 %collective-permute-start.61 = (bf16[64,1024]{1,0:T(8,128)(2,1)S(1)}, bf16[64,1024]{1,0:T(8,128)(2,1)S(1)}, u32[]{:S(2)}, u32[]{:S(2)}) collective-permute-start(bf16[64,1024]{1,0:T(8,128)(2,1)S(1)} %get-tuple-element.149), channel_id=1, source_target_pairs={{0,24},{8,0},{16,8},{24,16},{1,25},{9,1},{17,9},{25,17},{2,26},{10... | collective-permute-start | bytes 393224 | tf_op jit(solution)/shard_map/ppermute | solution.py:57
  502.8 23.2 %collective-permute-start.60 = (bf16[64,1024]{1,0:T(8,128)(2,1)S(1)}, bf16[64,1024]{1,0:T(8,128)(2,1)S(1)}, u32[]{:S(2)}, u32[]{:S(2)}) collective-permute-start(bf16[64,1024]{1,0:T(8,128)(2,1)S(1)} %get-tuple-element.150), channel_id=1, source_target_pairs={{0,16},{8,24},{16,0},{24,8},{1,17},{9,25},{17,1},{25,9},{2,18},{10... | collective-permute-start | bytes 393224 | tf_op jit(solution)/shard_map/ppermute | solution.py:57
  511.7 14.5 %collective-permute-start.59 = (bf16[64,1024]{1,0:T(8,128)(2,1)S(1)}, bf16[64,1024]{1,0:T(8,128)(2,1)S(1)}, u32[]{:S(2)}, u32[]{:S(2)}) collective-permute-start(bf16[64,1024]{1,0:T(8,128)(2,1)S(1)} %get-tuple-element.148), channel_id=1, source_target_pairs={{0,8},{8,16},{16,24},{24,0},{1,9},{9,17},{17,25},{25,1},{2,10},{10... | collective-permute-start | bytes 393224 | tf_op jit(solution)/shard_map/ppermute | solution.py:57
  512.5 24.6 %collective-permute-start.56 = (bf16[64,2048]{1,0:T(8,128)(2,1)S(1)}, bf16[64,2048]{1,0:T(8,128)(2,1)S(1)}, u32[]{:S(2)}, u32[]{:S(2)}) collective-permute-start(bf16[64,2048]{1,0:T(8,128)(2,1)S(1)} %get-tuple-element.144), channel_id=1, source_target_pairs={{0,16},{8,24},{16,0},{24,8},{1,17},{9,25},{17,1},{25,9},{2,18},{10... | collective-permute-start | bytes 786440 | tf_op jit(solution)/shard_map/ppermute | solution.py:57
  525.9 11.1 %collective-permute-start.55 = (bf16[64,2048]{1,0:T(8,128)(2,1)S(1)}, bf16[64,2048]{1,0:T(8,128)(2,1)S(1)}, u32[]{:S(2)}, u32[]{:S(2)}) collective-permute-start(bf16[64,2048]{1,0:T(8,128)(2,1)S(1)} %get-tuple-element.142), channel_id=1, source_target_pairs={{0,8},{8,16},{16,24},{24,0},{1,9},{9,17},{17,25},{25,1},{2,10},{10... | collective-permute-start | bytes 786440 | tf_op jit(solution)/shard_map/ppermute | solution.py:57
  527.2 10.1 %collective-permute-start.43 = (bf16[4,32,896]{2,1,0:T(8,128)(2,1)S(1)}, bf16[4,32,896]{2,1,0:T(8,128)(2,1)S(1)}, u32[]{:S(2)}, u32[]{:S(2)}) collective-permute-start(bf16[4,32,896]{2,1,0:T(8,128)(2,1)S(1)} %dynamic-slice_bitcast_fusion.23), channel_id=1, source_target_pairs={{0,2},{2,0},{1,3},{3,1},{4,6},{6,4},{5,7},{7,5},{8,10},{10,8},{9,1... | collective-permute-start | bytes 688136 | tf_op jit(solution)/shard_map/ppermute | solution.py:57
  (55 other events, 410.8 us)
Sparse Core Ops, SparseCore 0:
  100.1 155.1 all-gather.1

commit v4 on v3

--- a/solution.py
+++ b/solution.py
@@ -72,40 +72,12 @@
     return out
 
 
-def gather_line(x, axis, beside):
-    n = lax.axis_size(axis)
-    if n != 4:
-        for make in beside:
-            if make is not None:
-                make()
-        return gather_axis(x, axis)
-    me = lax.axis_index(axis)
-    up = [(i, i + 1) for i in range(n - 1)]
-    down = [(i + 1, i) for i in range(n - 1)]
-    left, right = [x], [x]
-    for i in range(n - 1):
-        left.append(lax.ppermute(left[-1], axis, up))
-        right.append(lax.ppermute(right[-1], axis, down))
-        if beside[i] is not None:
-            made = beside[i]()
-            left[-1], right[-1], _ = lax.optimization_barrier((left[-1], right[-1], made))
-    low = me < 2
-    first = jnp.where(low, right[1], left[1])
-    second = jnp.where(low, right[2], left[2])
-    inner = jnp.where(me == 1, left[1], right[1])
-    third = jnp.where(me == 0, right[3], jnp.where(me == 3, left[3], inner))
-    out = put(jnp.zeros((n,) + x.shape, x.dtype), x, me)
-    out = put(out, first, jnp.where(low, me + 1, me - 1))
-    out = put(out, second, jnp.where(low, me + 2, me - 2))
-    return put(out, third, jnp.where(me == 0, 3, jnp.where(me == 3, 0, jnp.where(me == 1, 0, 3))))
-
-
-def reduce_begin(x, axis):
+def reduce_begin(x, axis, dim=0):
     n = lax.axis_size(axis)
     if n == 1:
-        return [x[0]]
+        return [lax.index_in_dim(x, 0, dim, keepdims=False)]
     me = lax.axis_index(axis)
-    pieces = [lax.dynamic_index_in_dim(x, (me + k) % n, 0, keepdims=False) for k in range(n)]
+    pieces = [lax.dynamic_index_in_dim(x, (me + k) % n, dim, keepdims=False) for k in range(n)]
     return pieces[:1] + [shifted(pieces[k], axis, k) for k in range(1, n)]
 
 
@@ -116,8 +88,8 @@
     return total
 
 
-def reduce_axis(x, axis):
-    return reduce_end(reduce_begin(x, axis))
+def reduce_axis(x, axis, dim=0):
+    return reduce_end(reduce_begin(x, axis, dim))
 
 
 def exchange_axis(x, axis):
@@ -401,54 +373,46 @@
     chips = n_head * hb
     f_rows = down_weight.shape[0] // 2
 
-    up_cols = up_weight.reshape(w_rows, chips, n_rest, 2, f_rows).transpose(2, 0, 3, 1, 4)
-    up_cols = exchange_axis(up_cols.reshape(n_rest, w_rows, 2 * chips * f_rows), "rest").reshape(n_rest * w_rows, -1)
+    units = up_weight.reshape(w_rows, n_head, n_u, n_v, n_rest, 2, f_rows)
+    up_cols = jnp.concatenate(
+        [
+            units[..., 0, :].transpose(4, 0, 3, 2, 1, 5).reshape(n_rest, w_rows, -1),
+            units[..., 1, :].transpose(4, 0, 2, 3, 1, 5).reshape(n_rest, w_rows, -1),
+        ],
+        axis=2,
+    )
+    f_half = chips * f_rows
+    up_cols = exchange_axis(up_cols, "rest").reshape(n_rest * w_rows, 2 * f_half)
     out_rows = gather_axis(out_weight, "rest").reshape(n_rest * w_rows, width)
+    joint = jnp.concatenate([up_cols, out_rows], axis=1)
+    joint = lax.all_gather(joint, ("head", "u", "v"), axis=0, tiled=True)
+    w_up = joint[:, : 2 * f_half]
+    w_out = joint[:, 2 * f_half :]
+
+    n_up = up_bias.shape[0] // w_rows
+    vectors = [norm_gain, norm_shift, query_bias, value_bias, out_bias, post_gain, post_shift, down_bias]
+    vectors = jnp.concatenate([jnp.stack(vectors), up_bias.reshape(n_up, w_rows)]).T
+    vectors = jnp.pad(vectors, ((0, 0), (0, 128 - vectors.shape[1])))
+    cols = in_weight.reshape(w_rows, 3, n_head, hb, HEAD_DIM).transpose(2, 0, 3, 1, 4).reshape(n_head, w_rows, group)
+    cols = jnp.concatenate([cols, jnp.broadcast_to(vectors, (n_head, w_rows, 128))], axis=2)
+    cols = exchange_axis(cols, "head")
+    for axis in ("v", "u", "rest"):
+        cols = gather_axis(cols, axis)
+    cols = cols.transpose(3, 1, 2, 0, 4, 5).reshape(width, group + 128)
+    w_in = cols[:, :group]
+    vectors = cols[:, group : group + 8 + n_up].T.astype(f32)
+    gain_a, shift_a, bias_q, bias_v, bias_out, gain_b, shift_b, bias_down = (vectors[i] for i in range(8))
+    bias_up = vectors[8:].reshape(n_up, n_all, w_rows).transpose(1, 0, 2)
+
+    rows_all = gather_axis(tokens, "head").reshape(block_rows, width)
+
+    rows_all, down_weight = lax.optimization_barrier((rows_all, down_weight))
+    rows_all = rows_all.astype(f32)
     down_rows = down_weight.reshape(2, f_rows, width)
-    f_half = chips * f_rows
-
-    parts = [norm_gain, norm_shift, query_bias, value_bias, out_bias, post_gain, post_shift, down_bias, up_bias]
-    packed = [jnp.concatenate(parts).reshape(1, -1)]
-
-    cols = in_weight.reshape(w_rows, 3, n_head, hb, HEAD_DIM).transpose(2, 0, 3, 1, 4).reshape(n_head, w_rows, group)
-    w_in = [cols]
-
-    def chain_one():
-        for axis in ("rest", "v"):
-            packed[0] = gather_axis(packed[0], axis)
-        w_in[0] = exchange_axis(w_in[0], "head")
-        return (packed[0], w_in[0])
-
-    def chain_two():
-        for axis in ("u", "head"):
-            packed[0] = gather_axis(packed[0], axis)
-        w_in[0] = gather_axis(w_in[0], "v")
-        return (packed[0], w_in[0])
-
-    rows_all = gather_line(tokens, "head", [chain_one, chain_two, None]).reshape(block_rows, width).astype(f32)
-    rows_all, up_cols, down_rows, out_rows = lax.optimization_barrier((rows_all, up_cols, down_rows, out_rows))
-    if f_rows == n_rest * w_rows:
-        joint = jnp.concatenate([up_cols, down_rows[0], down_rows[1], out_rows], axis=1)
-        joint = lax.all_gather(joint, ("head", "u", "v"), axis=0, tiled=True)
-        w_up = joint[:, : 2 * f_half]
-        w_down = joint[:, 2 * f_half : 2 * f_half + width], joint[:, 2 * f_half + width : 2 * f_half + 2 * width]
-        w_out = joint[:, 2 * f_half + 2 * width :]
-    else:
-        w_up, w_down_a, w_down_b, w_out = (
-            lax.all_gather(w, ("head", "u", "v"), axis=0, tiled=True)
-            for w in (up_cols, down_rows[0], down_rows[1], out_rows)
-        )
-        w_down = w_down_a, w_down_b
-
-    packed = packed[0].reshape(n_all, -1)
-    vectors, at = [], 0
-    for part in parts:
-        size = part.shape[0]
-        vectors.append(packed[:, at : at + size].reshape(-1).astype(f32))
-        at += size
-    gain_a, shift_a, bias_q, bias_v, bias_out, gain_b, shift_b, bias_down, bias_up = vectors
-    w_in = gather_axis(gather_axis(w_in[0], "u"), "rest")
-    w_in = w_in.transpose(3, 1, 2, 0, 4, 5).reshape(width, group)
+    w_down = [gather_axis(down_rows[i], "head") for i in range(2)]
+    w_down = [gather_axis(w_down[0], "u"), gather_axis(w_down[1], "v")]
+    w_down = [gather_axis(w_down[0], "v"), gather_axis(w_down[1], "u")]
+    w_down = [w.reshape(f_half, width) for w in w_down]
 
     normed, unit_all, inverse_all = norm_forward(rows_all, gain_a, shift_a)
     normed_low = normed.astype(bf16)
@@ -487,8 +451,11 @@
     hidden_low = hidden_in.astype(bf16)
     hidden_all = gather_axis(hidden_low, "rest").reshape(n_rest * tok_rows, width)
     cot_all = gather_axis(cotangent, "rest").reshape(n_rest * tok_rows, width)
-    bias_units = lax.dynamic_index_in_dim(bias_up.reshape(chips, n_rest, 2, f_rows), me_rest, 1, keepdims=False)
-    bias_units = bias_units.transpose(1, 0, 2).reshape(-1)
+    bias_units = bias_up.reshape(n_head, n_u, n_v, n_rest, 2, f_rows)
+    bias_units = lax.dynamic_index_in_dim(bias_units, me_rest, 3, keepdims=False)
+    bias_units = jnp.concatenate(
+        [bias_units[..., 0, :].transpose(2, 1, 0, 3).reshape(-1), bias_units[..., 1, :].transpose(1, 2, 0, 3).reshape(-1)]
+    )
     pre = jnp.dot(hidden_all, w_up, preferred_element_type=f32) + bias_units
     act, slope = gelu_parts(pre)
     act_low = act.astype(bf16)
@@ -516,26 +483,31 @@
     out_grad = jnp.einsum("dt,te->de", back, grad_branch, preferred_element_type=f32).astype(bf16)
     out_grad = out_grad.reshape(chips, n_rest, w_rows, width).transpose(1, 0, 2, 3)
     out_grad = reduce_axis(out_grad, "rest").astype(bf16)
-    plane = lambda x: x.reshape(n_head, n_u, n_v, -1, x.shape[-1])
-    up_grad = plane(up_grad).transpose(1, 2, 0, 3, 4)
-    down_a, out_grad = (plane(x).transpose(2, 1, 0, 3, 4) for x in (down_grads[0], out_grad))
-    down_b = plane(down_grads[1])
+    up_grad = up_grad.reshape(n_head, n_u, n_v, -1, 2 * f_half)
+    out_grad = out_grad.reshape(n_head, n_u, n_v, -1, width)
+    down_a = down_grads[0].reshape(n_v, n_u, n_head, f_rows, width)
+    down_b = down_grads[1].reshape(n_u, n_v, n_head, f_rows, width)
     sums = [
         jnp.sum(grad_branch.astype(f32), axis=0),
         jnp.sum(grad_hidden * unit_mid, axis=0),
         jnp.sum(grad_hidden, axis=0),
         jnp.sum(grad_out, axis=0),
     ]
-    small = jnp.stack([s.reshape(chips, n_rest, -1) for s in sums], axis=2).reshape(chips, n_rest, -1)
-    small = reduce_axis(small.transpose(1, 0, 2), "rest")
-    unit_sum = jnp.sum(grad_pre.astype(f32), axis=0).reshape(2, chips, f_rows).transpose(1, 0, 2).reshape(chips, -1)
-    small = jnp.concatenate([small, unit_sum], axis=1).reshape(n_head, n_u, n_v, -1)
-
-    grad_heads, up_grad, down_a, out_grad, down_b, small = lax.optimization_barrier(
-        (grad_heads, up_grad, down_a, out_grad, down_b, small)
-    )
-    begun = [reduce_begin(up_grad, "u"), reduce_begin(down_a, "v"), reduce_begin(out_grad, "v")]
-    begun.append(reduce_begin(down_b, "head"))
+    unit_sum = jnp.sum(grad_pre.astype(f32), axis=0)
+    unit_sum = jnp.stack(
+        [
+            unit_sum[:f_half].reshape(n_v, n_u, n_head, f_rows).transpose(2, 1, 0, 3),
+            unit_sum[f_half:].reshape(n_u, n_v, n_head, f_rows).transpose(2, 0, 1, 3),
+        ],
+        axis=3,
+    ).reshape(chips, 1, 2 * f_rows)
+    unit_sum = jnp.where((jnp.arange(n_rest) == me_rest)[:, None], unit_sum, 0.0).reshape(n_head, n_blk, n_up, w_rows)
+
+    grad_heads, up_grad, down_a, out_grad, down_b = lax.optimization_barrier(
+        (grad_heads, up_grad, down_a, out_grad, down_b)
+    )
+    begun = [reduce_begin(up_grad, "u", 1), reduce_begin(down_a, "v"), reduce_begin(out_grad, "v", 2)]
+    begun.append(reduce_begin(down_b, "head", 2))
 
     dq, dkv = attention_backward(bounds, qkv, far, starts, grad_heads, wide, lse)
     dq, dkv, begun = lax.optimization_barrier((dq, dkv, begun))
@@ -545,61 +517,71 @@
         jnp.concatenate([dq, dkv], axis=1), ("u", "v"), split_axis=0, concat_axis=0, tiled=True
     ).reshape(group, block_rows)
 
-    grad_proj, up_grad, down_a, out_grad, down_b, small = lax.optimization_barrier(
-        (grad_proj, up_grad, down_a, out_grad, down_b, small)
-    )
-    up_grad = reduce_axis(up_grad, "v").astype(bf16)
-    down_a, out_grad, down_b = (reduce_axis(x, "u").astype(bf16) for x in (down_a, out_grad, down_b))
-    small = reduce_axis(reduce_axis(small, "head"), "u")
-    small = reduce_axis(small, "v")
-
     grad_normed = lax.dot_general(grad_proj, w_in, (((0,), (1,)), ((), ())), preferred_element_type=f32)
-    grad_tokens = reduce_axis(grad_normed.astype(bf16).reshape(n_head, tok_rows, width), "head")
-    grad_tokens, up_grad, down_a, out_grad, down_b = lax.optimization_barrier(
-        (grad_tokens, up_grad, down_a, out_grad, down_b)
-    )
-    up_weight_grad = reduce_axis(up_grad, "head").astype(bf16).reshape(n_rest, w_rows, -1)
-    up_weight_grad = exchange_axis(up_weight_grad, "rest").astype(f32)
-    up_weight_grad = up_weight_grad.reshape(n_rest, w_rows, 2, chips, f_rows).transpose(1, 3, 0, 2, 4)
-    up_weight_grad = up_weight_grad.reshape(w_rows, -1)
-    down_a, out_weight_grad = (reduce_axis(x, "head") for x in (down_a, out_grad))
-    down_b = reduce_axis(down_b, "v")
-    down_weight_grad = jnp.concatenate([down_a, down_b], axis=0)
-    size = width // n_all
-    out_bias_grad, post_gain_grad, post_shift_grad, down_bias_grad = (
-        small[i * size : (i + 1) * size] for i in range(4)
-    )
-    up_bias_grad = small[4 * size :]
-    unit_in = lax.dynamic_index_in_dim(unit_all.reshape(n_head, tok_rows, width), me_head, 0, keepdims=False)
-    inverse_in = lax.dynamic_index_in_dim(inverse_all.reshape(n_head, tok_rows, 1), me_head, 0, keepdims=False)
-    tokens_grad = (grad_middle + norm_inner(grad_tokens, unit_in, inverse_in, gain_a)).astype(bf16)
+    tokens_low = grad_normed.astype(bf16).reshape(n_head, tok_rows, width)
+    tokens_low, grad_proj, up_grad, down_a, out_grad, down_b = lax.optimization_barrier(
+        (tokens_low, grad_proj, up_grad, down_a, out_grad, down_b)
+    )
+    begun = reduce_begin(tokens_low, "head")
 
     in_grad = lax.dot_general(normed_low, grad_proj, (((0,), (1,)), ((), ())), preferred_element_type=f32)
-    gain_grad = jnp.sum(grad_normed * unit_all, axis=0).reshape(n_head, n_blk, w_rows)
-    shift_grad = jnp.sum(grad_normed, axis=0).reshape(n_head, n_blk, w_rows)
+    rowed = lambda x: x.reshape(n_head, n_blk, w_rows)
+    gain_grad = rowed(jnp.sum(grad_normed * unit_all, axis=0))
+    shift_grad = rowed(jnp.sum(grad_normed, axis=0))
     col_sum = jnp.sum(grad_proj.astype(f32), axis=1).reshape(hb, 3, HEAD_DIM)
     mine = (jnp.arange(n_head) == me_head)[:, None, None]
     query_sum = jnp.where(mine, col_sum[:, 0].reshape(1, n_blk, w_rows), 0.0)
     value_sum = jnp.where(mine, col_sum[:, 2].reshape(1, n_blk, w_rows), 0.0)
-    extra = jnp.stack([gain_grad, shift_grad, query_sum, value_sum], axis=-1)
-    extra = jnp.pad(extra, ((0, 0), (0, 0), (0, 0), (0, 124)))
+    extra = jnp.stack([gain_grad, shift_grad, query_sum, value_sum, *(rowed(x) for x in sums)], axis=2)
+    extra = jnp.concatenate([extra, unit_sum], axis=2)
+    n_extra = extra.shape[2]
+    extra = jnp.pad(extra.transpose(0, 1, 3, 2), ((0, 0), (0, 0), (0, 0), (0, 128 - n_extra)))
     joined = jnp.concatenate([in_grad.reshape(n_head, n_blk, w_rows, group), extra], axis=-1).astype(bf16)
-    joined = joined.transpose(1, 0, 2, 3).reshape(hb, n_rest, n_head, w_rows, group + 128).transpose(1, 0, 2, 3, 4)
-    joined = reduce_axis(joined, "rest").astype(bf16).reshape(n_u, n_v, n_head, w_rows, group + 128)
-    joined = reduce_axis(joined, "u").astype(bf16)
-    joined = reduce_axis(joined, "v").astype(bf16)
+    joined = joined.reshape(n_head, n_u, n_v, n_rest, w_rows, group + 128)
+    joined = reduce_axis(joined, "rest", 3).astype(bf16)
+    joined = reduce_axis(joined, "u", 1).astype(bf16)
+    joined = reduce_axis(joined, "v", 1).astype(bf16)
+
+    up_grad = reduce_axis(up_grad, "v", 1).astype(bf16)
+    down_a = reduce_axis(down_a, "u").astype(bf16)
+    out_grad = reduce_axis(out_grad, "u", 1).astype(bf16)
+    down_b = reduce_axis(down_b, "u").astype(bf16)
+
+    begun, joined, up_grad, down_a, out_grad, down_b = lax.optimization_barrier(
+        (begun, joined, up_grad, down_a, out_grad, down_b)
+    )
+    up_grad = reduce_axis(up_grad, "head").astype(bf16).reshape(n_rest, w_rows, 2 * f_half)
+    down_a, out_weight_grad = (reduce_axis(x, "head") for x in (down_a, out_grad))
+    down_b = reduce_axis(down_b, "v")
+    down_weight_grad = jnp.concatenate([down_a, down_b], axis=0)
+    up_grad = exchange_axis(up_grad, "rest").astype(f32)
+    up_weight_grad = jnp.stack(
+        [
+            up_grad[..., :f_half].reshape(n_rest, w_rows, n_v, n_u, n_head, f_rows).transpose(1, 4, 3, 2, 0, 5),
+            up_grad[..., f_half:].reshape(n_rest, w_rows, n_u, n_v, n_head, f_rows).transpose(1, 4, 2, 3, 0, 5),
+        ],
+        axis=5,
+    ).reshape(w_rows, -1)
     joined = exchange_axis(joined, "head").astype(f32)
     in_weight_grad = joined[:, :, :group].reshape(n_head, w_rows, hb, 3, HEAD_DIM).transpose(1, 3, 0, 2, 4)
     in_weight_grad = in_weight_grad.reshape(w_rows, 3 * width)
-    extra = jnp.sum(joined[:, :, group : group + 4], axis=0)
+    extra = jnp.sum(joined[:, :, group : group + n_extra], axis=0).T
+    norm_gain_grad, norm_shift_grad, query_bias_grad, value_bias_grad = (extra[i] for i in range(4))
+    out_bias_grad, post_gain_grad, post_shift_grad, down_bias_grad = (extra[i] for i in range(4, 8))
+    up_bias_grad = extra[8:].reshape(-1)
+
+    grad_tokens = reduce_end(begun)
+    unit_in = lax.dynamic_index_in_dim(unit_all.reshape(n_head, tok_rows, width), me_head, 0, keepdims=False)
+    inverse_in = lax.dynamic_index_in_dim(inverse_all.reshape(n_head, tok_rows, 1), me_head, 0, keepdims=False)
+    tokens_grad = (grad_middle + norm_inner(grad_tokens, unit_in, inverse_in, gain_a)).astype(bf16)
     return (
         output,
         tokens_grad,
-        extra[:, 0],
-        extra[:, 1],
+        norm_gain_grad,
+        norm_shift_grad,
         in_weight_grad,
-        extra[:, 2],
-        extra[:, 3],
+        query_bias_grad,
+        value_bias_grad,
         out_weight_grad,
         out_bias_grad,
         post_gain_grad,

time: 567 us -> 548 us (0.966)
  starting transfers between devices: 97.2 us -> 151 us
  waiting for transfers between devices: 180 us -> 133 us
  blocking collectives: 34.1 us -> 0 us
  local copies, waits for them, and re-layouts: 55.9 us -> 80.3 us
  Pallas kernels: 84.9 us -> 67.6 us
  matrix products: 48.4 us -> 54.7 us
  other arithmetic: 41.9 us -> 35.6 us
    ppermute x57 -> x58, starting transfers between devices: 61.1 us -> 129 us  [shifted(): return lax.ppermute(x, axis, [(i, (i + k) % n) for i in range(n)])]
    all_to_all x1 -> x0, blocking collectives: 34.1 us -> none  [on_device(): lax.all_to_all(projected.reshape(hb, 3 * HEAD_DIM, block_rows), ('u', 'v'...]
    all_gather x1, waiting for transfers between devices: 24.7 us -> 0.01 us  [on_device(): joint = lax.all_gather(joint, ('head', 'u', 'v'), axis=0, tiled=True)]
    ppermute x6 -> x0, waiting for transfers between devices: 20.7 us -> none  [the longest x3 11.1 us: gather_line(): right.append(lax.ppermute(right[-1], axis, down))]
    ppermute x6 -> x0, starting transfers between devices: 17.5 us -> none  [the longest x3 13.6 us: gather_line(): left.append(lax.ppermute(left[-1], axis, up))]
    dynamic_update_slice x30 -> x39, local copies, waits for them, and re-layouts: 10 us -> 26.3 us  [put(): return lax.dynamic_update_index_in_dim(buffer, x, index, 0)]
    all_to_all x1, waiting for transfers between devices: 18.2 us -> 3.77 us  [on_device(): lax.all_to_all(attended.reshape(HEADS, HEAD_DIM, tok_rows), ('head', 'u',...]
    pallas_call x1, Pallas kernels: 48.5 us -> 39.2 us  [attention_backward(): pl.pallas_call(functools.partial(backward_kernel, n_steps), grid_spec=plt...]
  transfers between devices with their start and end apart: 67 -> 63, of which waited for: 27 -> 25; matrix products, arithmetic and copies ran while one was open for 18% -> 22% of each run, Pallas kernels for 15% -> 13%
where the time goes in v4:
time: 548 us; the launch traced here: 538 us
  starting transfers between devices  151 us (28%)
  waiting for transfers between devices  133 us (24%)
  local copies, waits for them, and re-layouts  80.3 us (15%)
  Pallas kernels  67.6 us (12%)
  matrix products  54.7 us (10%)
  other arithmetic  35.6 us (6%)
  between operations  16 us (3%)
    ppermute x58, starting transfers between devices, shifted(): return lax.ppermute(x, axis, [(i, (i + k) % n) for i in range(n)])  129 us
    ppermute x58, waiting for transfers between devices, shifted(): return lax.ppermute(x, axis, [(i, (i + k) % n) for i in range(n)])  106 us
    pallas_call x1, Pallas kernels, attention_backward(): pl.pallas_call(functools.partial(backward_kernel, n_steps), grid_spec=plt...  39.2 us
    pallas_call x1, Pallas kernels, attention_forward(): pl.pallas_call(forward_kernel, grid_spec=pltpu.PrefetchScalarGridSpec(num...  28.4 us
    dynamic_update_slice x39, local copies, waits for them, and re-layouts, put(): return lax.dynamic_update_index_in_dim(buffer, x, index, 0)  26.3 us
    squeeze x19, local copies, waits for them, and re-layouts, reduce_begin(): lax.dynamic_index_in_dim(x, (me + k) % n, dim, keepdims=False)  14.2 us
    unnamed x146, local copies, waits for them, and re-layouts  11.2 us
    all_to_all x1, waiting for transfers between devices, on_device(): lax.all_to_all(jnp.concatenate([dq, dkv], axis=1), ('u', 'v'), split_axis...  11.1 us
  transfers between devices with their start and end apart: 63, of which 25 were waited for; matrix products, arithmetic and copies ran while one was open for 22% of the time, Pallas kernels for 13%

profile of v4, /device:TPU:0, one launch (start us, length us, event | category | flops | bytes accessed | tf_op | source)
XLA Modules:
  0.0 538.1 jit_solution(10409765846173983353)
XLA Ops:
  7.3 3.1 collective-permute-start.6
  31.7 19.7 %collective-permute-done = bf16[32,896]{1,0:T(8,128)(2,1)S(1)} collective-permute-done((bf16[32,896]{1,0:T(8,128)(2,1)S(1)}, bf16[32,896]{1,0:T(8,128)(2,1)S(1)}, u32[]{:S(2)}, u32[]{:S(2)}) %collective-permute-start) | collective-permute-done | bytes 57376 | tf_op jit(solution)/shard_map/ppermute | solution.py:57
  51.4 21.4 %collective-permute-start.1 = (bf16[32,896]{1,0:T(8,128)(2,1)S(1)}, bf16[32,896]{1,0:T(8,128)(2,1)S(1)}, u32[]{:S(2)}, u32[]{:S(2)}) collective-permute-start(bf16[32,896]{1,0:T(8,128)(2,1)S(1)} %get-tuple-element.179), channel_id=1, source_target_pairs={{0,16},{8,24},{16,0},{24,8},{1,17},{9,25},{17,1},{25,9},{2,18},{10... | collective-permute-start | bytes 172040 | tf_op jit(solution)/shard_map/ppermute | solution.py:57
  72.9 5.8 %collective-permute-done.1 = bf16[32,896]{1,0:T(8,128)(2,1)S(1)} collective-permute-done((bf16[32,896]{1,0:T(8,128)(2,1)S(1)}, bf16[32,896]{1,0:T(8,128)(2,1)S(1)}, u32[]{:S(2)}, u32[]{:S(2)}) %collective-permute-start.1) | collective-permute-done | bytes 57376 | tf_op jit(solution)/shard_map/ppermute | solution.py:57
  78.7 6.6 %collective-permute-done.2 = bf16[32,896]{1,0:T(8,128)(2,1)S(1)} collective-permute-done((bf16[32,896]{1,0:T(8,128)(2,1)S(1)}, bf16[32,896]{1,0:T(8,128)(2,1)S(1)}, u32[]{:S(2)}, u32[]{:S(2)}) %collective-permute-start.2) | collective-permute-done | bytes 57376 | tf_op jit(solution)/shard_map/ppermute | solution.py:57
  87.5 3.9 collective-permute-done.3
  98.3 3.1 collective-permute-start.15
  102.4 6.2 %collective-permute-done.4 = bf16[2,4,32,896]{3,2,0,1:T(8,128)(2,1)S(1)} collective-permute-done((bf16[2,4,32,896]{3,2,0,1:T(8,128)(2,1)S(1)}, bf16[2,4,32,896]{3,2,0,1:T(8,128)(2,1)S(1)}, u32[]{:S(2)}, u32[]{:S(2)}) %collective-permute-start.4) | collective-permute-done | bytes 458784 | tf_op jit(solution)/shard_map/ppermute | solution.py:57
  120.0 4.9 add_convert_fusion.2
  124.9 5.4 %all-to-all-start = ((bf16[4,192,1024]{2,1,0:T(8,128)(2,1)}), bf16[4,192,1024]{2,1,0:T(8,128)(2,1)}, u32[]{:S(2)}, u32[]{:S(2)}) async-start(bf16[4,192,1024]{2,1,0:T(8,128)(2,1)} %bitcast.376), calls=%async_computation | async-start | bytes 3145728 | tf_op jit(solution)/shard_map/all_to_all | solution.py:423
  131.8 3.7 collective-permute-start.20
  142.6 8.4 %all-to-all-done.q_ref.own_ref = bf16[4,192,1024]{2,1,0:T(8,128)(2,1)} async-done(((bf16[4,192,1024]{2,1,0:T(8,128)(2,1)}), bf16[4,192,1024]{2,1,0:T(8,128)(2,1)}, u32[]{:S(2)}, u32[]{:S(2)}) %all-to-all-start) | async-done | bytes 1572896 | tf_op jit(solution)/shard_map/all_to_all | solution.py:423
  158.2 3.3 collective-permute-done.16
  174.3 28.4 %attention_forward.1 = (bf16[4,4,64,256]{3,2,1,0:T(8,128)(2,1)}, f32[4,64,1024]{2,1,0:T(8,128)}, f32[4,1,1024]{2,1,0:T(1,128)}) custom-call(s32[8]{0:T(128)} %get-tuple-element.190.lo_ref, s32[8]{0:T(128)} %get-tuple-element.189.mid_ref, s32[8]{0:T(128)} %add.613.q0_ref, s32[1]{0:T(128)} %bitcast.me_ref, bf16[4,192,1024]{2,1,0:T(8,128)(2,1)} %all-to-all-done.q_ref.own_ref, ...), custom_call_target="tpu_custom_call" | custom-call | flops 17179869184 | bytes 4194304 | tf_op jit(solution)/shard_map/attention_forward/pallas_call | solution.py:282
  202.7 6.8 %all-to-all-start.1 = ((bf16[16,64,256]{2,1,0:T(8,128)(2,1)}), bf16[16,64,256]{2,1,0:T(8,128)(2,1)S(1)}, u32[]{:S(2)}, u32[]{:S(2)}) async-start(bf16[16,64,256]{2,1,0:T(8,128)(2,1)} %bitcast.386), calls=%async_computation.1 | async-start | bytes 1048576 | tf_op jit(solution)/shard_map/all_to_all | solution.py:443
  212.0 4.5 fusion.91
  216.5 3.8 all-to-all-done.1
  224.5 6.0 %collective-permute-start.12 = (bf16[256,1024]{1,0:T(8,128)(2,1)S(1)}, bf16[256,1024]{1,0:T(8,128)(2,1)S(1)}, u32[]{:S(2)}, u32[]{:S(2)}) collective-permute-start(bf16[256,1024]{1,0:T(8,128)(2,1)S(1)} %get-tuple-element.129), channel_id=1, source_target_pairs={{0,1},{1,0},{2,3},{3,2},{4,5},{5,4},{6,7},{7,6},{8,9},{9,8},{10,11... | collective-permute-start | bytes 1572872 | tf_op jit(solution)/shard_map/ppermute | solution.py:57
  234.8 6.2 %convert_reduce_fusion.1 = (bf16[2048]{0:T(1024)(128)(2,1)S(1)}, bf16[512,2048]{1,0:T(8,128)(2,1)S(1)}, bf16[512,2048]{1,0:T(8,128)(2,1)S(1)}) fusion(f32[2048]{0:T(1024)S(1)} %pad_maximum_fusion.6, f32[512,1024]{1,0:T(8,128)S(1)} %fusion.92, f32[512,1024]{1,0:T(8,128)S(1)} %copy-done.67, bf16[512,1024]{1,0:T(8,128)(2,1)S(1)} %bitcast.381, ...), kind=kOutput, calls=%fused_computation.16 | convolution fusion | flops 2173696000 | bytes 13643776 | tf_op jit(solution)/shard_map/dot_general | solution.py:459
  253.4 4.4 convolution_convert_fusion.3
  257.8 3.1 multiply_reduce_fusion.1
  263.3 3.2 fusion.33
  266.4 4.5 all-to-all-start.2
  271.0 4.3 convolution_convert_fusion.1
  275.3 4.4 convolution_convert_fusion
  282.3 3.7 all-to-all-done.2
  299.4 6.3 %collective-permute-done.30 = bf16[2,2,64,1024]{3,2,1,0:T(8,128)(2,1)S(1)} collective-permute-done((bf16[2,2,64,1024]{3,2,1,0:T(8,128)(2,1)S(1)}, bf16[2,2,64,1024]{3,2,1,0:T(8,128)(2,1)S(1)}, u32[]{:S(2)}, u32[]{:S(2)}) %collective-permute-start.30) | collective-permute-done | bytes 524320 | tf_op jit(solution)/shard_map/ppermute | solution.py:57
  306.7 39.2 %attention_backward.1 = (bf16[4,64,1024]{2,1,0:T(8,128)(2,1)}, bf16[2,4,128,1024]{3,2,1,0:T(8,128)(2,1)}) custom-call(s32[8]{0:T(128)} %get-tuple-element.190.lo_ref, s32[8]{0:T(128)} %get-tuple-element.189.mid_ref, s32[8]{0:T(128)} %add.613.q0_ref, s32[1]{0:T(128)} %bitcast.me_ref, bf16[4,192,1024]{2,1,0:T(8,128)(2,1)} %all-to-all-done.q_ref.own_ref, ...), custom_call_target="tpu_custom_call" | custom-call | flops 42949672960 | bytes 4194304 | tf_op jit(solution)/shard_map/attention_backward/pallas_call | solution.py:320
  349.4 6.8 %collective-permute-start.33 = (bf16[4,128,1024]{2,1,0:T(8,128)(2,1)}, bf16[4,128,1024]{2,1,0:T(8,128)(2,1)}, u32[]{:S(2)}, u32[]{:S(2)}) collective-permute-start(bf16[4,128,1024]{2,1,0:T(8,128)(2,1)} %dynamic-slice_bitcast_fusion.3), channel_id=1, source_target_pairs={{0,1},{1,0},{2,3},{3,2},{4,5},{5,4},{6,7},{7,6},{8,9},{9,8},{10,11... | collective-permute-start | bytes 3145736 | tf_op jit(solution)/shard_map/ppermute | solution.py:57
  362.2 4.8 all-to-all-start.3
  372.3 3.7 add_convert_fusion
  376.0 11.1 %all-to-all-done.3 = bf16[4,192,1024]{2,1,0:T(8,128)(2,1)} async-done(((bf16[4,192,1024]{2,1,0:T(8,128)(2,1)}), bf16[4,192,1024]{2,1,0:T(8,128)(2,1)}, u32[]{:S(2)}, u32[]{:S(2)}) %all-to-all-start.3) | async-done | bytes 1572896 | tf_op jit(solution)/shard_map/all_to_all | solution.py:516
  387.1 7.1 %fusion.81 = (bf16[1024]{0:T(1024)(128)(2,1)S(1)}, bf16[1024]{0:T(1024)(128)(2,1)S(1)}, bf16[1024,1024]{1,0:T(8,128)(2,1)}, f32[1024,1024]{1,0:T(8,128)}) fusion(f32[1024]{0:T(1024)S(1)} %copy-done.54, f32[1024]{0:T(1024)S(1)} %copy-done.53, bf16[1024,1024]{1,0:T(8,128)(2,1)S(1)} %bitcast.344, bf16[768,1024]{1,0:T(8,128)(2,1)} %bitcast.110, ...), kind=kOutput, calls=%fused_computation.280 | convolution fusion | flops 1617950720 | bytes 11546624 | tf_op jit(solution)/shard_map/dot_general | solution.py:520
  394.2 4.8 convolution_convert_fusion.4
  408.3 4.5 collective-permute-done.43
  412.8 14.1 %collective-permute-start.34 = (bf16[256,1024]{1,0:T(8,128)(2,1)S(1)}, bf16[256,1024]{1,0:T(8,128)(2,1)S(1)}, u32[]{:S(2)}, u32[]{:S(2)}) collective-permute-start(bf16[256,1024]{1,0:T(8,128)(2,1)S(1)} %get-tuple-element.139), channel_id=1, source_target_pairs={{0,8},{8,16},{16,24},{24,0},{1,9},{9,17},{17,25},{25,1},{2,10},{10... | collective-permute-start | bytes 1572872 | tf_op jit(solution)/shard_map/ppermute | solution.py:57
  434.1 6.7 %collective-permute-done.38 = bf16[4,2,32,896]{3,2,0,1:T(8,128)(2,1)S(1)} collective-permute-done((bf16[4,2,32,896]{3,2,0,1:T(8,128)(2,1)S(1)}, bf16[4,2,32,896]{3,2,0,1:T(8,128)(2,1)S(1)}, u32[]{:S(2)}, u32[]{:S(2)}) %collective-permute-start.38) | collective-permute-done | bytes 458784 | tf_op jit(solution)/shard_map/ppermute | solution.py:57
  442.9 4.1 collective-permute-done.39
  447.1 7.0 %collective-permute-done.35 = bf16[256,1024]{1,0:T(8,128)(2,1)S(1)} collective-permute-done((bf16[256,1024]{1,0:T(8,128)(2,1)S(1)}, bf16[256,1024]{1,0:T(8,128)(2,1)S(1)}, u32[]{:S(2)}, u32[]{:S(2)}) %collective-permute-start.35) | collective-permute-done | bytes 524320 | tf_op jit(solution)/shard_map/ppermute | solution.py:57
  454.1 9.2 %collective-permute-done.36 = bf16[256,1024]{1,0:T(8,128)(2,1)S(1)} collective-permute-done((bf16[256,1024]{1,0:T(8,128)(2,1)S(1)}, bf16[256,1024]{1,0:T(8,128)(2,1)S(1)}, u32[]{:S(2)}, u32[]{:S(2)}) %collective-permute-start.36) | collective-permute-done | bytes 524320 | tf_op jit(solution)/shard_map/ppermute | solution.py:57
  464.0 10.7 %collective-permute-start.54 = (bf16[64,1024]{1,0:T(8,128)(2,1)}, bf16[64,1024]{1,0:T(8,128)(2,1)}, u32[]{:S(2)}, u32[]{:S(2)}) collective-permute-start(bf16[64,1024]{1,0:T(8,128)(2,1)} %get-tuple-element.153), channel_id=1, source_target_pairs={{0,8},{8,16},{16,24},{24,0},{1,9},{9,17},{17,25},{25,1},{2,10},{10... | collective-permute-start | bytes 393224 | tf_op jit(solution)/shard_map/ppermute | solution.py:57
  474.7 3.4 collective-permute-start.55
  479.8 4.4 collective-permute-start.44
  487.4 3.6 collective-permute-start.45
  493.8 4.5 collective-permute-done.46
  507.1 3.1 collective-permute-start.52
  514.3 3.3 collective-permute-done.50
  517.5 8.2 %collective-permute-done.51 = bf16[64,2048]{1,0:T(8,128)(2,1)S(1)} collective-permute-done((bf16[64,2048]{1,0:T(8,128)(2,1)}, bf16[64,2048]{1,0:T(8,128)(2,1)S(1)}, u32[]{:S(2)}, u32[]{:S(2)}) %collective-permute-start.51) | collective-permute-done | bytes 262176 | tf_op jit(solution)/shard_map/ppermute | solution.py:57
  (454 shorter events, 173.1 us)
Async XLA Ops:
  7.3 213.0 %all-gather.2.cloned.1.call-start = ((), (), s32[]{:S(2)}) async-start(), calls=%async_computation.4 | async-start | bytes 6684672 | tf_op jit(solution)/shard_map/all_gather | solution.py:388
  7.3 86.0 %collective-permute-start.6 = (bf16[256,1024]{1,0:T(8,128)(2,1)}, bf16[256,1024]{1,0:T(8,128)(2,1)}, u32[]{:S(2)}, u32[]{:S(2)}) collective-permute-start(bf16[256,1024]{1,0:T(8,128)(2,1)} %param.16), channel_id=1, source_target_pairs={{0,8},{8,16},{16,24},{24,0},{1,9},{9,17},{17,25},{25,1},{2,10},{10... | collective-permute-start | bytes 1572872 | tf_op jit(solution)/shard_map/ppermute | solution.py:57
  10.4 84.2 %collective-permute-start.7 = (bf16[256,1024]{1,0:T(8,128)(2,1)}, bf16[256,1024]{1,0:T(8,128)(2,1)}, u32[]{:S(2)}, u32[]{:S(2)}) collective-permute-start(bf16[256,1024]{1,0:T(8,128)(2,1)} %param.16), channel_id=1, source_target_pairs={{0,16},{8,24},{16,0},{24,8},{1,17},{9,25},{17,1},{25,9},{2,18},{10... | collective-permute-start | bytes 1572872 | tf_op jit(solution)/shard_map/ppermute | solution.py:57
  13.0 82.7 %collective-permute-start.8 = (bf16[256,1024]{1,0:T(8,128)(2,1)}, bf16[256,1024]{1,0:T(8,128)(2,1)}, u32[]{:S(2)}, u32[]{:S(2)}) collective-permute-start(bf16[256,1024]{1,0:T(8,128)(2,1)} %param.16), channel_id=1, source_target_pairs={{0,24},{8,0},{16,8},{24,16},{1,25},{9,1},{17,9},{25,17},{2,26},{10... | collective-permute-start | bytes 1572872 | tf_op jit(solution)/shard_map/ppermute | solution.py:57
  14.4 14.4 %collective-permute-start.11 = (bf16[32,1024]{1,0:T(8,128)(2,1)}, bf16[32,1024]{1,0:T(8,128)(2,1)}, u32[]{:S(2)}, u32[]{:S(2)}) collective-permute-start(bf16[32,1024]{1,0:T(8,128)(2,1)} %param.24), channel_id=1, source_target_pairs={{0,1},{1,0},{2,3},{3,2},{4,5},{5,4},{6,7},{7,6},{8,9},{9,8},{10,11... | collective-permute-start | bytes 196616 | tf_op jit(solution)/shard_map/ppermute | solution.py:57
  14.4 95.0 %collective-permute-start.24 = (bf16[256,1024]{1,0:T(8,128)(2,1)}, bf16[256,1024]{1,0:T(8,128)(2,1)}, u32[]{:S(2)}, u32[]{:S(2)}) collective-permute-start(bf16[256,1024]{1,0:T(8,128)(2,1)} %param.17), channel_id=1, source_target_pairs={{0,1},{1,0},{2,3},{3,2},{4,5},{5,4},{6,7},{7,6},{8,9},{9,8},{10,11... | collective-permute-start | bytes 1572872 | tf_op jit(solution)/shard_map/ppermute | solution.py:57
  30.2 21.2 %collective-permute-start = (bf16[32,896]{1,0:T(8,128)(2,1)S(1)}, bf16[32,896]{1,0:T(8,128)(2,1)S(1)}, u32[]{:S(2)}, u32[]{:S(2)}) collective-permute-start(bf16[32,896]{1,0:T(8,128)(2,1)S(1)} %get-tuple-element.178), channel_id=1, source_target_pairs={{0,8},{8,16},{16,24},{24,0},{1,9},{9,17},{17,25},{25,1},{2,10},{10... | collective-permute-start | bytes 172040 | tf_op jit(solution)/shard_map/ppermute | solution.py:57
  51.4 27.2 %collective-permute-start.1 = (bf16[32,896]{1,0:T(8,128)(2,1)S(1)}, bf16[32,896]{1,0:T(8,128)(2,1)S(1)}, u32[]{:S(2)}, u32[]{:S(2)}) collective-permute-start(bf16[32,896]{1,0:T(8,128)(2,1)S(1)} %get-tuple-element.179), channel_id=1, source_target_pairs={{0,16},{8,24},{16,0},{24,8},{1,17},{9,25},{17,1},{25,9},{2,18},{10... | collective-permute-start | bytes 172040 | tf_op jit(solution)/shard_map/ppermute | solution.py:57
  91.5 17.1 %collective-permute-start.4 = (bf16[2,4,32,896]{3,2,0,1:T(8,128)(2,1)S(1)}, bf16[2,4,32,896]{3,2,0,1:T(8,128)(2,1)S(1)}, u32[]{:S(2)}, u32[]{:S(2)}) collective-permute-start(bf16[2,4,32,896]{3,2,0,1:T(8,128)(2,1)S(1)} %bitcast_dynamic-update-slice_fusion.21), channel_id=1, source_target_pairs={{0,4},{4,0},{1,5},{5,1},{2,6},{6,2},{3,7},{7,3},{8,12},{12,8},{9,1... | collective-permute-start | bytes 1376264 | tf_op jit(solution)/shard_map/ppermute | solution.py:57
  97.5 34.3 %collective-permute-start.13 = (bf16[64,1024]{1,0:T(8,128)(2,1)}, bf16[64,1024]{1,0:T(8,128)(2,1)}, u32[]{:S(2)}, u32[]{:S(2)}) collective-permute-start(bf16[64,1024]{1,0:T(8,128)(2,1)} %get-tuple-element.168), channel_id=1, source_target_pairs={{0,8},{8,16},{16,24},{24,0},{1,9},{9,17},{17,25},{25,1},{2,10},{10... | collective-permute-start | bytes 393224 | tf_op jit(solution)/shard_map/ppermute | solution.py:57
  97.5 38.8 %collective-permute-start.14 = (bf16[64,1024]{1,0:T(8,128)(2,1)}, bf16[64,1024]{1,0:T(8,128)(2,1)}, u32[]{:S(2)}, u32[]{:S(2)}) collective-permute-start(bf16[64,1024]{1,0:T(8,128)(2,1)} %get-tuple-element.168), channel_id=1, source_target_pairs={{0,16},{8,24},{16,0},{24,8},{1,17},{9,25},{17,1},{25,9},{2,18},{10... | collective-permute-start | bytes 393224 | tf_op jit(solution)/shard_map/ppermute | solution.py:57
  98.3 39.0 %collective-permute-start.15 = (bf16[64,1024]{1,0:T(8,128)(2,1)}, bf16[64,1024]{1,0:T(8,128)(2,1)S(1)}, u32[]{:S(2)}, u32[]{:S(2)}) collective-permute-start(bf16[64,1024]{1,0:T(8,128)(2,1)} %get-tuple-element.168), channel_id=1, source_target_pairs={{0,24},{8,0},{16,8},{24,16},{1,25},{9,1},{17,9},{25,17},{2,26},{10... | collective-permute-start | bytes 393224 | tf_op jit(solution)/shard_map/ppermute | solution.py:57
  109.4 30.0 %collective-permute-start.18 = (bf16[64,1024]{1,0:T(8,128)(2,1)}, bf16[64,1024]{1,0:T(8,128)(2,1)}, u32[]{:S(2)}, u32[]{:S(2)}) collective-permute-start(bf16[64,1024]{1,0:T(8,128)(2,1)} %get-tuple-element.169), channel_id=1, source_target_pairs={{0,8},{8,16},{16,24},{24,0},{1,9},{9,17},{17,25},{25,1},{2,10},{10... | collective-permute-start | bytes 393224 | tf_op jit(solution)/shard_map/ppermute | solution.py:57
  112.5 28.6 %collective-permute-start.19 = (bf16[64,1024]{1,0:T(8,128)(2,1)}, bf16[64,1024]{1,0:T(8,128)(2,1)}, u32[]{:S(2)}, u32[]{:S(2)}) collective-permute-start(bf16[64,1024]{1,0:T(8,128)(2,1)} %get-tuple-element.169), channel_id=1, source_target_pairs={{0,16},{8,24},{16,0},{24,8},{1,17},{9,25},{17,1},{25,9},{2,18},{10... | collective-permute-start | bytes 393224 | tf_op jit(solution)/shard_map/ppermute | solution.py:57
  124.9 26.1 %all-to-all-start = ((bf16[4,192,1024]{2,1,0:T(8,128)(2,1)}), bf16[4,192,1024]{2,1,0:T(8,128)(2,1)}, u32[]{:S(2)}, u32[]{:S(2)}) async-start(bf16[4,192,1024]{2,1,0:T(8,128)(2,1)} %bitcast.376), calls=%async_computation | async-start | bytes 3145728 | tf_op jit(solution)/shard_map/all_to_all | solution.py:423
  131.8 19.2 %collective-permute-start.20 = (bf16[64,1024]{1,0:T(8,128)(2,1)}, bf16[64,1024]{1,0:T(8,128)(2,1)S(1)}, u32[]{:S(2)}, u32[]{:S(2)}) collective-permute-start(bf16[64,1024]{1,0:T(8,128)(2,1)} %get-tuple-element.169), channel_id=1, source_target_pairs={{0,24},{8,0},{16,8},{24,16},{1,25},{9,1},{17,9},{25,17},{2,26},{10... | collective-permute-start | bytes 393224 | tf_op jit(solution)/shard_map/ppermute | solution.py:57
  137.3 24.2 %collective-permute-start.16 = (bf16[4,64,1024]{2,1,0:T(8,128)(2,1)S(1)}, bf16[4,64,1024]{2,1,0:T(8,128)(2,1)}, u32[]{:S(2)}, u32[]{:S(2)}) collective-permute-start(bf16[4,64,1024]{2,1,0:T(8,128)(2,1)S(1)} %bitcast_dynamic-update-slice_fusion.27), channel_id=1, source_target_pairs={{0,4},{4,0},{1,5},{5,1},{2,6},{6,2},{3,7},{7,3},{8,12},{12,8},{9,1... | collective-permute-start | bytes 1572872 | tf_op jit(solution)/shard_map/ppermute | solution.py:57
  151.0 23.3 %collective-permute-start.9 = (bf16[4,192,1024]{2,1,0:T(8,128)(2,1)}, bf16[4,192,1024]{2,1,0:T(8,128)(2,1)}, u32[]{:S(2)}, u32[]{:S(2)}) collective-permute-start(bf16[4,192,1024]{2,1,0:T(8,128)(2,1)} %all-to-all-done.q_ref.own_ref), channel_id=1, source_target_pairs={{0,1},{1,0},{2,3},{3,2},{4,5},{5,4},{6,7},{7,6},{8,9},{9,8},{10,11... | collective-permute-start | bytes 4718600 | tf_op jit(solution)/shard_map/ppermute | solution.py:57
  151.6 14.5 %collective-permute-start.21 = (bf16[4,64,1024]{2,1,0:T(8,128)(2,1)}, bf16[4,64,1024]{2,1,0:T(8,128)(2,1)S(1)}, u32[]{:S(2)}, u32[]{:S(2)}) collective-permute-start(bf16[4,64,1024]{2,1,0:T(8,128)(2,1)} %bitcast_dynamic-update-slice_fusion.23), channel_id=1, source_target_pairs={{0,2},{2,0},{1,3},{3,1},{4,6},{6,4},{5,7},{7,5},{8,10},{10,8},{9,1... | collective-permute-start | bytes 1572872 | tf_op jit(solution)/shard_map/ppermute | solution.py:57
  163.4 46.3 %collective-permute-start.17 = (bf16[2,4,64,1024]{3,2,1,0:T(8,128)(2,1)}, bf16[2,4,64,1024]{3,2,1,0:T(8,128)(2,1)}, u32[]{:S(2)}, u32[]{:S(2)}) collective-permute-start(bf16[2,4,64,1024]{3,2,1,0:T(8,128)(2,1)} %bitcast_dynamic-update-slice_fusion.10), channel_id=1, source_target_pairs={{0,2},{2,0},{1,3},{3,1},{4,6},{6,4},{5,7},{7,5},{8,10},{10,8},{9,1... | collective-permute-start | bytes 3145736 | tf_op jit(solution)/shard_map/ppermute | solution.py:57
  167.0 63.5 %collective-permute-start.22 = (bf16[2,4,64,1024]{3,2,1,0:T(8,128)(2,1)}, bf16[2,4,64,1024]{3,2,1,0:T(8,128)(2,1)}, u32[]{:S(2)}, u32[]{:S(2)}) collective-permute-start(bf16[2,4,64,1024]{3,2,1,0:T(8,128)(2,1)} %bitcast_dynamic-update-slice_fusion.8), channel_id=1, source_target_pairs={{0,4},{4,0},{1,5},{5,1},{2,6},{6,2},{3,7},{7,3},{8,12},{12,8},{9,1... | collective-permute-start | bytes 3145736 | tf_op jit(solution)/shard_map/ppermute | solution.py:57
  202.7 17.6 %all-to-all-start.1 = ((bf16[16,64,256]{2,1,0:T(8,128)(2,1)}), bf16[16,64,256]{2,1,0:T(8,128)(2,1)S(1)}, u32[]{:S(2)}, u32[]{:S(2)}) async-start(bf16[16,64,256]{2,1,0:T(8,128)(2,1)} %bitcast.386), calls=%async_computation.1 | async-start | bytes 1048576 | tf_op jit(solution)/shard_map/all_to_all | solution.py:443
  224.5 10.2 %collective-permute-start.12 = (bf16[256,1024]{1,0:T(8,128)(2,1)S(1)}, bf16[256,1024]{1,0:T(8,128)(2,1)S(1)}, u32[]{:S(2)}, u32[]{:S(2)}) collective-permute-start(bf16[256,1024]{1,0:T(8,128)(2,1)S(1)} %get-tuple-element.129), channel_id=1, source_target_pairs={{0,1},{1,0},{2,3},{3,2},{4,5},{5,4},{6,7},{7,6},{8,9},{9,8},{10,11... | collective-permute-start | bytes 1572872 | tf_op jit(solution)/shard_map/ppermute | solution.py:57
  262.7 17.0 %collective-permute-start.26 = (bf16[16,32,1024]{2,1,0:T(8,128)(2,1)S(1)}, bf16[16,32,1024]{2,1,0:T(8,128)(2,1)}, u32[]{:S(2)}, u32[]{:S(2)}) collective-permute-start(bf16[16,32,1024]{2,1,0:T(8,128)(2,1)S(1)} %dynamic-slice_bitcast_fusion.6), channel_id=1, source_target_pairs={{0,1},{1,0},{2,3},{3,2},{4,5},{5,4},{6,7},{7,6},{8,9},{9,8},{10,11... | collective-permute-start | bytes 3145736 | tf_op jit(solution)/shard_map/ppermute | solution.py:57
  266.4 19.6 %all-to-all-start.2 = ((bf16[16,64,256]{2,1,0:T(8,128)(2,1)}), bf16[16,64,256]{2,1,0:T(8,128)(2,1)}, u32[]{:S(2)}, u32[]{:S(2)}) async-start(bf16[16,64,256]{2,1,0:T(8,128)(2,1)} %bitcast.387), calls=%async_computation.2 | async-start | bytes 1048576 | tf_op jit(solution)/shard_map/all_to_all | solution.py:477
  288.9 16.8 %collective-permute-start.30 = (bf16[2,2,64,1024]{3,2,1,0:T(8,128)(2,1)S(1)}, bf16[2,2,64,1024]{3,2,1,0:T(8,128)(2,1)S(1)}, u32[]{:S(2)}, u32[]{:S(2)}) collective-permute-start(bf16[2,2,64,1024]{3,2,1,0:T(8,128)(2,1)S(1)} %get-tuple-element.143), channel_id=1, source_target_pairs={{0,8},{8,16},{16,24},{24,0},{1,9},{9,17},{17,25},{25,1},{2,10},{10... | collective-permute-start | bytes 1572872 | tf_op jit(solution)/shard_map/ppermute | solution.py:57
  293.1 52.8 %collective-permute-start.27 = (bf16[4,2,64,2048]{3,2,1,0:T(8,128)(2,1)S(1)}, bf16[4,2,64,2048]{3,2,1,0:T(8,128)(2,1)}, u32[]{:S(2)}, u32[]{:S(2)}) collective-permute-start(bf16[4,2,64,2048]{3,2,1,0:T(8,128)(2,1)S(1)} %get-tuple-element.134), channel_id=1, source_target_pairs={{0,4},{4,0},{1,5},{5,1},{2,6},{6,2},{3,7},{7,3},{8,12},{12,8},{9,1... | collective-permute-start | bytes 6291464 | tf_op jit(solution)/shard_map/ppermute | solution.py:57
  294.0 51.8 %collective-permute-start.31 = (bf16[2,2,64,1024]{3,2,1,0:T(8,128)(2,1)}, bf16[2,2,64,1024]{3,2,1,0:T(8,128)(2,1)}, u32[]{:S(2)}, u32[]{:S(2)}) collective-permute-start(bf16[2,2,64,1024]{3,2,1,0:T(8,128)(2,1)} %get-tuple-element.142), channel_id=1, source_target_pairs={{0,16},{8,24},{16,0},{24,8},{1,17},{9,25},{17,1},{25,9},{2,18},{10... | collective-permute-start | bytes 1572872 | tf_op jit(solution)/shard_map/ppermute | solution.py:57
  295.4 50.5 %collective-permute-start.32 = (bf16[2,2,64,1024]{3,2,1,0:T(8,128)(2,1)}, bf16[2,2,64,1024]{3,2,1,0:T(8,128)(2,1)}, u32[]{:S(2)}, u32[]{:S(2)}) collective-permute-start(bf16[2,2,64,1024]{3,2,1,0:T(8,128)(2,1)} %get-tuple-element.141), channel_id=1, source_target_pairs={{0,24},{8,0},{16,8},{24,16},{1,25},{9,1},{17,9},{25,17},{2,26},{10... | collective-permute-start | bytes 1572872 | tf_op jit(solution)/shard_map/ppermute | solution.py:57
  298.0 47.9 %collective-permute-start.28 = (bf16[2,4,64,1024]{3,2,1,0:T(8,128)(2,1)}, bf16[2,4,64,1024]{3,2,1,0:T(8,128)(2,1)S(1)}, u32[]{:S(2)}, u32[]{:S(2)}) collective-permute-start(bf16[2,4,64,1024]{3,2,1,0:T(8,128)(2,1)} %get-tuple-element.145), channel_id=1, source_target_pairs={{0,2},{2,0},{1,3},{3,1},{4,6},{6,4},{5,7},{7,5},{8,10},{10,8},{9,1... | collective-permute-start | bytes 3145736 | tf_op jit(solution)/shard_map/ppermute | solution.py:57
  305.7 40.2 %collective-permute-start.29 = (bf16[4,2,32,1024]{3,2,0,1:T(8,128)(2,1)S(1)}, bf16[4,2,32,1024]{3,2,0,1:T(8,128)(2,1)S(1)}, u32[]{:S(2)}, u32[]{:S(2)}) collective-permute-start(bf16[4,2,32,1024]{3,2,0,1:T(8,128)(2,1)S(1)} %get-tuple-element.150), channel_id=1, source_target_pairs={{0,2},{2,0},{1,3},{3,1},{4,6},{6,4},{5,7},{7,5},{8,10},{10,8},{9,1... | collective-permute-start | bytes 1572872 | tf_op jit(solution)/shard_map/ppermute | solution.py:57
  362.2 24.9 %all-to-all-start.3 = ((bf16[4,192,1024]{2,1,0:T(8,128)(2,1)}), bf16[4,192,1024]{2,1,0:T(8,128)(2,1)}, u32[]{:S(2)}, u32[]{:S(2)}) async-start(bf16[4,192,1024]{2,1,0:T(8,128)(2,1)} %pad_maximum_fusion), calls=%async_computation.3 | async-start | bytes 3145728 | tf_op jit(solution)/shard_map/all_to_all | solution.py:516
  403.5 23.5 %collective-permute-start.37 = (bf16[4,2,2,32,896]{4,3,0,2,1:T(8,128)(2,1)S(1)}, bf16[4,2,2,32,896]{4,3,0,2,1:T(8,128)(2,1)S(1)}, u32[]{:S(2)}, u32[]{:S(2)}) collective-permute-start(bf16[4,2,2,32,896]{4,3,0,2,1:T(8,128)(2,1)S(1)} %fusion.51), channel_id=1, source_target_pairs={{0,1},{1,0},{2,3},{3,2},{4,5},{5,4},{6,7},{7,6},{8,9},{9,8},{10,11... | collective-permute-start | bytes 2752520 | tf_op jit(solution)/shard_map/ppermute | solution.py:57
  405.2 24.1 %collective-permute-start.42 = (bf16[4,32,1024]{2,1,0:T(8,128)(2,1)S(1)}, bf16[4,32,1024]{2,1,0:T(8,128)(2,1)S(1)}, u32[]{:S(2)}, u32[]{:S(2)}) collective-permute-start(bf16[4,32,1024]{2,1,0:T(8,128)(2,1)S(1)} %dynamic-slice_bitcast_fusion.25), channel_id=1, source_target_pairs={{0,4},{4,0},{1,5},{5,1},{2,6},{6,2},{3,7},{7,3},{8,12},{12,8},{9,1... | collective-permute-start | bytes 786440 | tf_op jit(solution)/shard_map/ppermute | solution.py:57
  405.8 25.1 %collective-permute-start.41 = (bf16[4,64,1024]{2,1,0:T(8,128)(2,1)S(1)}, bf16[4,64,1024]{2,1,0:T(8,128)(2,1)S(1)}, u32[]{:S(2)}, u32[]{:S(2)}) collective-permute-start(bf16[4,64,1024]{2,1,0:T(8,128)(2,1)S(1)} %dynamic-slice_bitcast_fusion.9), channel_id=1, source_target_pairs={{0,4},{4,0},{1,5},{5,1},{2,6},{6,2},{3,7},{7,3},{8,12},{12,8},{9,1... | collective-permute-start | bytes 1572872 | tf_op jit(solution)/shard_map/ppermute | solution.py:57
  407.5 35.0 %collective-permute-start.40 = (bf16[4,64,2048]{2,1,0:T(8,128)(2,1)S(1)}, bf16[4,64,2048]{2,1,0:T(8,128)(2,1)S(1)}, u32[]{:S(2)}, u32[]{:S(2)}) collective-permute-start(bf16[4,64,2048]{2,1,0:T(8,128)(2,1)S(1)} %dynamic-slice_bitcast_fusion.2), channel_id=1, source_target_pairs={{0,2},{2,0},{1,3},{3,1},{4,6},{6,4},{5,7},{7,5},{8,10},{10,8},{9,1... | collective-permute-start | bytes 3145736 | tf_op jit(solution)/shard_map/ppermute | solution.py:57
  412.8 34.3 %collective-permute-start.34 = (bf16[256,1024]{1,0:T(8,128)(2,1)S(1)}, bf16[256,1024]{1,0:T(8,128)(2,1)S(1)}, u32[]{:S(2)}, u32[]{:S(2)}) collective-permute-start(bf16[256,1024]{1,0:T(8,128)(2,1)S(1)} %get-tuple-element.139), channel_id=1, source_target_pairs={{0,8},{8,16},{16,24},{24,0},{1,9},{9,17},{17,25},{25,1},{2,10},{10... | collective-permute-start | bytes 1572872 | tf_op jit(solution)/shard_map/ppermute | solution.py:57
  427.0 27.1 %collective-permute-start.35 = (bf16[256,1024]{1,0:T(8,128)(2,1)S(1)}, bf16[256,1024]{1,0:T(8,128)(2,1)S(1)}, u32[]{:S(2)}, u32[]{:S(2)}) collective-permute-start(bf16[256,1024]{1,0:T(8,128)(2,1)S(1)} %get-tuple-element.138), channel_id=1, source_target_pairs={{0,16},{8,24},{16,0},{24,8},{1,17},{9,25},{17,1},{25,9},{2,18},{10... | collective-permute-start | bytes 1572872 | tf_op jit(solution)/shard_map/ppermute | solution.py:57
  429.3 11.5 %collective-permute-start.38 = (bf16[4,2,32,896]{3,2,0,1:T(8,128)(2,1)S(1)}, bf16[4,2,32,896]{3,2,0,1:T(8,128)(2,1)S(1)}, u32[]{:S(2)}, u32[]{:S(2)}) collective-permute-start(bf16[4,2,32,896]{3,2,0,1:T(8,128)(2,1)S(1)} %dynamic-slice_bitcast_fusion.20), channel_id=1, source_target_pairs={{0,4},{4,0},{1,5},{5,1},{2,6},{6,2},{3,7},{7,3},{8,12},{12,8},{9,1... | collective-permute-start | bytes 1376264 | tf_op jit(solution)/shard_map/ppermute | solution.py:57
  430.9 32.3 %collective-permute-start.36 = (bf16[256,1024]{1,0:T(8,128)(2,1)S(1)}, bf16[256,1024]{1,0:T(8,128)(2,1)S(1)}, u32[]{:S(2)}, u32[]{:S(2)}) collective-permute-start(bf16[256,1024]{1,0:T(8,128)(2,1)S(1)} %get-tuple-element.137), channel_id=1, source_target_pairs={{0,24},{8,0},{16,8},{24,16},{1,25},{9,1},{17,9},{25,17},{2,26},{10... | collective-permute-start | bytes 1572872 | tf_op jit(solution)/shard_map/ppermute | solution.py:57
  464.0 43.1 %collective-permute-start.54 = (bf16[64,1024]{1,0:T(8,128)(2,1)}, bf16[64,1024]{1,0:T(8,128)(2,1)}, u32[]{:S(2)}, u32[]{:S(2)}) collective-permute-start(bf16[64,1024]{1,0:T(8,128)(2,1)} %get-tuple-element.153), channel_id=1, source_target_pairs={{0,8},{8,16},{16,24},{24,0},{1,9},{9,17},{17,25},{25,1},{2,10},{10... | collective-permute-start | bytes 393224 | tf_op jit(solution)/shard_map/ppermute | solution.py:57
  474.7 37.1 %collective-permute-start.55 = (bf16[64,1024]{1,0:T(8,128)(2,1)}, bf16[64,1024]{1,0:T(8,128)(2,1)}, u32[]{:S(2)}, u32[]{:S(2)}) collective-permute-start(bf16[64,1024]{1,0:T(8,128)(2,1)} %get-tuple-element.155), channel_id=1, source_target_pairs={{0,16},{8,24},{16,0},{24,8},{1,17},{9,25},{17,1},{25,9},{2,18},{10... | collective-permute-start | bytes 393224 | tf_op jit(solution)/shard_map/ppermute | solution.py:57
  479.7 24.2 %collective-permute-start.47 = (bf16[32,1024]{1,0:T(8,128)(2,1)}, bf16[32,1024]{1,0:T(8,128)(2,1)}, u32[]{:S(2)}, u32[]{:S(2)}) collective-permute-start(bf16[32,1024]{1,0:T(8,128)(2,1)} %get-tuple-element.165), channel_id=1, source_target_pairs={{0,8},{8,16},{16,24},{24,0},{1,9},{9,17},{17,25},{25,1},{2,10},{10... | collective-permute-start | bytes 196616 | tf_op jit(solution)/shard_map/ppermute | solution.py:57
  479.7 26.6 %collective-permute-start.48 = (bf16[32,1024]{1,0:T(8,128)(2,1)}, bf16[32,1024]{1,0:T(8,128)(2,1)}, u32[]{:S(2)}, u32[]{:S(2)}) collective-permute-start(bf16[32,1024]{1,0:T(8,128)(2,1)} %get-tuple-element.167), channel_id=1, source_target_pairs={{0,16},{8,24},{16,0},{24,8},{1,17},{9,25},{17,1},{25,9},{2,18},{10... | collective-permute-start | bytes 196616 | tf_op jit(solution)/shard_map/ppermute | solution.py:57
  506.3 11.3 %collective-permute-start.50 = (bf16[64,2048]{1,0:T(8,128)(2,1)}, bf16[64,2048]{1,0:T(8,128)(2,1)S(1)}, u32[]{:S(2)}, u32[]{:S(2)}) collective-permute-start(bf16[64,2048]{1,0:T(8,128)(2,1)} %get-tuple-element.147), channel_id=1, source_target_pairs={{0,8},{8,16},{16,24},{24,0},{1,9},{9,17},{17,25},{25,1},{2,10},{10... | collective-permute-start | bytes 786440 | tf_op jit(solution)/shard_map/ppermute | solution.py:57
  506.3 19.5 %collective-permute-start.51 = (bf16[64,2048]{1,0:T(8,128)(2,1)}, bf16[64,2048]{1,0:T(8,128)(2,1)S(1)}, u32[]{:S(2)}, u32[]{:S(2)}) collective-permute-start(bf16[64,2048]{1,0:T(8,128)(2,1)} %get-tuple-element.149), channel_id=1, source_target_pairs={{0,16},{8,24},{16,0},{24,8},{1,17},{9,25},{17,1},{25,9},{2,18},{10... | collective-permute-start | bytes 786440 | tf_op jit(solution)/shard_map/ppermute | solution.py:57
  507.1 18.7 %collective-permute-start.52 = (bf16[64,2048]{1,0:T(8,128)(2,1)}, bf16[64,2048]{1,0:T(8,128)(2,1)S(1)}, u32[]{:S(2)}, u32[]{:S(2)}) collective-permute-start(bf16[64,2048]{1,0:T(8,128)(2,1)} %get-tuple-element.148), channel_id=1, source_target_pairs={{0,24},{8,0},{16,8},{24,16},{1,25},{9,1},{17,9},{25,17},{2,26},{10... | collective-permute-start | bytes 786440 | tf_op jit(solution)/shard_map/ppermute | solution.py:57
  511.8 14.3 %collective-permute-start.57 = (bf16[64,1024]{1,0:T(8,128)(2,1)S(1)}, bf16[64,1024]{1,0:T(8,128)(2,1)S(1)}, u32[]{:S(2)}, u32[]{:S(2)}) collective-permute-start(bf16[64,1024]{1,0:T(8,128)(2,1)S(1)} %dynamic-slice_bitcast_fusion.27), channel_id=1, source_target_pairs={{0,2},{2,0},{1,3},{3,1},{4,6},{6,4},{5,7},{7,5},{8,10},{10,8},{9,1... | collective-permute-start | bytes 393224 | tf_op jit(solution)/shard_map/ppermute | solution.py:57
  (87 other events, 951.9 us)
Sparse Core Ops, SparseCore 0:
  31.8 117.9 all-gather.1
